TPU v7x, 512 devices: a whole 4x4x16 slice. The times are simulated.
512 devices in a mesh: gx: 32 (over z, x_hi), gy: 4 (over y), gz: 4 (over x_lo, core).
Axes of the slice: x: 4 (x_hi: 2, x_lo: 2; x = x_hi * 2 + x_lo), y: 4, z: 16, core: 2. Of those that a mesh axis runs over, the one named last changes fastest.
Arguments:
- tangent: bfloat16 [32, 128, 32, 512], P(None, 'gx', 'gy', 'gz'), may hold values from -130 to 130
- slopes: bfloat16 [32, 128, 32, 512], P(None, 'gx', 'gy', 'gz'), may hold values from -0.099609375 to 1.09375
- first_kernel: bfloat16 [27, 32, 32], replicated, may hold values from -0.21875 to 0.21875
- second_kernel: bfloat16 [27, 32, 32], replicated, may hold values from -0.21875 to 0.21875
Outputs:
- next_vector: float32 [32, 128, 32, 512], P(None, 'gx', 'gy', 'gz')
- jvp_norm: float32 [1], replicated
All inputs are finite; a program needn't handle non-finite values.
Results may differ from a plain program's by a relative error of at most 0.0038.
Values may be sent and summed in bfloat16 or wider, within the bound.
No kernel may reach another device: no remote copies, remote signals or barrier semaphores. Data moves between devices by JAX's collectives and lax.ppermute only.
A program may use at most 192 MiB of HBM per device.

v0:
```python
import jax
import jax.numpy as jnp
from jax import lax
from jax.experimental import pallas as pl
from jax.experimental.pallas import tpu as pltpu
from jax.sharding import PartitionSpec as P

ALL = ("gx", "gy", "gz")
CH = 32
LANES = 128


def shift_pair(up, down, axis):
    ends = lax.axis_size(axis) - 1
    from_prev = lax.ppermute(up, axis, [(i, i + 1) for i in range(ends)])
    from_next = lax.ppermute(down, axis, [(i + 1, i) for i in range(ends)])
    return from_prev, from_next


def pack_kernel(f_ref, left_ref, right_ref):
    lane = lax.broadcasted_iota(jnp.int32, (CH, LANES), 1)

    def group(g, carry):
        left = jnp.zeros((CH, LANES), jnp.float32)
        right = jnp.zeros((CH, LANES), jnp.float32)
        for k in range(32):
            tile = f_ref[2 * g + k // 16, k % 16].astype(jnp.float32)
            rolled = pltpu.roll(tile, (4 * k + 4) % LANES, 1)
            right = jnp.where(lane // 4 == k, rolled, right)
            left = jnp.where(lane // 4 == (k + 1) % 32, rolled, left)
        left_ref[g] = left.astype(jnp.bfloat16)
        right_ref[g] = right.astype(jnp.bfloat16)
        return carry

    lax.fori_loop(0, left_ref.shape[0], group, 0)


def pack_edges(f):
    groups = f.shape[0] // 2
    out = jax.ShapeDtypeStruct((groups, CH, LANES), jnp.bfloat16)
    return pl.pallas_call(
        pack_kernel,
        out_shape=(out, out),
        compiler_params=pltpu.CompilerParams(vmem_limit_bytes=40 << 20),
        name="pack_edges",
    )(f)


def main_kernel(place, f_ref, rl_ref, rr_ref, w_ref, out_ref, sum_ref, h_ref, hid, img, pul):
    lane = lax.broadcasted_iota(jnp.int32, (CH, LANES), 1)

    def unpack(g, carry):
        rl = rl_ref[g].astype(jnp.float32)
        rr = rr_ref[g].astype(jnp.float32)
        low = (lane & 7) < 4
        even = jnp.where(low, rl, rr)
        odd = jnp.where(low, rr, rl)
        for k in range(32):
            tile = pltpu.roll(odd if k % 2 else even, (LANES - 4 * k - 4) % LANES, 1)
            h_ref[2 * g + k // 16, k % 16] = tile.astype(jnp.bfloat16)
        return carry

    lax.fori_loop(0, rl_ref.shape[0], unpack, 0)

    wide_lane = lax.broadcasted_iota(jnp.int32, (2 * CH, LANES), 1)

    def t_layer(t):
        return t + 2 + 4 * lax.shift_right_logical(t, 2)

    def s_layer(s):
        return s + 4 * lax.shift_right_logical(s + 2, 2)

    def field_rows(t, r):
        i = t_layer(t)
        a = f_ref[i, pl.ds(r, 4)].reshape(4 * CH, LANES)
        b = h_ref[i, pl.ds(r, 4)].reshape(4 * CH, LANES)
        return jnp.concatenate([a, b], axis=1)

    def scratch_rows(ref):
        def get(t, r):
            return ref[t, pl.ds(r, 4)].reshape(4 * CH, 2 * LANES)

        return get

    def conv_pair(which, get, m, r):
        rhs = jnp.concatenate([get(m + a, r) for a in range(3)], axis=0)
        g = jnp.dot(w_ref[which], rhs, preferred_element_type=jnp.float32)
        n = 2 * CH
        before = (g[:n, :LANES], g[:n, LANES:])
        mid = (g[n : 2 * n, :LANES], g[n : 2 * n, LANES:])
        after = (g[2 * n :, :LANES], g[2 * n :, LANES:])
        b0, b1 = (pltpu.roll(v, 1, 1) for v in before)
        a0, a1 = (pltpu.roll(v, LANES - 1, 1) for v in after)
        first = wide_lane == 0
        last = wide_lane == LANES - 1
        own = mid[0] + jnp.where(first, b1, b0) + jnp.where(last, a1, a0)
        halo = mid[1] + jnp.where(first, b0, b1) + jnp.where(last, a0, a1)
        return own, halo

    def slopes_at(m, r):
        i = s_layer(m)
        a = f_ref[i, pl.ds(r, 2)].reshape(2 * CH, LANES).astype(jnp.float32)
        b = h_ref[i, pl.ds(r, 2)].reshape(2 * CH, LANES).astype(jnp.float32)
        return a, b

    def store(ref, m, r, own, halo):
        ref[m, pl.ds(r, 2), :, :LANES] = own.astype(jnp.bfloat16).reshape(2, CH, LANES)
        ref[m, pl.ds(r, 2), :, LANES:] = halo.astype(jnp.bfloat16).reshape(2, CH, LANES)

    def stage_hidden(m, carry):
        for j in range(7):
            own, halo = conv_pair(0, field_rows, m, 2 * j)
            a, b = slopes_at(m, 2 * j + 1)
            store(hid, m, 2 * j, a * own, b * halo)
        return carry

    lax.fori_loop(0, 10, stage_hidden, 0)

    gx, gy, gz = place[0], place[1], place[2]
    nx, ny, nz = place[3], place[4], place[5]
    halo_lane = jnp.where(
        wide_lane < LANES // 2,
        jnp.where(gz < nz, 1.0, 0.0),
        jnp.where(gz > 0, 1.0, 0.0),
    )
    sum_ref[...] = jnp.zeros_like(sum_ref)

    def stage_image(m, carry):
        x_in = ((m >= 2) | (gx > 0)) & ((m < 6) | (gx < nx))
        x_own = (m >= 2) & (m < 6)
        for j in range(6):
            own, halo = conv_pair(1, scratch_rows(hid), m, 2 * j)
            keep = x_in
            if j < 1:
                keep = keep & (gy > 0)
            if j > 4:
                keep = keep & (gy < ny)
            scale = jnp.where(keep, 1.0, 0.0)
            store(img, m, 2 * j, own * scale, halo * (halo_lane * scale))
            if 1 <= j <= 4:
                square = own * own * jnp.where(x_own, 1.0, 0.0)
                part = square[0:8]
                for q in range(1, 8):
                    part = part + square[8 * q : 8 * q + 8]
                sum_ref[...] += part
        return carry

    lax.fori_loop(0, 8, stage_image, 0)

    def stage_pulled(m, carry):
        for j in range(5):
            own, halo = conv_pair(2, scratch_rows(img), m, 2 * j)
            a, b = slopes_at(m + 2, 2 * j + 3)
            store(pul, m, 2 * j, a * own, b * halo)
        return carry

    lax.fori_loop(0, 6, stage_pulled, 0)

    def stage_out(m, carry):
        for j in range(4):
            own, halo = conv_pair(3, scratch_rows(pul), m, 2 * j)
            out_ref[m, pl.ds(2 * j, 2)] = own.reshape(2, CH, LANES)
        return carry

    lax.fori_loop(0, 4, stage_out, 0)


def all_convs(place, f, rl, rr, weights):
    layers, rows = f.shape[0], f.shape[1]
    return pl.pallas_call(
        main_kernel,
        out_shape=(
            jax.ShapeDtypeStruct((4, 8, CH, LANES), jnp.float32),
            jax.ShapeDtypeStruct((8, LANES), jnp.float32),
        ),
        in_specs=[pl.BlockSpec(memory_space=pltpu.SMEM)]
        + [pl.BlockSpec(memory_space=pltpu.VMEM)] * 4,
        scratch_shapes=[
            pltpu.VMEM((layers, rows, CH, LANES), jnp.bfloat16),
            pltpu.VMEM((10, 14, CH, 2 * LANES), jnp.bfloat16),
            pltpu.VMEM((8, 12, CH, 2 * LANES), jnp.bfloat16),
            pltpu.VMEM((6, 10, CH, 2 * LANES), jnp.bfloat16),
        ],
        compiler_params=pltpu.CompilerParams(vmem_limit_bytes=48 << 20),
        name="all_convs",
    )(place, f, rl, rr, weights)


def pair_matrix(kernel):
    taps = kernel.reshape(3, 3, 3, CH, CH)
    none = ((0, 0), (0, 0), (0, 0), (0, 0))
    top = jnp.pad(taps, (none[0], (0, 1)) + none[:3])
    low = jnp.pad(taps, (none[0], (1, 0)) + none[:3])
    both = jnp.stack([top, low])
    return both.transpose(3, 0, 4, 1, 2, 5).reshape(6 * CH, 12 * CH)


def on_device(tangent, slopes, first_kernel, second_kernel):
    t = tangent.transpose(1, 2, 0, 3)
    s = slopes.transpose(1, 2, 0, 3)
    mine = jnp.concatenate([s[0:3], t, s[3:4]], axis=0)
    from_prev, from_next = shift_pair(mine[1:8], mine[0:7], "gx")
    deep = jnp.concatenate([from_prev, mine, from_next], axis=0)
    above, below = shift_pair(deep[:, 4:8], deep[:, 0:4], "gy")
    f = jnp.concatenate([above, deep, below], axis=1)
    left_edge, right_edge = pack_edges(f)
    rl, rr = shift_pair(right_edge, left_edge, "gz")

    adjoint = lambda k: k[::-1].transpose(0, 2, 1)
    weights = jnp.stack(
        [
            pair_matrix(first_kernel),
            pair_matrix(second_kernel),
            pair_matrix(adjoint(second_kernel)),
            pair_matrix(adjoint(first_kernel)),
        ]
    )
    place = jnp.stack(
        [lax.axis_index(a) for a in ALL] + [jnp.int32(lax.axis_size(a) - 1) for a in ALL]
    ).astype(jnp.int32)
    result, squares = all_convs(place, f, rl, rr, weights)

    part = jnp.sum(squares, axis=0, keepdims=True)
    for axes in (("gy", "gz"), "gx"):
        count = lax.axis_size(axes)
        spread = jnp.broadcast_to(part, (count, LANES))
        part = jnp.sum(lax.all_to_all(spread, axes, 0, 0, tiled=True), axis=0, keepdims=True)
    jvp_norm = jnp.sqrt(jnp.sum(part) + 1e-06)
    next_vector = result.transpose(2, 0, 1, 3) / jvp_norm
    return (next_vector, jvp_norm.reshape(1))


def solution(mesh):
    return jax.shard_map(
        on_device,
        mesh=mesh,
        in_specs=(P(None, "gx", "gy", "gz"), P(None, "gx", "gy", "gz"), P(), P()),
        out_specs=(P(None, "gx", "gy", "gz"), P()),
        check_vma=False,
    )
```

profile of v0, /device:TPU:1, one launch (start us, length us, event | category | flops | bytes accessed | tf_op | source)
XLA Modules:
  0.0 130.4 jit_solution(5408559165422819066)
XLA Ops:
  0.6 0.0 copy-start.2
  0.6 1.1 copy.46
  1.8 1.1 copy.45
  2.8 0.8 pad_maximum_fusion.4
  3.7 6.2 %collective-permute-start = (bf16[7,8,32,128]{3,2,1,0:T(8,128)(2,1)S(1)}, bf16[7,8,32,128]{3,2,1,0:T(8,128)(2,1)}, u32[]{:S(2)}, u32[]{:S(2)}) collective-permute-start(bf16[7,8,32,128]{3,2,1,0:T(8,128)(2,1)S(1)} %get-tuple-element.19), channel_id=1, source_target_pairs={{0,16},{16,32},{32,48},{48,64},{64,80},{80,96},{96,112},{112,128},... | collective-permute-start | bytes 1376264 | tf_op jit(solution)/shard_map/ppermute | solution.py:15
  9.9 1.3 collective-permute-start.1
  11.2 0.0 copy-done.2
  11.2 0.2 copy.34
  11.4 0.0 copy-start.1
  11.5 0.3 pad_bitcast_fusion.3
  11.8 0.5 maximum_bitcast_fusion.2
  12.3 0.0 copy-start
  12.3 0.3 stack_reshape.14
  12.7 0.0 copy-done.1
  12.7 0.2 copy.36
  12.9 13.5 %collective-permute-done = bf16[7,8,32,128]{3,2,1,0:T(8,128)(2,1)} collective-permute-done((bf16[7,8,32,128]{3,2,1,0:T(8,128)(2,1)S(1)}, bf16[7,8,32,128]{3,2,1,0:T(8,128)(2,1)}, u32[]{:S(2)}, u32[]{:S(2)}) %collective-permute-start) | collective-permute-done | bytes 458784 | tf_op jit(solution)/shard_map/ppermute | solution.py:15
  26.4 1.0 constant_dynamic-update-slice_fusion.4
  27.4 0.0 copy-done
  27.5 0.1 constant_dynamic-update-slice_fusion.2
  27.6 0.0 collective-permute-done.1
  27.6 1.1 constant_dynamic-update-slice_fusion
  28.7 1.4 %fusion = (bf16[22,4,32,128]{3,2,1,0:T(8,128)(2,1)}, bf16[22,4,32,128]{3,2,1,0:T(8,128)(2,1)}) fusion(bf16[22,8,32,128]{3,2,1,0:T(8,128)(2,1)S(1)} %constant_dynamic-update-slice_fusion), kind=kLoop, calls=%fused_computation.25 | loop fusion | bytes 2883584 | tf_op jit(solution)/shard_map/slice | solution.py:204
  30.2 5.9 %collective-permute-start.2 = (bf16[22,4,32,128]{3,2,1,0:T(8,128)(2,1)}, bf16[22,4,32,128]{3,2,1,0:T(8,128)(2,1)}, u32[]{:S(2)}, u32[]{:S(2)}) collective-permute-start(bf16[22,4,32,128]{3,2,1,0:T(8,128)(2,1)} %get-tuple-element.16), channel_id=1, source_target_pairs={{0,4},{4,8},{8,12},{1,5},{5,9},{9,13},{2,6},{6,10},{10,14},{3,7},{... | collective-permute-start | bytes 2162696 | tf_op jit(solution)/shard_map/ppermute | solution.py:15
  36.0 1.3 collective-permute-start.3
  37.3 0.3 pad_bitcast_fusion.1
  37.6 0.5 maximum_bitcast_fusion.3
  38.1 0.3 stack_reshape.15
  38.5 0.2 copy.30
  38.6 0.3 pad_bitcast_fusion.7
  39.0 0.5 maximum_bitcast_fusion
  39.5 0.3 stack_reshape.12
  39.8 0.2 copy.32
  40.0 0.3 pad_bitcast_fusion.5
  40.3 0.5 maximum_bitcast_fusion.1
  40.8 0.3 stack_reshape.13
  41.2 0.1 stack.54.place
  41.3 8.0 %collective-permute-done.2 = bf16[22,4,32,128]{3,2,1,0:T(8,128)(2,1)} collective-permute-done((bf16[22,4,32,128]{3,2,1,0:T(8,128)(2,1)}, bf16[22,4,32,128]{3,2,1,0:T(8,128)(2,1)}, u32[]{:S(2)}, u32[]{:S(2)}) %collective-permute-start.2) | collective-permute-done | bytes 720928 | tf_op jit(solution)/shard_map/ppermute | solution.py:15
  49.3 4.7 %collective-permute-done.3 = bf16[22,4,32,128]{3,2,1,0:T(8,128)(2,1)} collective-permute-done((bf16[22,4,32,128]{3,2,1,0:T(8,128)(2,1)}, bf16[22,4,32,128]{3,2,1,0:T(8,128)(2,1)}, u32[]{:S(2)}, u32[]{:S(2)}) %collective-permute-start.3) | collective-permute-done | bytes 720928 | tf_op jit(solution)/shard_map/ppermute | solution.py:16
  54.0 1.6 %pad_maximum_fusion.f_ref = bf16[22,16,32,128]{3,2,1,0:T(8,128)(2,1)S(1)} fusion(bf16[22,4,32,128]{3,2,1,0:T(8,128)(2,1)} %collective-permute-done.3, bf16[22,8,32,128]{3,2,1,0:T(8,128)(2,1)S(1)} %constant_dynamic-update-slice_fusion, bf16[22,4,32,128]{3,2,1,0:T(8,128)(2,1)} %collective-permute-done.2), kind=kLoop, calls=%fused_computation | loop fusion | flops 2883584 | bytes 5767168 | tf_op jit(solution)/shard_map/concatenate | solution.py:205
  55.7 1.5 %pack_edges.1 = (bf16[11,32,128]{2,1,0:T(8,128)(2,1)S(1)}, bf16[11,32,128]{2,1,0:T(8,128)(2,1)S(1)}) custom-call(bf16[22,16,32,128]{3,2,1,0:T(8,128)(2,1)S(1)} %pad_maximum_fusion.f_ref), custom_call_target="tpu_custom_call" | custom-call | tf_op jit(solution)/shard_map/pack_edges/pallas_call | solution.py:41
  57.2 4.9 %collective-permute-start.4 = (bf16[11,32,128]{2,1,0:T(8,128)(2,1)S(1)}, bf16[11,32,128]{2,1,0:T(8,128)(2,1)S(1)}, u32[]{:S(2)}, u32[]{:S(2)}) collective-permute-start(bf16[11,32,128]{2,1,0:T(8,128)(2,1)S(1)} %get-tuple-element.6), channel_id=1, source_target_pairs={{0,1},{1,2},{2,3},{4,5},{5,6},{6,7},{8,9},{9,10},{10,11},{12,13},{... | collective-permute-start | bytes 270344 | tf_op jit(solution)/shard_map/ppermute | solution.py:15
  62.0 1.9 %collective-permute-start.5 = (bf16[11,32,128]{2,1,0:T(8,128)(2,1)S(1)}, bf16[11,32,128]{2,1,0:T(8,128)(2,1)S(1)}, u32[]{:S(2)}, u32[]{:S(2)}) collective-permute-start(bf16[11,32,128]{2,1,0:T(8,128)(2,1)S(1)} %get-tuple-element.7), channel_id=1, source_target_pairs={{1,0},{2,1},{3,2},{5,4},{6,5},{7,6},{9,8},{10,9},{11,10},{13,12},{... | collective-permute-start | bytes 270344 | tf_op jit(solution)/shard_map/ppermute | solution.py:16
  64.0 0.1 pad_maximum_fusion.1.w_ref
  64.1 0.0 collective-permute-done.4.rl_ref
  64.1 3.8 %collective-permute-done.5.rr_ref = bf16[11,32,128]{2,1,0:T(8,128)(2,1)S(1)} collective-permute-done((bf16[11,32,128]{2,1,0:T(8,128)(2,1)S(1)}, bf16[11,32,128]{2,1,0:T(8,128)(2,1)S(1)}, u32[]{:S(2)}, u32[]{:S(2)}) %collective-permute-start.5) | collective-permute-done | bytes 90144 | tf_op jit(solution)/shard_map/ppermute | solution.py:16
  67.9 17.5 %all_convs.1 = (f32[4,8,32,128]{3,2,1,0:T(8,128)S(1)}, f32[8,128]{1,0:T(8,128)S(1)}) custom-call(s32[6]{0:T(128)S(1)} %stack.54.place, bf16[22,16,32,128]{3,2,1,0:T(8,128)(2,1)S(1)} %pad_maximum_fusion.f_ref, bf16[11,32,128]{2,1,0:T(8,128)(2,1)S(1)} %collective-permute-done.4.rl_ref, bf16[11,32,128]{2,1,0:T(8,128)(2,1)S(1)} %collective-permute-done.5.rr_ref, ...), custom_call_target="tpu_custom_call" | custom-call | tf_op jit(solution)/shard_map/all_convs/pallas_call | solution.py:170
  85.4 8.7 %all_to_all.12 = f32[16,1,128]{2,1,0:T(1,128)S(1)} all-to-all(f32[16,1,128]{2,1,0:T(1,128)S(1)} %broadcast_in_dim.4), channel_id=1, replica_groups=mesh['gx'=32,'gy'=4,'gz'=4] {'gy','gz'}, dimensions={0} | all-to-all | bytes 16384 | tf_op jit(solution)/shard_map/all_to_all | solution.py:227
  94.1 32.7 %all_to_all.13 = f32[32,1,128]{2,1,0:T(1,128)S(1)} all-to-all(f32[32,1,128]{2,1,0:T(1,128)S(1)} %broadcast_in_dim.5), channel_id=1, replica_groups=mesh['gx'=32,'gy'=4,'gz'=4] {'gx'}, dimensions={0} | all-to-all | bytes 32768 | tf_op jit(solution)/shard_map/all_to_all | solution.py:227
  126.8 0.6 reduce_sum.33
  128.1 0.1 divide_bitcast_fusion
  128.2 1.1 copy.40
  (11 shorter events, 0.2 us)
Async XLA Ops:
  0.6 10.6 %copy-start.2 = (bf16[27,32,32]{2,1,0:T(8,128)(2,1)S(1)}, bf16[27,32,32]{2,1,0:T(8,128)(2,1)}, u32[]{:S(2)}) copy-start(bf16[27,32,32]{2,1,0:T(8,128)(2,1)} %param.7) | copy-start | bytes 165892
  3.7 22.7 %collective-permute-start = (bf16[7,8,32,128]{3,2,1,0:T(8,128)(2,1)S(1)}, bf16[7,8,32,128]{3,2,1,0:T(8,128)(2,1)}, u32[]{:S(2)}, u32[]{:S(2)}) collective-permute-start(bf16[7,8,32,128]{3,2,1,0:T(8,128)(2,1)S(1)} %get-tuple-element.19), channel_id=1, source_target_pairs={{0,16},{16,32},{32,48},{48,64},{64,80},{80,96},{96,112},{112,128},... | collective-permute-start | bytes 1376264 | tf_op jit(solution)/shard_map/ppermute | solution.py:15
  9.9 17.7 %collective-permute-start.1 = (bf16[7,8,32,128]{3,2,1,0:T(8,128)(2,1)}, bf16[7,8,32,128]{3,2,1,0:T(8,128)(2,1)}, u32[]{:S(2)}, u32[]{:S(2)}) collective-permute-start(bf16[7,8,32,128]{3,2,1,0:T(8,128)(2,1)} %get-tuple-element.18), channel_id=1, source_target_pairs={{16,0},{32,16},{48,32},{64,48},{80,64},{96,80},{112,96},{128,112},... | collective-permute-start | bytes 1376264 | tf_op jit(solution)/shard_map/ppermute | solution.py:16
  11.4 1.2 copy-start.1
  12.3 15.2 %copy-start = (bf16[32,4,8,128]{3,2,1,0:T(8,128)(2,1)S(1)}, bf16[32,4,8,128]{3,2,1,0:T(8,128)(2,1)}, u32[]{:S(2)}) copy-start(bf16[32,4,8,128]{3,2,1,0:T(8,128)(2,1)} %param.4) | copy-start | bytes 786436
  30.2 19.2 %collective-permute-start.2 = (bf16[22,4,32,128]{3,2,1,0:T(8,128)(2,1)}, bf16[22,4,32,128]{3,2,1,0:T(8,128)(2,1)}, u32[]{:S(2)}, u32[]{:S(2)}) collective-permute-start(bf16[22,4,32,128]{3,2,1,0:T(8,128)(2,1)} %get-tuple-element.16), channel_id=1, source_target_pairs={{0,4},{4,8},{8,12},{1,5},{5,9},{9,13},{2,6},{6,10},{10,14},{3,7},{... | collective-permute-start | bytes 2162696 | tf_op jit(solution)/shard_map/ppermute | solution.py:15
  36.0 18.0 %collective-permute-start.3 = (bf16[22,4,32,128]{3,2,1,0:T(8,128)(2,1)}, bf16[22,4,32,128]{3,2,1,0:T(8,128)(2,1)}, u32[]{:S(2)}, u32[]{:S(2)}) collective-permute-start(bf16[22,4,32,128]{3,2,1,0:T(8,128)(2,1)} %get-tuple-element.17), channel_id=1, source_target_pairs={{4,0},{8,4},{12,8},{5,1},{9,5},{13,9},{6,2},{10,6},{14,10},{7,3},{... | collective-permute-start | bytes 2162696 | tf_op jit(solution)/shard_map/ppermute | solution.py:16
  57.2 6.9 %collective-permute-start.4 = (bf16[11,32,128]{2,1,0:T(8,128)(2,1)S(1)}, bf16[11,32,128]{2,1,0:T(8,128)(2,1)S(1)}, u32[]{:S(2)}, u32[]{:S(2)}) collective-permute-start(bf16[11,32,128]{2,1,0:T(8,128)(2,1)S(1)} %get-tuple-element.6), channel_id=1, source_target_pairs={{0,1},{1,2},{2,3},{4,5},{5,6},{6,7},{8,9},{9,10},{10,11},{12,13},{... | collective-permute-start | bytes 270344 | tf_op jit(solution)/shard_map/ppermute | solution.py:15
  62.0 5.8 %collective-permute-start.5 = (bf16[11,32,128]{2,1,0:T(8,128)(2,1)S(1)}, bf16[11,32,128]{2,1,0:T(8,128)(2,1)S(1)}, u32[]{:S(2)}, u32[]{:S(2)}) collective-permute-start(bf16[11,32,128]{2,1,0:T(8,128)(2,1)S(1)} %get-tuple-element.7), channel_id=1, source_target_pairs={{1,0},{2,1},{3,2},{5,4},{6,5},{7,6},{9,8},{10,9},{11,10},{13,12},{... | collective-permute-start | bytes 270344 | tf_op jit(solution)/shard_map/ppermute | solution.py:16
where the time goes:
time: 131 us; the launch traced here: 130 us
  blocking collectives  41.4 us (32%)
  waiting for transfers between devices  30 us (23%)
  starting transfers between devices  21.4 us (16%)
  Pallas kernels  19 us (15%)
  local copies, waits for them, and re-layouts  10.6 us (8%)
  other arithmetic  5.2 us (4%)
  between operations  2.8 us (2%)
    all_to_all x2, blocking collectives, on_device(): lax.all_to_all(spread, axes, 0, 0, tiled=True)  41.4 us
    ppermute x3, waiting for transfers between devices, shift_pair(): from_prev = lax.ppermute(up, axis, [(i, i + 1) for i in range(ends)])  21.5 us
    pallas_call x1, Pallas kernels, all_convs(): pl.pallas_call(main_kernel, out_shape=(jax.ShapeDtypeStruct((4, 8, CH, LA...  17.5 us
    ppermute x3, starting transfers between devices, shift_pair(): from_prev = lax.ppermute(up, axis, [(i, i + 1) for i in range(ends)])  17 us
    ppermute x3, waiting for transfers between devices, shift_pair(): from_next = lax.ppermute(down, axis, [(i + 1, i) for i in range(ends)])  8.5 us
    unnamed x13, local copies, waits for them, and re-layouts  4.48 us
    ppermute x3, starting transfers between devices, shift_pair(): from_next = lax.ppermute(down, axis, [(i + 1, i) for i in range(ends)])  4.48 us
  transfers between devices with their start and end apart: 6, of which 4 were waited for; matrix products, arithmetic and copies ran while one was open for 5% of the time, Pallas kernels for 0%

commit v1 on v0

v1 whole, which is shorter than its diff:
```python
import jax
import jax.numpy as jnp
from jax import lax
from jax.experimental import pallas as pl
from jax.experimental.pallas import tpu as pltpu
from jax.sharding import PartitionSpec as P

ALL = ("gx", "gy", "gz")
CH = 32
LANES = 128


def shift_pair(up, down, axis):
    ends = lax.axis_size(axis) - 1
    from_prev = lax.ppermute(up, axis, [(i, i + 1) for i in range(ends)])
    from_next = lax.ppermute(down, axis, [(i + 1, i) for i in range(ends)])
    return from_prev, from_next


def pack_kernel(f_ref, left_ref, right_ref):
    lane = lax.broadcasted_iota(jnp.int32, (CH, LANES), 1)
    low = (lane & 7) < 4

    def edges(layer):
        tile = jnp.zeros((CH, LANES), jnp.float32)
        for row in range(16):
            slot = 8 * (row % 2) + row // 2
            rolled = pltpu.roll(f_ref[layer, row].astype(jnp.float32), (8 * slot + 4) % LANES, 1)
            tile = jnp.where(lane // 8 == slot, rolled, tile)
        return tile

    def group(g, carry):
        one, two = edges(2 * g), edges(2 * g + 1)
        right_ref[g] = jnp.where(low, one, pltpu.roll(two, 4, 1)).astype(jnp.bfloat16)
        left_ref[g] = jnp.where(low, pltpu.roll(two, LANES - 4, 1), one).astype(jnp.bfloat16)
        return carry

    lax.fori_loop(0, left_ref.shape[0], group, 0)


def pack_edges(f):
    groups = f.shape[0] // 2
    out = jax.ShapeDtypeStruct((groups, CH, LANES), jnp.bfloat16)
    return pl.pallas_call(
        pack_kernel,
        out_shape=(out, out),
        compiler_params=pltpu.CompilerParams(vmem_limit_bytes=40 << 20),
        name="pack_edges",
    )(f)


def roll(v, shift):
    return pltpu.roll(v, shift % LANES, 1)


def main_kernel(
    place, f_ref, rl_ref, rr_ref, w_ref, out_ref, sum_ref, edge, t_h, hid, hid_h, img, img_h, pul, pul_h
):
    lane = lax.broadcasted_iota(jnp.int32, (CH, LANES), 1)
    low = (lane & 7) < 4

    def unpack(g, carry):
        rl = rl_ref[g].astype(jnp.float32)
        rr = rr_ref[g].astype(jnp.float32)
        edge[2 * g] = jnp.where(low, rl, rr)
        edge[2 * g + 1] = jnp.where(low, roll(rl, -4), roll(rr, 4))
        return carry

    lax.fori_loop(0, rl_ref.shape[0], unpack, 0)

    def t_layer(t):
        return t + 2 + 4 * lax.shift_right_logical(t, 2)

    def s_layer(s):
        return s + 4 * lax.shift_right_logical(s + 2, 2)

    def t_halo(t, carry):
        tile = edge[t_layer(t)]
        for q, shift in enumerate((0, 64, -8, 56)):
            t_h[t, q * CH : (q + 1) * CH] = roll(tile, shift).astype(jnp.bfloat16)
        return carry

    lax.fori_loop(0, 12, t_halo, 0)

    wide = lax.broadcasted_iota(jnp.int32, (2 * CH, LANES), 1)
    wide8 = wide & 7
    first = wide == 0
    n = 2 * CH

    def convolve_layer(which, get, get_halo, m, pairs, put, put_halo):
        def columns(p):
            if p < 0:
                return jnp.concatenate([get_halo(m + a) for a in range(3)], axis=0)
            return jnp.concatenate([get(m + a, 2 * p) for a in range(3)], axis=0)

        cross = None
        halo = None
        tiles = list(range(-1, pairs))
        for start in range(0, len(tiles), 2):
            here = tiles[start : start + 2]
            rhs = jnp.concatenate([columns(p) for p in here], axis=1)
            g = jnp.dot(w_ref[which], rhs, preferred_element_type=jnp.float32)
            for k, p in enumerate(here):
                part = g[:, k * LANES : (k + 1) * LANES]
                before = roll(part[:n], 1)
                after = roll(part[2 * n :], -1)
                if p < 0:
                    cross = jnp.where(wide8 == 4, before, after)
                    halo = (
                        part[n : 2 * n]
                        + jnp.where(wide8 == 4, 0.0, before)
                        + jnp.where(wide8 == 3, 0.0, after)
                    )
                    continue
                mine = roll(cross, -(8 * p + 4))
                own = (
                    part[n : 2 * n]
                    + jnp.where(first, mine, before)
                    + jnp.where(wide == LANES - 1, mine, after)
                )
                put(p, own)
                if put_halo is not None:
                    give = roll(jnp.where(first, before, after), 8 * p + 4)
                    halo = halo + jnp.where((wide == 8 * p + 3) | (wide == 8 * p + 4), give, 0.0)
        if put_halo is not None:
            put_halo(halo)

    def store_halo(ref, m, v):
        for q, piece in enumerate((v[:CH], v[CH:], roll(v[:CH], -8), roll(v[CH:], -8))):
            ref[m, q * CH : (q + 1) * CH] = piece.astype(jnp.bfloat16)

    def store(ref, m, p, v):
        ref[m, pl.ds(2 * p, 2)] = v.astype(jnp.bfloat16).reshape(2, CH, LANES)

    def scaled(ref, ref_h, s, row):
        i = s_layer(s)

        def put(m):
            def own(p, v):
                slope = f_ref[i, pl.ds(2 * p + row, 2)].reshape(2 * CH, LANES)
                store(ref, m, p, slope.astype(jnp.float32) * v)

            return own

        def put_halo(m):
            def halo(v):
                tile = edge[i]
                q = row // 2
                slope = jnp.concatenate([roll(tile, 64 - 8 * q), roll(tile, -8 * (q + 1))], axis=0)
                store_halo(ref_h, m, slope * v)

            return halo

        return put, put_halo

    def rows_of(ref):
        return lambda t, r: ref[t, pl.ds(r, 4)].reshape(4 * CH, LANES)

    def field_rows(t, r):
        return f_ref[t_layer(t), pl.ds(r, 4)].reshape(4 * CH, LANES)

    def stage_hidden(m, carry):
        put, put_halo = scaled(hid, hid_h, m, 1)
        convolve_layer(0, field_rows, lambda t: t_h[t], m, 7, put(m), put_halo(m))
        return carry

    lax.fori_loop(0, 10, stage_hidden, 0)

    gx, gy, gz = place[0], place[1], place[2]
    nx, ny, nz = place[3], place[4], place[5]
    top_in = jnp.where(gy > 0, 1.0, 0.0)
    low_in = jnp.where(gy < ny, 1.0, 0.0)
    halo_in = jnp.where(wide8 < 4, jnp.where(gz > 0, 1.0, 0.0), jnp.where(gz < nz, 1.0, 0.0))
    halo_in = jnp.where(wide < 8, halo_in * top_in, halo_in)
    halo_in = jnp.where(wide >= 40, halo_in * low_in, halo_in)
    sum_ref[...] = jnp.zeros_like(sum_ref)

    def stage_image(m, carry):
        x_in = jnp.where(((m >= 2) | (gx > 0)) & ((m < 6) | (gx < nx)), 1.0, 0.0)
        x_own = jnp.where((m >= 2) & (m < 6), 1.0, 0.0)

        def put(p, v):
            keep = x_in * (top_in if p == 0 else low_in if p == 5 else 1.0)
            store(img, m, p, v * keep)
            if 1 <= p <= 4:
                square = v * v * x_own
                part = square[0:8]
                for q in range(1, 8):
                    part = part + square[8 * q : 8 * q + 8]
                sum_ref[...] += part

        def put_halo(v):
            store_halo(img_h, m, v * (halo_in * x_in))

        convolve_layer(1, rows_of(hid), lambda t: hid_h[t], m, 6, put, put_halo)
        return carry

    lax.fori_loop(0, 8, stage_image, 0)

    def stage_pulled(m, carry):
        put, put_halo = scaled(pul, pul_h, m + 2, 3)
        convolve_layer(2, rows_of(img), lambda t: img_h[t], m, 5, put(m), put_halo(m))
        return carry

    lax.fori_loop(0, 6, stage_pulled, 0)

    def stage_out(m, carry):
        def put(p, v):
            out_ref[m, pl.ds(2 * p, 2)] = v.reshape(2, CH, LANES)

        convolve_layer(3, rows_of(pul), lambda t: pul_h[t], m, 4, put, None)
        return carry

    lax.fori_loop(0, 4, stage_out, 0)


def all_convs(place, f, rl, rr, weights):
    layers = f.shape[0]

    def field(deep, rows):
        return [
            pltpu.VMEM((deep, rows, CH, LANES), jnp.bfloat16),
            pltpu.VMEM((deep, 4 * CH, LANES), jnp.bfloat16),
        ]

    return pl.pallas_call(
        main_kernel,
        out_shape=(
            jax.ShapeDtypeStruct((4, 8, CH, LANES), jnp.float32),
            jax.ShapeDtypeStruct((8, LANES), jnp.float32),
        ),
        in_specs=[pl.BlockSpec(memory_space=pltpu.SMEM)]
        + [pl.BlockSpec(memory_space=pltpu.VMEM)] * 4,
        scratch_shapes=[
            pltpu.VMEM((layers, CH, LANES), jnp.float32),
            pltpu.VMEM((12, 4 * CH, LANES), jnp.bfloat16),
        ]
        + field(10, 14)
        + field(8, 12)
        + field(6, 10),
        compiler_params=pltpu.CompilerParams(vmem_limit_bytes=48 << 20),
        name="all_convs",
    )(place, f, rl, rr, weights)


def pair_matrix(kernel):
    taps = kernel.reshape(3, 3, 3, CH, CH)
    none = ((0, 0), (0, 0), (0, 0), (0, 0))
    top = jnp.pad(taps, (none[0], (0, 1)) + none[:3])
    low = jnp.pad(taps, (none[0], (1, 0)) + none[:3])
    both = jnp.stack([top, low])
    return both.transpose(3, 0, 4, 1, 2, 5).reshape(6 * CH, 12 * CH)


def on_device(tangent, slopes, first_kernel, second_kernel):
    t = tangent.transpose(1, 2, 0, 3)
    s = slopes.transpose(1, 2, 0, 3)
    mine = jnp.concatenate([s[0:3], t, s[3:4]], axis=0)
    from_prev, from_next = shift_pair(mine[1:8], mine[0:7], "gx")
    deep = jnp.concatenate([from_prev, mine, from_next], axis=0)
    above, below = shift_pair(deep[:, 4:8], deep[:, 0:4], "gy")
    f = jnp.concatenate([above, deep, below], axis=1)
    left_edge, right_edge = pack_edges(f)
    rl, rr = shift_pair(right_edge, left_edge, "gz")

    adjoint = lambda k: k[::-1].transpose(0, 2, 1)
    weights = jnp.stack(
        [
            pair_matrix(first_kernel),
            pair_matrix(second_kernel),
            pair_matrix(adjoint(second_kernel)),
            pair_matrix(adjoint(first_kernel)),
        ]
    )
    place = jnp.stack(
        [lax.axis_index(a) for a in ALL] + [jnp.int32(lax.axis_size(a) - 1) for a in ALL]
    ).astype(jnp.int32)
    result, squares = all_convs(place, f, rl, rr, weights)

    part = jnp.sum(squares, axis=0, keepdims=True)
    for axes in (("gy", "gz"), "gx"):
        count = lax.axis_size(axes)
        spread = jnp.broadcast_to(part, (count, LANES))
        part = jnp.sum(lax.all_to_all(spread, axes, 0, 0, tiled=True), axis=0, keepdims=True)
    jvp_norm = jnp.sqrt(jnp.sum(part) + 1e-06)
    next_vector = result.transpose(2, 0, 1, 3) / jvp_norm
    return (next_vector, jvp_norm.reshape(1))


def solution(mesh):
    return jax.shard_map(
        on_device,
        mesh=mesh,
        in_specs=(P(None, "gx", "gy", "gz"), P(None, "gx", "gy", "gz"), P(), P()),
        out_specs=(P(None, "gx", "gy", "gz"), P()),
        check_vma=False,
    )
```

time: 131 us -> 133 us (1.015)
  Pallas kernels: 19 us -> 21 us
where the time goes in v1:
time: 133 us; the launch traced here: 132 us
  blocking collectives  41.4 us (31%)
  waiting for transfers between devices  30 us (23%)
  starting transfers between devices  21.4 us (16%)
  Pallas kernels  21 us (16%)
  local copies, waits for them, and re-layouts  10.6 us (8%)
  other arithmetic  5.2 us (4%)
  between operations  2.79 us (2%)
    all_to_all x2, blocking collectives, on_device(): lax.all_to_all(spread, axes, 0, 0, tiled=True)  41.4 us
    ppermute x3, waiting for transfers between devices, shift_pair(): from_prev = lax.ppermute(up, axis, [(i, i + 1) for i in range(ends)])  21.5 us
    pallas_call x1, Pallas kernels, all_convs(): pl.pallas_call(main_kernel, out_shape=(jax.ShapeDtypeStruct((4, 8, CH, LA...  18.7 us
    ppermute x3, starting transfers between devices, shift_pair(): from_prev = lax.ppermute(up, axis, [(i, i + 1) for i in range(ends)])  16.9 us
    ppermute x3, waiting for transfers between devices, shift_pair(): from_next = lax.ppermute(down, axis, [(i + 1, i) for i in range(ends)])  8.5 us
    unnamed x13, local copies, waits for them, and re-layouts  4.48 us
    ppermute x3, starting transfers between devices, shift_pair(): from_next = lax.ppermute(down, axis, [(i + 1, i) for i in range(ends)])  4.48 us
  transfers between devices with their start and end apart: 6, of which 4 were waited for; matrix products, arithmetic and copies ran while one was open for 5% of the time, Pallas kernels for 0%

profile of v1, /device:TPU:1, one launch (start us, length us, event | category | flops | bytes accessed | tf_op | source)
XLA Modules:
  0.0 132.5 jit_solution(16774806815677527831)
XLA Ops:
  0.6 0.0 copy-start.2
  0.6 1.1 copy.46
  1.8 1.1 copy.45
  2.8 0.8 pad_maximum_fusion.4
  3.7 6.2 %collective-permute-start = (bf16[7,8,32,128]{3,2,1,0:T(8,128)(2,1)S(1)}, bf16[7,8,32,128]{3,2,1,0:T(8,128)(2,1)}, u32[]{:S(2)}, u32[]{:S(2)}) collective-permute-start(bf16[7,8,32,128]{3,2,1,0:T(8,128)(2,1)S(1)} %get-tuple-element.19), channel_id=1, source_target_pairs={{0,16},{16,32},{32,48},{48,64},{64,80},{80,96},{96,112},{112,128},... | collective-permute-start | bytes 1376264 | tf_op jit(solution)/shard_map/ppermute | solution.py:15
  9.9 1.3 collective-permute-start.1
  11.2 0.0 copy-done.2
  11.2 0.2 copy.34
  11.4 0.0 copy-start.1
  11.5 0.3 pad_bitcast_fusion.3
  11.8 0.5 maximum_bitcast_fusion.2
  12.3 0.0 copy-start
  12.3 0.3 stack_reshape.14
  12.7 0.0 copy-done.1
  12.7 0.2 copy.36
  12.9 13.5 %collective-permute-done = bf16[7,8,32,128]{3,2,1,0:T(8,128)(2,1)} collective-permute-done((bf16[7,8,32,128]{3,2,1,0:T(8,128)(2,1)S(1)}, bf16[7,8,32,128]{3,2,1,0:T(8,128)(2,1)}, u32[]{:S(2)}, u32[]{:S(2)}) %collective-permute-start) | collective-permute-done | bytes 458784 | tf_op jit(solution)/shard_map/ppermute | solution.py:15
  26.4 1.0 constant_dynamic-update-slice_fusion.4
  27.4 0.0 copy-done
  27.5 0.1 constant_dynamic-update-slice_fusion.2
  27.6 0.0 collective-permute-done.1
  27.6 1.1 constant_dynamic-update-slice_fusion
  28.7 1.4 %fusion = (bf16[22,4,32,128]{3,2,1,0:T(8,128)(2,1)}, bf16[22,4,32,128]{3,2,1,0:T(8,128)(2,1)}) fusion(bf16[22,8,32,128]{3,2,1,0:T(8,128)(2,1)S(1)} %constant_dynamic-update-slice_fusion), kind=kLoop, calls=%fused_computation.25 | loop fusion | bytes 2883584 | tf_op jit(solution)/shard_map/slice | solution.py:261
  30.2 5.9 %collective-permute-start.2 = (bf16[22,4,32,128]{3,2,1,0:T(8,128)(2,1)}, bf16[22,4,32,128]{3,2,1,0:T(8,128)(2,1)}, u32[]{:S(2)}, u32[]{:S(2)}) collective-permute-start(bf16[22,4,32,128]{3,2,1,0:T(8,128)(2,1)} %get-tuple-element.16), channel_id=1, source_target_pairs={{0,4},{4,8},{8,12},{1,5},{5,9},{9,13},{2,6},{6,10},{10,14},{3,7},{... | collective-permute-start | bytes 2162696 | tf_op jit(solution)/shard_map/ppermute | solution.py:15
  36.0 1.3 collective-permute-start.3
  37.3 0.3 pad_bitcast_fusion.1
  37.6 0.5 maximum_bitcast_fusion.3
  38.1 0.3 stack_reshape.15
  38.5 0.2 copy.30
  38.6 0.3 pad_bitcast_fusion.7
  39.0 0.5 maximum_bitcast_fusion
  39.5 0.3 stack_reshape.12
  39.8 0.2 copy.32
  40.0 0.3 pad_bitcast_fusion.5
  40.3 0.5 maximum_bitcast_fusion.1
  40.8 0.3 stack_reshape.13
  41.2 0.1 stack.54.place
  41.3 8.0 %collective-permute-done.2 = bf16[22,4,32,128]{3,2,1,0:T(8,128)(2,1)} collective-permute-done((bf16[22,4,32,128]{3,2,1,0:T(8,128)(2,1)}, bf16[22,4,32,128]{3,2,1,0:T(8,128)(2,1)}, u32[]{:S(2)}, u32[]{:S(2)}) %collective-permute-start.2) | collective-permute-done | bytes 720928 | tf_op jit(solution)/shard_map/ppermute | solution.py:15
  49.3 4.7 %collective-permute-done.3 = bf16[22,4,32,128]{3,2,1,0:T(8,128)(2,1)} collective-permute-done((bf16[22,4,32,128]{3,2,1,0:T(8,128)(2,1)}, bf16[22,4,32,128]{3,2,1,0:T(8,128)(2,1)}, u32[]{:S(2)}, u32[]{:S(2)}) %collective-permute-start.3) | collective-permute-done | bytes 720928 | tf_op jit(solution)/shard_map/ppermute | solution.py:16
  54.0 1.6 %pad_maximum_fusion.f_ref = bf16[22,16,32,128]{3,2,1,0:T(8,128)(2,1)S(1)} fusion(bf16[22,4,32,128]{3,2,1,0:T(8,128)(2,1)} %collective-permute-done.3, bf16[22,8,32,128]{3,2,1,0:T(8,128)(2,1)S(1)} %constant_dynamic-update-slice_fusion, bf16[22,4,32,128]{3,2,1,0:T(8,128)(2,1)} %collective-permute-done.2), kind=kLoop, calls=%fused_computation | loop fusion | flops 2883584 | bytes 5767168 | tf_op jit(solution)/shard_map/concatenate | solution.py:262
  55.7 2.3 %pack_edges.1 = (bf16[11,32,128]{2,1,0:T(8,128)(2,1)S(1)}, bf16[11,32,128]{2,1,0:T(8,128)(2,1)S(1)}) custom-call(bf16[22,16,32,128]{3,2,1,0:T(8,128)(2,1)S(1)} %pad_maximum_fusion.f_ref), custom_call_target="tpu_custom_call" | custom-call | tf_op jit(solution)/shard_map/pack_edges/pallas_call | solution.py:44
  58.0 4.9 %collective-permute-start.4 = (bf16[11,32,128]{2,1,0:T(8,128)(2,1)S(1)}, bf16[11,32,128]{2,1,0:T(8,128)(2,1)S(1)}, u32[]{:S(2)}, u32[]{:S(2)}) collective-permute-start(bf16[11,32,128]{2,1,0:T(8,128)(2,1)S(1)} %get-tuple-element.6), channel_id=1, source_target_pairs={{0,1},{1,2},{2,3},{4,5},{5,6},{6,7},{8,9},{9,10},{10,11},{12,13},{... | collective-permute-start | bytes 270344 | tf_op jit(solution)/shard_map/ppermute | solution.py:15
  62.8 1.9 %collective-permute-start.5 = (bf16[11,32,128]{2,1,0:T(8,128)(2,1)S(1)}, bf16[11,32,128]{2,1,0:T(8,128)(2,1)S(1)}, u32[]{:S(2)}, u32[]{:S(2)}) collective-permute-start(bf16[11,32,128]{2,1,0:T(8,128)(2,1)S(1)} %get-tuple-element.7), channel_id=1, source_target_pairs={{1,0},{2,1},{3,2},{5,4},{6,5},{7,6},{9,8},{10,9},{11,10},{13,12},{... | collective-permute-start | bytes 270344 | tf_op jit(solution)/shard_map/ppermute | solution.py:16
  64.8 0.1 pad_maximum_fusion.1.w_ref
  64.9 0.0 collective-permute-done.4.rl_ref
  64.9 3.8 %collective-permute-done.5.rr_ref = bf16[11,32,128]{2,1,0:T(8,128)(2,1)S(1)} collective-permute-done((bf16[11,32,128]{2,1,0:T(8,128)(2,1)S(1)}, bf16[11,32,128]{2,1,0:T(8,128)(2,1)S(1)}, u32[]{:S(2)}, u32[]{:S(2)}) %collective-permute-start.5) | collective-permute-done | bytes 90144 | tf_op jit(solution)/shard_map/ppermute | solution.py:16
  68.7 18.7 %all_convs.1 = (f32[4,8,32,128]{3,2,1,0:T(8,128)S(1)}, f32[8,128]{1,0:T(8,128)S(1)}) custom-call(s32[6]{0:T(128)S(1)} %stack.54.place, bf16[22,16,32,128]{3,2,1,0:T(8,128)(2,1)S(1)} %pad_maximum_fusion.f_ref, bf16[11,32,128]{2,1,0:T(8,128)(2,1)S(1)} %collective-permute-done.4.rl_ref, bf16[11,32,128]{2,1,0:T(8,128)(2,1)S(1)} %collective-permute-done.5.rr_ref, ...), custom_call_target="tpu_custom_call" | custom-call | tf_op jit(solution)/shard_map/all_convs/pallas_call | solution.py:226
  87.4 8.7 %all_to_all.12 = f32[16,1,128]{2,1,0:T(1,128)S(1)} all-to-all(f32[16,1,128]{2,1,0:T(1,128)S(1)} %broadcast_in_dim.4), channel_id=1, replica_groups=mesh['gx'=32,'gy'=4,'gz'=4] {'gy','gz'}, dimensions={0} | all-to-all | bytes 16384 | tf_op jit(solution)/shard_map/all_to_all | solution.py:284
  96.2 32.7 %all_to_all.13 = f32[32,1,128]{2,1,0:T(1,128)S(1)} all-to-all(f32[32,1,128]{2,1,0:T(1,128)S(1)} %broadcast_in_dim.5), channel_id=1, replica_groups=mesh['gx'=32,'gy'=4,'gz'=4] {'gx'}, dimensions={0} | all-to-all | bytes 32768 | tf_op jit(solution)/shard_map/all_to_all | solution.py:284
  128.9 0.6 reduce_sum.33
  130.2 0.1 divide_bitcast_fusion
  130.2 1.1 copy.40
  (11 shorter events, 0.2 us)
Async XLA Ops:
  0.6 10.6 %copy-start.2 = (bf16[27,32,32]{2,1,0:T(8,128)(2,1)S(1)}, bf16[27,32,32]{2,1,0:T(8,128)(2,1)}, u32[]{:S(2)}) copy-start(bf16[27,32,32]{2,1,0:T(8,128)(2,1)} %param.7) | copy-start | bytes 165892
  3.7 22.7 %collective-permute-start = (bf16[7,8,32,128]{3,2,1,0:T(8,128)(2,1)S(1)}, bf16[7,8,32,128]{3,2,1,0:T(8,128)(2,1)}, u32[]{:S(2)}, u32[]{:S(2)}) collective-permute-start(bf16[7,8,32,128]{3,2,1,0:T(8,128)(2,1)S(1)} %get-tuple-element.19), channel_id=1, source_target_pairs={{0,16},{16,32},{32,48},{48,64},{64,80},{80,96},{96,112},{112,128},... | collective-permute-start | bytes 1376264 | tf_op jit(solution)/shard_map/ppermute | solution.py:15
  9.9 17.7 %collective-permute-start.1 = (bf16[7,8,32,128]{3,2,1,0:T(8,128)(2,1)}, bf16[7,8,32,128]{3,2,1,0:T(8,128)(2,1)}, u32[]{:S(2)}, u32[]{:S(2)}) collective-permute-start(bf16[7,8,32,128]{3,2,1,0:T(8,128)(2,1)} %get-tuple-element.18), channel_id=1, source_target_pairs={{16,0},{32,16},{48,32},{64,48},{80,64},{96,80},{112,96},{128,112},... | collective-permute-start | bytes 1376264 | tf_op jit(solution)/shard_map/ppermute | solution.py:16
  11.4 1.2 copy-start.1
  12.3 15.2 %copy-start = (bf16[32,4,8,128]{3,2,1,0:T(8,128)(2,1)S(1)}, bf16[32,4,8,128]{3,2,1,0:T(8,128)(2,1)}, u32[]{:S(2)}) copy-start(bf16[32,4,8,128]{3,2,1,0:T(8,128)(2,1)} %param.4) | copy-start | bytes 786436
  30.2 19.2 %collective-permute-start.2 = (bf16[22,4,32,128]{3,2,1,0:T(8,128)(2,1)}, bf16[22,4,32,128]{3,2,1,0:T(8,128)(2,1)}, u32[]{:S(2)}, u32[]{:S(2)}) collective-permute-start(bf16[22,4,32,128]{3,2,1,0:T(8,128)(2,1)} %get-tuple-element.16), channel_id=1, source_target_pairs={{0,4},{4,8},{8,12},{1,5},{5,9},{9,13},{2,6},{6,10},{10,14},{3,7},{... | collective-permute-start | bytes 2162696 | tf_op jit(solution)/shard_map/ppermute | solution.py:15
  36.0 18.0 %collective-permute-start.3 = (bf16[22,4,32,128]{3,2,1,0:T(8,128)(2,1)}, bf16[22,4,32,128]{3,2,1,0:T(8,128)(2,1)}, u32[]{:S(2)}, u32[]{:S(2)}) collective-permute-start(bf16[22,4,32,128]{3,2,1,0:T(8,128)(2,1)} %get-tuple-element.17), channel_id=1, source_target_pairs={{4,0},{8,4},{12,8},{5,1},{9,5},{13,9},{6,2},{10,6},{14,10},{7,3},{... | collective-permute-start | bytes 2162696 | tf_op jit(solution)/shard_map/ppermute | solution.py:16
  58.0 6.9 %collective-permute-start.4 = (bf16[11,32,128]{2,1,0:T(8,128)(2,1)S(1)}, bf16[11,32,128]{2,1,0:T(8,128)(2,1)S(1)}, u32[]{:S(2)}, u32[]{:S(2)}) collective-permute-start(bf16[11,32,128]{2,1,0:T(8,128)(2,1)S(1)} %get-tuple-element.6), channel_id=1, source_target_pairs={{0,1},{1,2},{2,3},{4,5},{5,6},{6,7},{8,9},{9,10},{10,11},{12,13},{... | collective-permute-start | bytes 270344 | tf_op jit(solution)/shard_map/ppermute | solution.py:15
  62.8 5.8 %collective-permute-start.5 = (bf16[11,32,128]{2,1,0:T(8,128)(2,1)S(1)}, bf16[11,32,128]{2,1,0:T(8,128)(2,1)S(1)}, u32[]{:S(2)}, u32[]{:S(2)}) collective-permute-start(bf16[11,32,128]{2,1,0:T(8,128)(2,1)S(1)} %get-tuple-element.7), channel_id=1, source_target_pairs={{1,0},{2,1},{3,2},{5,4},{6,5},{7,6},{9,8},{10,9},{11,10},{13,12},{... | collective-permute-start | bytes 270344 | tf_op jit(solution)/shard_map/ppermute | solution.py:16

commit v2 on v1

v2 whole, which is shorter than its diff:
```python
import jax
import jax.numpy as jnp
from jax import lax
from jax.experimental import pallas as pl
from jax.experimental.pallas import tpu as pltpu
from jax.sharding import PartitionSpec as P

ALL = ("gx", "gy", "gz")
CH = 32
LANES = 128


def shift_pair(up, down, axis):
    ends = lax.axis_size(axis) - 1
    from_prev = lax.ppermute(up, axis, [(i, i + 1) for i in range(ends)])
    from_next = lax.ppermute(down, axis, [(i + 1, i) for i in range(ends)])
    return from_prev, from_next


def roll(v, shift):
    return pltpu.roll(v, shift % LANES, 1)


def slot_of(row):
    return 8 * (row % 2) + row // 2


def gather_edges(tile, rows, load, lane):
    for row in rows:
        slot = slot_of(row)
        rolled = roll(load(row).astype(jnp.float32), 8 * slot + 4)
        tile = jnp.where(lane // 8 == slot, rolled, tile)
    return tile


def pack_mid_kernel(prev_ref, mine_ref, next_ref, tile_ref):
    lane = lax.broadcasted_iota(jnp.int32, (CH, LANES), 1)

    def layers(ref, base):
        def body(i, carry):
            tile = gather_edges(
                jnp.zeros((CH, LANES), jnp.float32), range(4, 12), lambda r: ref[i, r - 4], lane
            )
            tile_ref[base + i] = tile
            return carry

        lax.fori_loop(0, ref.shape[0], body, 0)

    layers(prev_ref, 0)
    layers(mine_ref, 7)
    layers(next_ref, 15)


def pack_mid(prev, mine, following):
    return pl.pallas_call(
        pack_mid_kernel,
        out_shape=jax.ShapeDtypeStruct((22, CH, LANES), jnp.float32),
        compiler_params=pltpu.CompilerParams(vmem_limit_bytes=16 << 20),
        cost_estimate=pl.CostEstimate(flops=0, bytes_accessed=1 << 21, transcendentals=0),
        name="pack_mid",
    )(prev, mine, following)


def pack_kernel(a1, b1, a2, b2, tile_ref, left_ref, right_ref, full):
    lane = lax.broadcasted_iota(jnp.int32, (CH, LANES), 1)
    low = (lane & 7) < 4

    def layers(above, below, base, count, skip):
        def body(i, carry):
            def load(r):
                return above[i + skip, r] if r < 4 else below[i + skip, r - 12]

            rows = list(range(4)) + list(range(12, 16))
            full[base + i] = gather_edges(tile_ref[base + i], rows, load, lane)
            return carry

        lax.fori_loop(0, count, body, 0)

    layers(a2, b2, 0, 7, 0)
    layers(a1, b1, 7, 8, 0)
    layers(a2, b2, 15, 7, 7)

    def group(g, carry):
        one, two = full[2 * g], full[2 * g + 1]
        right_ref[g] = jnp.where(low, one, roll(two, 4)).astype(jnp.bfloat16)
        left_ref[g] = jnp.where(low, roll(two, -4), one).astype(jnp.bfloat16)
        return carry

    lax.fori_loop(0, left_ref.shape[0], group, 0)


def pack_edges(a1, b1, a2, b2, tiles):
    out = jax.ShapeDtypeStruct((11, CH, LANES), jnp.bfloat16)
    return pl.pallas_call(
        pack_kernel,
        out_shape=(out, out),
        scratch_shapes=[pltpu.VMEM((22, CH, LANES), jnp.float32)],
        compiler_params=pltpu.CompilerParams(vmem_limit_bytes=16 << 20),
        cost_estimate=pl.CostEstimate(flops=0, bytes_accessed=1 << 21, transcendentals=0),
        name="pack_edges",
    )(a1, b1, a2, b2, tiles)


def convolve_layer(w, get, get_halo, m, pairs, put, put_halo):
    wide = lax.broadcasted_iota(jnp.int32, (2 * CH, LANES), 1)
    wide8 = wide & 7
    first = wide == 0
    n = 2 * CH

    def columns(p):
        if p < 0:
            return jnp.concatenate([get_halo(m + a) for a in range(3)], axis=0)
        return jnp.concatenate([get(m + a, 2 * p) for a in range(3)], axis=0)

    cross = None
    halo = None
    tiles = [-1] + list(pairs)
    for start in range(0, len(tiles), 2):
        here = tiles[start : start + 2]
        rhs = jnp.concatenate([columns(p) for p in here], axis=1)
        g = jnp.dot(w, rhs, preferred_element_type=jnp.float32)
        for k, p in enumerate(here):
            part = g[:, k * LANES : (k + 1) * LANES]
            before = roll(part[:n], 1)
            after = roll(part[2 * n :], -1)
            if p < 0:
                cross = jnp.where(wide8 == 4, before, after)
                halo = (
                    part[n : 2 * n]
                    + jnp.where(wide8 == 4, 0.0, before)
                    + jnp.where(wide8 == 3, 0.0, after)
                )
                continue
            mine = roll(cross, -(8 * p + 4))
            own = (
                part[n : 2 * n]
                + jnp.where(first, mine, before)
                + jnp.where(wide == LANES - 1, mine, after)
            )
            put(p, own)
            if put_halo is not None:
                give = roll(jnp.where(first, before, after), 8 * p + 4)
                halo = halo + jnp.where((wide == 8 * p + 3) | (wide == 8 * p + 4), give, 0.0)
    if put_halo is not None:
        put_halo(halo)


def store_halo(ref, m, v):
    for q, piece in enumerate((v[:CH], v[CH:], roll(v[:CH], -8), roll(v[CH:], -8))):
        ref[m, q * CH : (q + 1) * CH] = piece.astype(jnp.bfloat16)


def store(ref, m, p, v):
    ref[m, pl.ds(2 * p, 2)] = v.astype(jnp.bfloat16).reshape(2, CH, LANES)


def rows_of(ref):
    return lambda t, r: ref[t, pl.ds(r, 4)].reshape(4 * CH, LANES)


def first_kernel_body(
    prev, mine, following, a1, b1, a2, b2, rl_ref, rr_ref, w_ref,
    hid, hid_h, own_ref, own_h, slope_ref, slope_h, sum_ref,
    f_ref, edge, t_h, sems,
):
    moves = [
        (prev, f_ref.at[0:7, 4:12]),
        (mine, f_ref.at[7:15, 4:12]),
        (following, f_ref.at[15:22, 4:12]),
        (a1, f_ref.at[7:15, 0:4]),
        (b1, f_ref.at[7:15, 12:16]),
        (a2.at[0:7], f_ref.at[0:7, 0:4]),
        (a2.at[7:14], f_ref.at[15:22, 0:4]),
        (b2.at[0:7], f_ref.at[0:7, 12:16]),
        (b2.at[7:14], f_ref.at[15:22, 12:16]),
    ]
    copies = [pltpu.make_async_copy(x, y, sems.at[i]) for i, (x, y) in enumerate(moves)]
    for copy in copies:
        copy.start()

    lane = lax.broadcasted_iota(jnp.int32, (CH, LANES), 1)
    low = (lane & 7) < 4

    def unpack(g, carry):
        rl = rl_ref[g].astype(jnp.float32)
        rr = rr_ref[g].astype(jnp.float32)
        edge[2 * g] = jnp.where(low, rl, rr)
        edge[2 * g + 1] = jnp.where(low, roll(rl, -4), roll(rr, 4))
        return carry

    lax.fori_loop(0, rl_ref.shape[0], unpack, 0)

    def t_layer(t):
        return t + 2 + 4 * lax.shift_right_logical(t, 2)

    def s_layer(s):
        return s + 4 * lax.shift_right_logical(s + 2, 2)

    def t_halo(t, carry):
        tile = edge[t_layer(t)]
        for q, shift in enumerate((0, 64, -8, 56)):
            t_h[t, q * CH : (q + 1) * CH] = roll(tile, shift).astype(jnp.bfloat16)
        return carry

    lax.fori_loop(0, 12, t_halo, 0)
    for copy in copies:
        copy.wait()

    def slope_halo(i, row):
        tile = edge[i]
        q = row // 2
        return jnp.concatenate([roll(tile, 64 - 8 * q), roll(tile, -8 * (q + 1))], axis=0)

    def keep_slopes(m, carry):
        i = s_layer(m + 2)
        slope_ref[m] = f_ref[i, 3:13]
        slope_h[m] = slope_halo(i, 3)
        return carry

    lax.fori_loop(0, 6, keep_slopes, 0)

    def field_rows(t, r):
        return f_ref[t_layer(t), pl.ds(r, 4)].reshape(4 * CH, LANES)

    def stage_hidden(m, carry):
        i = s_layer(m)

        def put(p, v):
            slope = f_ref[i, pl.ds(2 * p + 1, 2)].reshape(2 * CH, LANES)
            store(hid, m, p, slope.astype(jnp.float32) * v)

        def put_halo(v):
            store_halo(hid_h, m, slope_halo(i, 1) * v)

        convolve_layer(w_ref[0], field_rows, lambda t: t_h[t], m, range(7), put, put_halo)
        return carry

    lax.fori_loop(0, 10, stage_hidden, 0)
    sum_ref[...] = jnp.zeros_like(sum_ref)

    def stage_own(m, carry):
        def put(p, v):
            own_ref[m, pl.ds(2 * p - 2, 2)] = v.astype(jnp.bfloat16).reshape(2, CH, LANES)
            square = v * v
            part = square[0:8]
            for q in range(1, 8):
                part = part + square[8 * q : 8 * q + 8]
            sum_ref[...] += part

        def put_halo(v):
            own_h[m] = v

        convolve_layer(
            w_ref[1], rows_of(hid), lambda t: hid_h[t], m + 2, range(1, 5), put, put_halo
        )
        return carry

    lax.fori_loop(0, 4, stage_own, 0)


def first_convs(pieces, rl, rr, weights):
    shape = jax.ShapeDtypeStruct
    return pl.pallas_call(
        first_kernel_body,
        out_shape=(
            shape((10, 14, CH, LANES), jnp.bfloat16),
            shape((10, 4 * CH, LANES), jnp.bfloat16),
            shape((4, 8, CH, LANES), jnp.bfloat16),
            shape((4, 2 * CH, LANES), jnp.float32),
            shape((6, 10, CH, LANES), jnp.bfloat16),
            shape((6, 2 * CH, LANES), jnp.float32),
            shape((8, LANES), jnp.float32),
        ),
        in_specs=[pl.BlockSpec(memory_space=pl.ANY)] * 7
        + [pl.BlockSpec(memory_space=pltpu.VMEM)] * 3,
        scratch_shapes=[
            pltpu.VMEM((22, 16, CH, LANES), jnp.bfloat16),
            pltpu.VMEM((22, CH, LANES), jnp.float32),
            pltpu.VMEM((12, 4 * CH, LANES), jnp.bfloat16),
            pltpu.SemaphoreType.DMA((9,)),
        ],
        compiler_params=pltpu.CompilerParams(vmem_limit_bytes=16 << 20),
        cost_estimate=pl.CostEstimate(flops=8 << 30, bytes_accessed=8 << 20, transcendentals=0),
        name="first_convs",
    )(*pieces, rl, rr, weights)


def second_kernel_body(
    place, hid, hid_h, own_ref, own_h, slope_ref, slope_h, w_ref, out_ref, img, img_h, pul, pul_h
):
    wide = lax.broadcasted_iota(jnp.int32, (2 * CH, LANES), 1)
    wide8 = wide & 7
    gx, gy, gz = place[0], place[1], place[2]
    nx, ny, nz = place[3], place[4], place[5]
    top_in = jnp.where(gy > 0, 1.0, 0.0)
    low_in = jnp.where(gy < ny, 1.0, 0.0)
    halo_in = jnp.where(wide8 < 4, jnp.where(gz > 0, 1.0, 0.0), jnp.where(gz < nz, 1.0, 0.0))
    halo_in = jnp.where(wide < 8, halo_in * top_in, halo_in)
    halo_in = jnp.where(wide >= 40, halo_in * low_in, halo_in)

    def image_layer(m, x_in, pairs, merge):
        def put(p, v):
            keep = x_in * (top_in if p == 0 else low_in if p == 5 else 1.0)
            store(img, m, p, v * keep)

        def put_halo(v):
            store_halo(img_h, m, merge(v) * (halo_in * x_in))

        convolve_layer(w_ref[0], rows_of(hid), lambda t: hid_h[t], m, pairs, put, put_halo)

    def stage_ends(i, carry):
        m = jnp.where(i < 2, i, i + 4)
        x_in = jnp.where(((i >= 2) | (gx > 0)) & ((i < 2) | (gx < nx)), 1.0, 0.0)
        image_layer(m, x_in, range(6), lambda v: v)
        return carry

    lax.fori_loop(0, 4, stage_ends, 0)

    def stage_rim(i, carry):
        m = i + 2
        img[m, 2:10] = own_ref[i]
        outer = (wide < 8) | (wide >= 40)
        image_layer(m, 1.0, (0, 5), lambda v: jnp.where(outer, v, own_h[i]))
        return carry

    lax.fori_loop(0, 4, stage_rim, 0)

    def stage_pulled(m, carry):
        def put(p, v):
            slope = slope_ref[m, pl.ds(2 * p, 2)].reshape(2 * CH, LANES)
            store(pul, m, p, slope.astype(jnp.float32) * v)

        def put_halo(v):
            store_halo(pul_h, m, slope_h[m] * v)

        convolve_layer(w_ref[1], rows_of(img), lambda t: img_h[t], m, range(5), put, put_halo)
        return carry

    lax.fori_loop(0, 6, stage_pulled, 0)

    def stage_out(m, carry):
        def put(p, v):
            out_ref[m, pl.ds(2 * p, 2)] = v.reshape(2, CH, LANES)

        convolve_layer(w_ref[2], rows_of(pul), lambda t: pul_h[t], m, range(4), put, None)
        return carry

    lax.fori_loop(0, 4, stage_out, 0)


def second_convs(place, fields, weights):
    return pl.pallas_call(
        second_kernel_body,
        out_shape=jax.ShapeDtypeStruct((4, 8, CH, LANES), jnp.float32),
        in_specs=[pl.BlockSpec(memory_space=pltpu.SMEM)]
        + [pl.BlockSpec(memory_space=pltpu.VMEM)] * 7,
        scratch_shapes=[
            pltpu.VMEM((8, 12, CH, LANES), jnp.bfloat16),
            pltpu.VMEM((8, 4 * CH, LANES), jnp.bfloat16),
            pltpu.VMEM((6, 10, CH, LANES), jnp.bfloat16),
            pltpu.VMEM((6, 4 * CH, LANES), jnp.bfloat16),
        ],
        compiler_params=pltpu.CompilerParams(vmem_limit_bytes=16 << 20),
        cost_estimate=pl.CostEstimate(flops=8 << 30, bytes_accessed=4 << 20, transcendentals=0),
        name="second_convs",
    )(place, *fields, weights)


def pair_matrix(kernel):
    taps = kernel.reshape(3, 3, 3, CH, CH)
    none = ((0, 0), (0, 0), (0, 0), (0, 0))
    top = jnp.pad(taps, (none[0], (0, 1)) + none[:3])
    low = jnp.pad(taps, (none[0], (1, 0)) + none[:3])
    both = jnp.stack([top, low])
    return both.transpose(3, 0, 4, 1, 2, 5).reshape(6 * CH, 12 * CH)


def on_device(tangent, slopes, first_kernel, second_kernel):
    t = tangent.transpose(1, 2, 0, 3)
    s = slopes.transpose(1, 2, 0, 3)
    mine = jnp.concatenate([s[0:3], t, s[3:4]], axis=0)
    prev, following = shift_pair(mine[1:8], mine[0:7], "gx")
    a1, b1 = shift_pair(mine[:, 4:8], mine[:, 0:4], "gy")
    to_below = jnp.concatenate([prev[:, 4:8], following[:, 4:8]], axis=0)
    to_above = jnp.concatenate([prev[:, 0:4], following[:, 0:4]], axis=0)
    a2, b2 = shift_pair(to_below, to_above, "gy")
    tiles = pack_mid(prev, mine, following)
    left_edge, right_edge = pack_edges(a1, b1, a2, b2, tiles)
    rl, rr = shift_pair(right_edge, left_edge, "gz")

    adjoint = lambda k: k[::-1].transpose(0, 2, 1)
    second = pair_matrix(second_kernel)
    forward = jnp.stack([pair_matrix(first_kernel), second])
    backward = jnp.stack(
        [second, pair_matrix(adjoint(second_kernel)), pair_matrix(adjoint(first_kernel))]
    )
    place = jnp.stack(
        [lax.axis_index(a) for a in ALL] + [jnp.int32(lax.axis_size(a) - 1) for a in ALL]
    ).astype(jnp.int32)
    *fields, squares = first_convs((prev, mine, following, a1, b1, a2, b2), rl, rr, forward)

    def exchange(part, axes):
        count = lax.axis_size(axes)
        spread = jnp.broadcast_to(part, (count, LANES))
        return jnp.sum(lax.all_to_all(spread, axes, 0, 0, tiled=True), axis=0, keepdims=True)

    part = exchange(jnp.sum(squares, axis=0, keepdims=True), ("gy", "gz"))
    part, *fields = lax.optimization_barrier((part, *fields))
    result = second_convs(place, fields, backward)
    part = exchange(part, "gx")
    jvp_norm = jnp.sqrt(jnp.sum(part) + 1e-06)
    next_vector = result.transpose(2, 0, 1, 3) / jvp_norm
    return (next_vector, jvp_norm.reshape(1))


def solution(mesh):
    return jax.shard_map(
        on_device,
        mesh=mesh,
        in_specs=(P(None, "gx", "gy", "gz"), P(None, "gx", "gy", "gz"), P(), P()),
        out_specs=(P(None, "gx", "gy", "gz"), P()),
        check_vma=False,
    )
```

time: 133 us -> 124 us (0.932)
  blocking collectives: 41.4 us -> 0 us
  starting transfers between devices: 21.4 us -> 48.4 us
  waiting for transfers between devices: 30 us -> 15.9 us
  local copies, waits for them, and re-layouts: 10.6 us -> 22.7 us
  Pallas kernels: 21 us -> 25.4 us
  other arithmetic: 5.2 us -> 7.99 us
    all_to_all x2 -> x0, blocking collectives: 41.4 us -> none  [on_device(): lax.all_to_all(spread, axes, 0, 0, tiled=True)]
    all_to_all x0 -> x2, starting transfers between devices: none -> 24.8 us  [exchange(): lax.all_to_all(spread, axes, 0, 0, tiled=True)]
    ppermute x3 -> x4, waiting for transfers between devices: 21.5 us -> 7.78 us  [shift_pair(): from_prev = lax.ppermute(up, axis, [(i, i + 1) for i in range(ends)])]
    unnamed x13 -> x31, local copies, waits for them, and re-layouts: 4.48 us -> 9.55 us
    another operation x5, local copies, waits for them, and re-layouts: 1.35 us -> 6.38 us  [the longest x2 3.22 us: on_device(): forward = jnp.stack([pair_matrix(first_kernel), second])]
    ppermute x3 -> x4, waiting for transfers between devices: 8.5 us -> 3.85 us  [shift_pair(): from_next = lax.ppermute(down, axis, [(i + 1, i) for i in range(ends)])]
    pallas_call x2 -> x4, Pallas kernels: 21 us -> 25.4 us  [the longest x1 11.1 us: first_convs(): pl.pallas_call(first_kernel_body, out_shape=(shape((10, 14, CH, LANES), j...]
    all_to_all x0 -> x2, waiting for transfers between devices: none -> 4.26 us  [exchange(): lax.all_to_all(spread, axes, 0, 0, tiled=True)]
  transfers between devices with their start and end apart: 6 -> 10, of which waited for: 4 -> 3; matrix products, arithmetic and copies ran while one was open for 5% -> 15% of each run, Pallas kernels for 0% -> 9%
where the time goes in v2:
time: 124 us; the launch traced here: 123 us
  starting transfers between devices  48.4 us (39%)
  Pallas kernels  25.4 us (20%)
  local copies, waits for them, and re-layouts  22.7 us (18%)
  waiting for transfers between devices  15.9 us (13%)
  other arithmetic  7.99 us (6%)
  between operations  2.86 us (2%)
    all_to_all x2, starting transfers between devices, exchange(): lax.all_to_all(spread, axes, 0, 0, tiled=True)  24.8 us
    ppermute x4, starting transfers between devices, shift_pair(): from_prev = lax.ppermute(up, axis, [(i, i + 1) for i in range(ends)])  17.8 us
    pallas_call x1, Pallas kernels, first_convs(): pl.pallas_call(first_kernel_body, out_shape=(shape((10, 14, CH, LANES), j...  11.1 us
    pallas_call x1, Pallas kernels, second_convs(): pl.pallas_call(second_kernel_body, out_shape=jax.ShapeDtypeStruct((4, 8,...  9.69 us
    unnamed x31, local copies, waits for them, and re-layouts  9.55 us
    ppermute x4, waiting for transfers between devices, shift_pair(): from_prev = lax.ppermute(up, axis, [(i, i + 1) for i in range(ends)])  7.78 us
    ppermute x4, starting transfers between devices, shift_pair(): from_next = lax.ppermute(down, axis, [(i + 1, i) for i in range(ends)])  5.9 us
    all_to_all x2, waiting for transfers between devices, exchange(): lax.all_to_all(spread, axes, 0, 0, tiled=True)  4.26 us
  transfers between devices with their start and end apart: 10, of which 3 were waited for; matrix products, arithmetic and copies ran while one was open for 15% of the time, Pallas kernels for 9%

profile of v2, /device:TPU:1, one launch (start us, length us, event | category | flops | bytes accessed | tf_op | source)
XLA Modules:
  0.0 123.3 jit_solution(1845929247488775217)
XLA Ops:
  0.6 1.1 copy.44
  1.8 0.1 copy.43
  1.9 0.1 pad_maximum_fusion.mine_ref.mine
  2.0 0.8 slice.40
  2.8 5.6 %collective-permute-start = (bf16[7,8,32,128]{3,2,1,0:T(8,128)(2,1)}, bf16[7,8,32,128]{3,2,1,0:T(8,128)(2,1)S(1)}, u32[]{:S(2)}, u32[]{:S(2)}) collective-permute-start(bf16[7,8,32,128]{3,2,1,0:T(8,128)(2,1)} %slice.40), channel_id=1, source_target_pairs={{0,16},{16,32},{32,48},{48,64},{64,80},{80,96},{96,112},{112,128},... | collective-permute-start | bytes 1376264 | tf_op jit(solution)/shard_map/ppermute | solution.py:15
  8.4 0.8 pad_maximum_fusion.1
  9.2 1.4 %collective-permute-start.1 = (bf16[7,8,32,128]{3,2,1,0:T(8,128)(2,1)}, bf16[7,8,32,128]{3,2,1,0:T(8,128)(2,1)S(1)}, u32[]{:S(2)}, u32[]{:S(2)}) collective-permute-start(bf16[7,8,32,128]{3,2,1,0:T(8,128)(2,1)} %pad_maximum_fusion.1), channel_id=1, source_target_pairs={{16,0},{32,16},{48,32},{64,48},{80,64},{96,80},{112,96},{128,112},... | collective-permute-start | bytes 1376264 | tf_op jit(solution)/shard_map/ppermute | solution.py:16
  10.7 0.8 fusion
  11.5 3.2 %collective-permute-start.2 = (bf16[8,4,32,128]{3,2,1,0:T(8,128)(2,1)}, bf16[8,4,32,128]{3,2,1,0:T(8,128)(2,1)S(1)}, u32[]{:S(2)}, u32[]{:S(2)}) collective-permute-start(bf16[8,4,32,128]{3,2,1,0:T(8,128)(2,1)} %get-tuple-element.41), channel_id=1, source_target_pairs={{0,4},{4,8},{8,12},{1,5},{5,9},{9,13},{2,6},{6,10},{10,14},{3,7},{... | collective-permute-start | bytes 786440 | tf_op jit(solution)/shard_map/ppermute | solution.py:15
  14.7 1.3 %collective-permute-start.3 = (bf16[8,4,32,128]{3,2,1,0:T(8,128)(2,1)}, bf16[8,4,32,128]{3,2,1,0:T(8,128)(2,1)S(1)}, u32[]{:S(2)}, u32[]{:S(2)}) collective-permute-start(bf16[8,4,32,128]{3,2,1,0:T(8,128)(2,1)} %get-tuple-element.40), channel_id=1, source_target_pairs={{4,0},{8,4},{12,8},{5,1},{9,5},{13,9},{6,2},{10,6},{14,10},{7,3},{... | collective-permute-start | bytes 786440 | tf_op jit(solution)/shard_map/ppermute | solution.py:16
  16.1 0.2 copy.32
  16.2 0.2 copy.30
  16.4 0.2 copy.35
  16.6 0.3 pad_bitcast_fusion.5
  16.9 0.3 pad_bitcast_fusion.7
  17.3 0.3 pad_bitcast_fusion.3
  17.7 0.5 maximum_bitcast_fusion.1
  18.1 7.8 %collective-permute-done.prev_ref.prev = bf16[7,8,32,128]{3,2,1,0:T(8,128)(2,1)S(1)} collective-permute-done((bf16[7,8,32,128]{3,2,1,0:T(8,128)(2,1)}, bf16[7,8,32,128]{3,2,1,0:T(8,128)(2,1)S(1)}, u32[]{:S(2)}, u32[]{:S(2)}) %collective-permute-start) | collective-permute-done | bytes 458784 | tf_op jit(solution)/shard_map/ppermute | solution.py:15
  25.9 0.0 collective-permute-done.1.next_ref.following
  26.0 0.8 pad_maximum_fusion.2
  26.8 5.0 %collective-permute-start.4 = (bf16[14,4,32,128]{3,2,1,0:T(8,128)(2,1)}, bf16[14,4,32,128]{3,2,1,0:T(8,128)(2,1)S(1)}, u32[]{:S(2)}, u32[]{:S(2)}) collective-permute-start(bf16[14,4,32,128]{3,2,1,0:T(8,128)(2,1)} %pad_maximum_fusion.2), channel_id=1, source_target_pairs={{0,4},{4,8},{8,12},{1,5},{5,9},{9,13},{2,6},{6,10},{10,14},{3,7},{... | collective-permute-start | bytes 1376264 | tf_op jit(solution)/shard_map/ppermute | solution.py:15
  31.8 0.8 pad_maximum_fusion.3
  32.7 1.3 %collective-permute-start.5 = (bf16[14,4,32,128]{3,2,1,0:T(8,128)(2,1)}, bf16[14,4,32,128]{3,2,1,0:T(8,128)(2,1)S(1)}, u32[]{:S(2)}, u32[]{:S(2)}) collective-permute-start(bf16[14,4,32,128]{3,2,1,0:T(8,128)(2,1)} %pad_maximum_fusion.3), channel_id=1, source_target_pairs={{4,0},{8,4},{12,8},{5,1},{9,5},{13,9},{6,2},{10,6},{14,10},{7,3},{... | collective-permute-start | bytes 1376264 | tf_op jit(solution)/shard_map/ppermute | solution.py:16
  33.9 1.3 %maximum_bitcast_fusion = bf16[3,2,32,3,4,32]{5,4,3,2,1,0:T(4,128)(2,1)} fusion(bf16[1,3,4,3,32,32]{5,2,1,4,0,3:T(4,128)(2,1)S(1)} %get-tuple-element.51, bf16[1,3,4,3,32,32]{5,2,1,4,0,3:T(4,128)(2,1)S(1)} %get-tuple-element.50), kind=kLoop, calls=%fused_computation | loop fusion | flops 73728 | bytes 294912 | tf_op jit(solution)/shard_map/transpose | solution.py:375
  35.3 1.3 %maximum_bitcast_fusion.2 = bf16[3,2,32,3,4,32]{5,4,3,2,1,0:T(4,128)(2,1)} fusion(bf16[1,3,4,3,32,32]{5,2,1,4,0,3:T(4,128)(2,1)S(1)} %get-tuple-element.47, bf16[1,3,4,3,32,32]{5,2,1,4,0,3:T(4,128)(2,1)S(1)} %get-tuple-element.46), kind=kLoop, calls=%fused_computation.2 | loop fusion | flops 73728 | bytes 294912 | tf_op jit(solution)/shard_map/transpose | solution.py:375
  36.6 1.6 %rev.7 = bf16[27,32,32]{2,1,0:T(8,128)(2,1)} reverse(bf16[27,32,32]{2,1,0:T(8,128)(2,1)} %param.6), dimensions={0} | reverse | bytes 110592 | tf_op jit(solution)/shard_map/rev | solution.py:391
  38.2 1.0 stack_reshape.14
  39.2 2.2 %stack_reshape.13 = bf16[1,192,384]{2,1,0:T(8,128)(2,1)} reshape(bf16[3,2,32,3,4,32]{5,4,3,2,1,0:T(4,128)(2,1)} %maximum_bitcast_fusion) | data formatting | bytes 294912 | tf_op jit(solution)/shard_map/stack;reshape | solution.py:393
  41.4 2.2 %stack_reshape.15 = bf16[1,192,384]{2,1,0:T(8,128)(2,1)} reshape(bf16[3,2,32,3,4,32]{5,4,3,2,1,0:T(4,128)(2,1)} %maximum_bitcast_fusion.2) | data formatting | bytes 294912 | tf_op jit(solution)/shard_map/stack;reshape | solution.py:394
  43.6 0.2 copy.37
  43.8 0.3 pad_bitcast_fusion.1
  44.2 0.5 maximum_bitcast_fusion.3
  44.6 1.0 stack_reshape.16
  45.6 1.9 %pack_mid.1.tile_ref = f32[22,32,128]{2,1,0:T(8,128)S(1)} custom-call(bf16[7,8,32,128]{3,2,1,0:T(8,128)(2,1)S(1)} %collective-permute-done.prev_ref.prev, bf16[8,8,32,128]{3,2,1,0:T(8,128)(2,1)S(1)} %pad_maximum_fusion.mine_ref.mine, bf16[7,8,32,128]{3,2,1,0:T(8,128)(2,1)S(1)} %collective-permute-done.1.next_ref.following), custom_call_target="tpu_custom_call" | custom-call | bytes 2097152 | tf_op jit(solution)/shard_map/pack_mid/pallas_call | solution.py:55
  47.6 0.0 collective-permute-done.2.a1
  47.6 0.0 collective-permute-done.3.b1
  47.6 0.0 collective-permute-done.4.a2
  47.6 0.0 collective-permute-done.5.b2
  47.6 2.7 %pack_edges.1 = (bf16[11,32,128]{2,1,0:T(8,128)(2,1)S(1)}, bf16[11,32,128]{2,1,0:T(8,128)(2,1)S(1)}) custom-call(bf16[8,4,32,128]{3,2,1,0:T(8,128)(2,1)S(1)} %collective-permute-done.2.a1, bf16[8,4,32,128]{3,2,1,0:T(8,128)(2,1)S(1)} %collective-permute-done.3.b1, bf16[14,4,32,128]{3,2,1,0:T(8,128)(2,1)S(1)} %collective-permute-done.4.a2, ...), custom_call_target="tpu_custom_call" | custom-call | bytes 2097152 | tf_op jit(solution)/shard_map/pack_edges/pallas_call | solution.py:94
  50.4 3.9 %collective-permute-start.6 = (bf16[11,32,128]{2,1,0:T(8,128)(2,1)S(1)}, bf16[11,32,128]{2,1,0:T(8,128)(2,1)S(1)}, u32[]{:S(2)}, u32[]{:S(2)}) collective-permute-start(bf16[11,32,128]{2,1,0:T(8,128)(2,1)S(1)} %get-tuple-element.18), channel_id=1, source_target_pairs={{0,1},{1,2},{2,3},{4,5},{5,6},{6,7},{8,9},{9,10},{10,11},{12,13},{... | collective-permute-start | bytes 270344 | tf_op jit(solution)/shard_map/ppermute | solution.py:15
  54.3 1.9 %collective-permute-start.7 = (bf16[11,32,128]{2,1,0:T(8,128)(2,1)S(1)}, bf16[11,32,128]{2,1,0:T(8,128)(2,1)S(1)}, u32[]{:S(2)}, u32[]{:S(2)}) collective-permute-start(bf16[11,32,128]{2,1,0:T(8,128)(2,1)S(1)} %get-tuple-element.19), channel_id=1, source_target_pairs={{1,0},{2,1},{3,2},{5,4},{6,5},{7,6},{9,8},{10,9},{11,10},{13,12},{... | collective-permute-start | bytes 270344 | tf_op jit(solution)/shard_map/ppermute | solution.py:16
  56.3 0.0 collective-permute-done.6.rl_ref
  56.3 3.8 %collective-permute-done.7.rr_ref = bf16[11,32,128]{2,1,0:T(8,128)(2,1)S(1)} collective-permute-done((bf16[11,32,128]{2,1,0:T(8,128)(2,1)S(1)}, bf16[11,32,128]{2,1,0:T(8,128)(2,1)S(1)}, u32[]{:S(2)}, u32[]{:S(2)}) %collective-permute-start.7) | collective-permute-done | bytes 90144 | tf_op jit(solution)/shard_map/ppermute | solution.py:16
  60.2 11.1 %first_convs.1 = (bf16[10,14,32,128]{3,2,1,0:T(8,128)(2,1)S(1)}, bf16[10,128,128]{2,1,0:T(8,128)(2,1)S(1)}, bf16[4,8,32,128]{3,2,1,0:T(8,128)(2,1)S(1)}, f32[4,6...) custom-call(bf16[7,8,32,128]{3,2,1,0:T(8,128)(2,1)S(1)} %collective-, ...), custom_call_target="tpu_custom_call" | custom-call | flops 8589934592 | bytes 8388608 | tf_op jit(solution)/shard_map/first_convs/pallas_call | solution.py:263
  71.3 1.0 copy-done
  72.3 0.7 copy-done.2
  73.0 0.7 copy-done.4
  73.7 0.7 copy-done.6
  74.4 0.6 broadcast_in_dim.6
  75.0 5.6 %all-to-all-start = ((f32[16,1,128]{2,1,0:T(1,128)}), f32[16,1,128]{2,1,0:T(1,128)S(1)}, u32[]{:S(2)}, u32[]{:S(2)}) async-start(f32[16,1,128]{2,1,0:T(1,128)} %broadcast_in_dim.6), calls=%async_computation | async-start | bytes 16384 | tf_op jit(solution)/shard_map/all_to_all | solution.py:405
  80.7 1.1 pad_maximum_fusion.4.w_ref
  81.8 0.1 stack.57.place
  81.9 4.3 %all-to-all-done = f32[16,1,128]{2,1,0:T(1,128)S(1)} async-done(((f32[16,1,128]{2,1,0:T(1,128)}), f32[16,1,128]{2,1,0:T(1,128)S(1)}, u32[]{:S(2)}, u32[]{:S(2)}) %all-to-all-start) | async-done | bytes 8224 | tf_op jit(solution)/shard_map/all_to_all | solution.py:405
  86.1 0.6 broadcast_in_dim.8
  86.8 19.1 %all-to-all-start.1 = ((f32[32,1,128]{2,1,0:T(1,128)}), f32[32,1,128]{2,1,0:T(1,128)S(1)}, u32[]{:S(2)}, u32[]{:S(2)}) async-start(f32[32,1,128]{2,1,0:T(1,128)} %broadcast_in_dim.8), calls=%async_computation.1 | async-start | bytes 32768 | tf_op jit(solution)/shard_map/all_to_all | solution.py:405
  105.9 1.2 %copy-done.1 = bf16[10,14,32,128]{3,2,1,0:T(8,128)(2,1)S(1)} copy-done((bf16[10,14,32,128]{3,2,1,0:T(8,128)(2,1)S(1)}, bf16[10,14,32,128]{3,2,1,0:T(8,128)(2,1)}, u32[]{:S(2)}) %copy-start.1) | copy-done | bytes 1146904
  107.2 1.0 copy-done.3
  108.1 0.9 copy-done.5
  109.1 0.9 copy-done.7
  110.0 9.7 %second_convs.1 = f32[4,8,32,128]{3,2,1,0:T(8,128)S(1)} custom-call(s32[6]{0:T(128)S(1)} %stack.57.place, bf16[10,14,32,128]{3,2,1,0:T(8,128)(2,1)S(1)} %copy-done.1, bf16[10,128,128]{2,1,0:T(8,128)(2,1)S(1)} %copy-done.3, bf16[4,8,32,128]{3,2,1,0:T(8,128)(2,1)S(1)} %copy-done.5, f32[4,64,128]{2,1,0:T(8,128)S(1)} %get-tuple-element.30.own_h, ...), custom_call_target="tpu_custom_call" | custom-call | flops 8589934592 | bytes 4194304 | tf_op jit(solution)/shard_map/second_convs/pallas_call | solution.py:352
  119.7 0.0 all-to-all-done.1
  119.7 0.6 reduce_sum.33
  121.0 0.1 divide_bitcast_fusion
  121.1 1.1 copy.40
  (29 shorter events, 0.2 us)
Async XLA Ops:
  0.6 1.1 copy-start.13
  2.8 13.2 %copy-start.9 = (bf16[27,32,32]{2,1,0:T(8,128)(2,1)S(1)}, bf16[27,32,32]{2,1,0:T(8,128)(2,1)}, u32[]{:S(2)}) copy-start(bf16[27,32,32]{2,1,0:T(8,128)(2,1)} %param.7) | copy-start | bytes 165892
  2.8 23.1 %collective-permute-start = (bf16[7,8,32,128]{3,2,1,0:T(8,128)(2,1)}, bf16[7,8,32,128]{3,2,1,0:T(8,128)(2,1)S(1)}, u32[]{:S(2)}, u32[]{:S(2)}) collective-permute-start(bf16[7,8,32,128]{3,2,1,0:T(8,128)(2,1)} %slice.40), channel_id=1, source_target_pairs={{0,16},{16,32},{32,48},{48,64},{64,80},{80,96},{96,112},{112,128},... | collective-permute-start | bytes 1376264 | tf_op jit(solution)/shard_map/ppermute | solution.py:15
  9.2 7.0 %copy-start.10 = (bf16[27,32,32]{2,1,0:T(8,128)(2,1)S(1)}, bf16[27,32,32]{2,1,0:T(8,128)(2,1)}, u32[]{:S(2)}) copy-start(bf16[27,32,32]{2,1,0:T(8,128)(2,1)} %param.6) | copy-start | bytes 165892
  9.2 16.7 %collective-permute-start.1 = (bf16[7,8,32,128]{3,2,1,0:T(8,128)(2,1)}, bf16[7,8,32,128]{3,2,1,0:T(8,128)(2,1)S(1)}, u32[]{:S(2)}, u32[]{:S(2)}) collective-permute-start(bf16[7,8,32,128]{3,2,1,0:T(8,128)(2,1)} %pad_maximum_fusion.1), channel_id=1, source_target_pairs={{16,0},{32,16},{48,32},{64,48},{80,64},{96,80},{112,96},{128,112},... | collective-permute-start | bytes 1376264 | tf_op jit(solution)/shard_map/ppermute | solution.py:16
  11.5 36.1 %collective-permute-start.2 = (bf16[8,4,32,128]{3,2,1,0:T(8,128)(2,1)}, bf16[8,4,32,128]{3,2,1,0:T(8,128)(2,1)S(1)}, u32[]{:S(2)}, u32[]{:S(2)}) collective-permute-start(bf16[8,4,32,128]{3,2,1,0:T(8,128)(2,1)} %get-tuple-element.41), channel_id=1, source_target_pairs={{0,4},{4,8},{8,12},{1,5},{5,9},{9,13},{2,6},{6,10},{10,14},{3,7},{... | collective-permute-start | bytes 786440 | tf_op jit(solution)/shard_map/ppermute | solution.py:15
  14.7 32.9 %collective-permute-start.3 = (bf16[8,4,32,128]{3,2,1,0:T(8,128)(2,1)}, bf16[8,4,32,128]{3,2,1,0:T(8,128)(2,1)S(1)}, u32[]{:S(2)}, u32[]{:S(2)}) collective-permute-start(bf16[8,4,32,128]{3,2,1,0:T(8,128)(2,1)} %get-tuple-element.40), channel_id=1, source_target_pairs={{4,0},{8,4},{12,8},{5,1},{9,5},{13,9},{6,2},{10,6},{14,10},{7,3},{... | collective-permute-start | bytes 786440 | tf_op jit(solution)/shard_map/ppermute | solution.py:16
  26.8 20.8 %collective-permute-start.4 = (bf16[14,4,32,128]{3,2,1,0:T(8,128)(2,1)}, bf16[14,4,32,128]{3,2,1,0:T(8,128)(2,1)S(1)}, u32[]{:S(2)}, u32[]{:S(2)}) collective-permute-start(bf16[14,4,32,128]{3,2,1,0:T(8,128)(2,1)} %pad_maximum_fusion.2), channel_id=1, source_target_pairs={{0,4},{4,8},{8,12},{1,5},{5,9},{9,13},{2,6},{6,10},{10,14},{3,7},{... | collective-permute-start | bytes 1376264 | tf_op jit(solution)/shard_map/ppermute | solution.py:15
  32.7 15.0 %collective-permute-start.5 = (bf16[14,4,32,128]{3,2,1,0:T(8,128)(2,1)}, bf16[14,4,32,128]{3,2,1,0:T(8,128)(2,1)S(1)}, u32[]{:S(2)}, u32[]{:S(2)}) collective-permute-start(bf16[14,4,32,128]{3,2,1,0:T(8,128)(2,1)} %pad_maximum_fusion.3), channel_id=1, source_target_pairs={{4,0},{8,4},{12,8},{5,1},{9,5},{13,9},{6,2},{10,6},{14,10},{7,3},{... | collective-permute-start | bytes 1376264 | tf_op jit(solution)/shard_map/ppermute | solution.py:16
  39.2 4.4 %copy-start.11 = (bf16[27,32,32]{2,1,0:T(8,128)(2,1)S(1)}, bf16[27,32,32]{2,1,0:T(8,128)(2,1)}, u32[]{:S(2)}) copy-start(bf16[27,32,32]{2,1,0:T(8,128)(2,1)} %rev.7) | copy-start | bytes 165892
  47.6 8.7 %copy-start.8 = (bf16[1,192,384]{2,1,0:T(8,128)(2,1)S(1)}, bf16[1,192,384]{2,1,0:T(8,128)(2,1)}, u32[]{:S(2)}) copy-start(bf16[1,192,384]{2,1,0:T(8,128)(2,1)} %stack_reshape.14) | copy-start | bytes 442372
  47.6 8.7 %copy-start.12 = (bf16[1,192,384]{2,1,0:T(8,128)(2,1)S(1)}, bf16[1,192,384]{2,1,0:T(8,128)(2,1)}, u32[]{:S(2)}) copy-start(bf16[1,192,384]{2,1,0:T(8,128)(2,1)} %stack_reshape.13) | copy-start | bytes 442372
  50.4 5.9 %collective-permute-start.6 = (bf16[11,32,128]{2,1,0:T(8,128)(2,1)S(1)}, bf16[11,32,128]{2,1,0:T(8,128)(2,1)S(1)}, u32[]{:S(2)}, u32[]{:S(2)}) collective-permute-start(bf16[11,32,128]{2,1,0:T(8,128)(2,1)S(1)} %get-tuple-element.18), channel_id=1, source_target_pairs={{0,1},{1,2},{2,3},{4,5},{5,6},{6,7},{8,9},{9,10},{10,11},{12,13},{... | collective-permute-start | bytes 270344 | tf_op jit(solution)/shard_map/ppermute | solution.py:15
  54.3 5.8 %collective-permute-start.7 = (bf16[11,32,128]{2,1,0:T(8,128)(2,1)S(1)}, bf16[11,32,128]{2,1,0:T(8,128)(2,1)S(1)}, u32[]{:S(2)}, u32[]{:S(2)}) collective-permute-start(bf16[11,32,128]{2,1,0:T(8,128)(2,1)S(1)} %get-tuple-element.19), channel_id=1, source_target_pairs={{1,0},{2,1},{3,2},{5,4},{6,5},{7,6},{9,8},{10,9},{11,10},{13,12},{... | collective-permute-start | bytes 270344 | tf_op jit(solution)/shard_map/ppermute | solution.py:16
  71.3 1.0 copy-start
  72.3 0.7 copy-start.2
  73.0 0.7 copy-start.4
  73.7 0.7 copy-start.6
  75.0 11.1 %all-to-all-start = ((f32[16,1,128]{2,1,0:T(1,128)}), f32[16,1,128]{2,1,0:T(1,128)S(1)}, u32[]{:S(2)}, u32[]{:S(2)}) async-start(f32[16,1,128]{2,1,0:T(1,128)} %broadcast_in_dim.6), calls=%async_computation | async-start | bytes 16384 | tf_op jit(solution)/shard_map/all_to_all | solution.py:405
  86.8 32.9 %all-to-all-start.1 = ((f32[32,1,128]{2,1,0:T(1,128)}), f32[32,1,128]{2,1,0:T(1,128)S(1)}, u32[]{:S(2)}, u32[]{:S(2)}) async-start(f32[32,1,128]{2,1,0:T(1,128)} %broadcast_in_dim.8), calls=%async_computation.1 | async-start | bytes 32768 | tf_op jit(solution)/shard_map/all_to_all | solution.py:405
  105.9 1.3 %copy-start.1 = (bf16[10,14,32,128]{3,2,1,0:T(8,128)(2,1)S(1)}, bf16[10,14,32,128]{3,2,1,0:T(8,128)(2,1)}, u32[]{:S(2)}) copy-start(bf16[10,14,32,128]{3,2,1,0:T(8,128)(2,1)} %copy-done) | copy-start | bytes 3440644
  107.2 1.0 copy-start.3
  108.1 0.9 copy-start.5
  109.1 0.9 copy-start.7

commit v3 on v2

--- a/solution.py
+++ b/solution.py
@@ -33,52 +33,74 @@
     return tile
 
 
-def pack_mid_kernel(prev_ref, mine_ref, next_ref, tile_ref):
+def rows_kernel(prev_ref, next_ref, low_ref, top_ref):
+    low_ref[0:7] = prev_ref[:, 4:8]
+    low_ref[7:14] = next_ref[:, 4:8]
+    top_ref[0:7] = prev_ref[:, 0:4]
+    top_ref[7:14] = next_ref[:, 0:4]
+
+
+def edge_rows(prev, following):
+    out = jax.ShapeDtypeStruct((14, 4, CH, LANES), jnp.bfloat16)
+    return pl.pallas_call(
+        rows_kernel,
+        out_shape=(out, out),
+        compiler_params=pltpu.CompilerParams(vmem_limit_bytes=16 << 20),
+        cost_estimate=pl.CostEstimate(flops=0, bytes_accessed=1 << 21, transcendentals=0),
+        name="edge_rows",
+    )(prev, following)
+
+
+OUTER = list(range(4)) + list(range(12, 16))
+
+
+def pack_mid_kernel(prev_ref, mine_ref, next_ref, a1, b1, tile_ref):
     lane = lax.broadcasted_iota(jnp.int32, (CH, LANES), 1)
+    none = jnp.zeros((CH, LANES), jnp.float32)
 
     def layers(ref, base):
         def body(i, carry):
-            tile = gather_edges(
-                jnp.zeros((CH, LANES), jnp.float32), range(4, 12), lambda r: ref[i, r - 4], lane
-            )
-            tile_ref[base + i] = tile
+            tile_ref[base + i] = gather_edges(none, range(4, 12), lambda r: ref[i, r - 4], lane)
             return carry
 
         lax.fori_loop(0, ref.shape[0], body, 0)
 
+    def own(i, carry):
+        def load(r):
+            if 4 <= r < 12:
+                return mine_ref[i, r - 4]
+            return a1[i, r] if r < 4 else b1[i, r - 12]
+
+        tile_ref[7 + i] = gather_edges(none, range(16), load, lane)
+        return carry
+
     layers(prev_ref, 0)
-    layers(mine_ref, 7)
+    lax.fori_loop(0, 8, own, 0)
     layers(next_ref, 15)
 
 
-def pack_mid(prev, mine, following):
+def pack_mid(prev, mine, following, a1, b1):
     return pl.pallas_call(
         pack_mid_kernel,
         out_shape=jax.ShapeDtypeStruct((22, CH, LANES), jnp.float32),
         compiler_params=pltpu.CompilerParams(vmem_limit_bytes=16 << 20),
         cost_estimate=pl.CostEstimate(flops=0, bytes_accessed=1 << 21, transcendentals=0),
         name="pack_mid",
-    )(prev, mine, following)
-
-
-def pack_kernel(a1, b1, a2, b2, tile_ref, left_ref, right_ref, full):
+    )(prev, mine, following, a1, b1)
+
+
+def pack_kernel(a2, b2, tile_ref, left_ref, right_ref, full):
     lane = lax.broadcasted_iota(jnp.int32, (CH, LANES), 1)
     low = (lane & 7) < 4
-
-    def layers(above, below, base, count, skip):
-        def body(i, carry):
-            def load(r):
-                return above[i + skip, r] if r < 4 else below[i + skip, r - 12]
-
-            rows = list(range(4)) + list(range(12, 16))
-            full[base + i] = gather_edges(tile_ref[base + i], rows, load, lane)
-            return carry
-
-        lax.fori_loop(0, count, body, 0)
-
-    layers(a2, b2, 0, 7, 0)
-    layers(a1, b1, 7, 8, 0)
-    layers(a2, b2, 15, 7, 7)
+    full[7:15] = tile_ref[7:15]
+
+    def received(i, carry):
+        at = jnp.where(i < 7, i, i + 8)
+        load = lambda r: a2[i, r] if r < 4 else b2[i, r - 12]
+        full[at] = gather_edges(tile_ref[at], OUTER, load, lane)
+        return carry
+
+    lax.fori_loop(0, 14, received, 0)
 
     def group(g, carry):
         one, two = full[2 * g], full[2 * g + 1]
@@ -89,7 +111,7 @@
     lax.fori_loop(0, left_ref.shape[0], group, 0)
 
 
-def pack_edges(a1, b1, a2, b2, tiles):
+def pack_edges(a2, b2, tiles):
     out = jax.ShapeDtypeStruct((11, CH, LANES), jnp.bfloat16)
     return pl.pallas_call(
         pack_kernel,
@@ -98,7 +120,7 @@
         compiler_params=pltpu.CompilerParams(vmem_limit_bytes=16 << 20),
         cost_estimate=pl.CostEstimate(flops=0, bytes_accessed=1 << 21, transcendentals=0),
         name="pack_edges",
-    )(a1, b1, a2, b2, tiles)
+    )(a2, b2, tiles)
 
 
 def convolve_layer(w, get, get_halo, m, pairs, put, put_halo):
@@ -160,8 +182,8 @@
 
 def first_kernel_body(
     prev, mine, following, a1, b1, a2, b2, rl_ref, rr_ref, w_ref,
-    hid, hid_h, own_ref, own_h, slope_ref, slope_h, sum_ref,
-    f_ref, edge, t_h, sems,
+    hid_out, hid_h_out, own_out, own_h_out, slope_out, slope_h_out, sum_ref,
+    f_ref, edge, t_h, hid, hid_h, own_ref, own_h, slope_h, sum_acc, sems, out_sems,
 ):
     moves = [
         (prev, f_ref.at[0:7, 4:12]),
@@ -203,40 +225,44 @@
         return carry
 
     lax.fori_loop(0, 12, t_halo, 0)
+
+    def slope_halo(m, row):
+        tile = edge[s_layer(m)]
+        q = row // 2
+        return jnp.concatenate([roll(tile, 64 - 8 * q), roll(tile, -8 * (q + 1))], axis=0)
+
+    def keep_slopes(m, carry):
+        slope_h[m] = slope_halo(m + 2, 3)
+        return carry
+
+    def field_rows(t, r):
+        return f_ref[t_layer(t), pl.ds(r, 4)].reshape(4 * CH, LANES)
+
+    lax.fori_loop(0, 6, keep_slopes, 0)
     for copy in copies:
         copy.wait()
 
-    def slope_halo(i, row):
-        tile = edge[i]
-        q = row // 2
-        return jnp.concatenate([roll(tile, 64 - 8 * q), roll(tile, -8 * (q + 1))], axis=0)
-
-    def keep_slopes(m, carry):
-        i = s_layer(m + 2)
-        slope_ref[m] = f_ref[i, 3:13]
-        slope_h[m] = slope_halo(i, 3)
-        return carry
-
-    lax.fori_loop(0, 6, keep_slopes, 0)
-
-    def field_rows(t, r):
-        return f_ref[t_layer(t), pl.ds(r, 4)].reshape(4 * CH, LANES)
-
     def stage_hidden(m, carry):
-        i = s_layer(m)
-
         def put(p, v):
-            slope = f_ref[i, pl.ds(2 * p + 1, 2)].reshape(2 * CH, LANES)
+            slope = f_ref[s_layer(m), pl.ds(2 * p + 1, 2)].reshape(2 * CH, LANES)
             store(hid, m, p, slope.astype(jnp.float32) * v)
 
         def put_halo(v):
-            store_halo(hid_h, m, slope_halo(i, 1) * v)
+            store_halo(hid_h, m, slope_halo(m, 1) * v)
 
         convolve_layer(w_ref[0], field_rows, lambda t: t_h[t], m, range(7), put, put_halo)
         return carry
 
     lax.fori_loop(0, 10, stage_hidden, 0)
-    sum_ref[...] = jnp.zeros_like(sum_ref)
+    early = [
+        (hid, hid_out), (hid_h, hid_h_out), (slope_h, slope_h_out),
+        (f_ref.at[6:10, 3:13], slope_out.at[0:4]), (f_ref.at[14:16, 3:13], slope_out.at[4:6]),
+    ]
+    late = [(own_ref, own_out), (own_h, own_h_out)]
+    writes = [pltpu.make_async_copy(x, y, out_sems.at[i]) for i, (x, y) in enumerate(early + late)]
+    for copy in writes[:5]:
+        copy.start()
+    sum_acc[...] = jnp.zeros_like(sum_acc)
 
     def stage_own(m, carry):
         def put(p, v):
@@ -245,7 +271,7 @@
             part = square[0:8]
             for q in range(1, 8):
                 part = part + square[8 * q : 8 * q + 8]
-            sum_ref[...] += part
+            sum_acc[...] += part
 
         def put_halo(v):
             own_h[m] = v
@@ -256,38 +282,61 @@
         return carry
 
     lax.fori_loop(0, 4, stage_own, 0)
-
-
-def first_convs(pieces, rl, rr, weights):
+    for copy in writes[5:]:
+        copy.start()
+    total = jnp.sum(sum_acc[...], axis=0, keepdims=True)
+    for i in range(sum_ref.shape[0]):
+        sum_ref[i] = total
+    for copy in writes:
+        copy.wait()
+
+
+def first_convs(pieces, rl, rr, weights, spread):
     shape = jax.ShapeDtypeStruct
+    anywhere = pl.BlockSpec(memory_space=pl.ANY)
+    local = pl.BlockSpec(memory_space=pltpu.VMEM)
+    fields = (
+        shape((10, 14, CH, LANES), jnp.bfloat16),
+        shape((10, 4 * CH, LANES), jnp.bfloat16),
+        shape((4, 8, CH, LANES), jnp.bfloat16),
+        shape((4, 2 * CH, LANES), jnp.float32),
+        shape((6, 10, CH, LANES), jnp.bfloat16),
+        shape((6, 2 * CH, LANES), jnp.float32),
+    )
+    keep = [pltpu.VMEM(fields[i].shape, fields[i].dtype) for i in (0, 1, 2, 3, 5)]
     return pl.pallas_call(
         first_kernel_body,
-        out_shape=(
-            shape((10, 14, CH, LANES), jnp.bfloat16),
-            shape((10, 4 * CH, LANES), jnp.bfloat16),
-            shape((4, 8, CH, LANES), jnp.bfloat16),
-            shape((4, 2 * CH, LANES), jnp.float32),
-            shape((6, 10, CH, LANES), jnp.bfloat16),
-            shape((6, 2 * CH, LANES), jnp.float32),
-            shape((8, LANES), jnp.float32),
-        ),
-        in_specs=[pl.BlockSpec(memory_space=pl.ANY)] * 7
-        + [pl.BlockSpec(memory_space=pltpu.VMEM)] * 3,
+        out_shape=(*fields, shape((spread, 1, LANES), jnp.float32)),
+        in_specs=[anywhere] * 7 + [local] * 3,
+        out_specs=(*([anywhere] * 6), local),
         scratch_shapes=[
             pltpu.VMEM((22, 16, CH, LANES), jnp.bfloat16),
             pltpu.VMEM((22, CH, LANES), jnp.float32),
             pltpu.VMEM((12, 4 * CH, LANES), jnp.bfloat16),
+            *keep,
+            pltpu.VMEM((8, LANES), jnp.float32),
             pltpu.SemaphoreType.DMA((9,)),
+            pltpu.SemaphoreType.DMA((7,)),
         ],
-        compiler_params=pltpu.CompilerParams(vmem_limit_bytes=16 << 20),
+        compiler_params=pltpu.CompilerParams(vmem_limit_bytes=62 << 20),
         cost_estimate=pl.CostEstimate(flops=8 << 30, bytes_accessed=8 << 20, transcendentals=0),
         name="first_convs",
     )(*pieces, rl, rr, weights)
 
 
 def second_kernel_body(
-    place, hid, hid_h, own_ref, own_h, slope_ref, slope_h, w_ref, out_ref, img, img_h, pul, pul_h
+    place, hid_in, hid_h_in, own_in, own_h_in, slope_in, slope_h_in, w_ref, after, out_ref,
+    hid, hid_h, own_h, slope_ref, slope_h, img, img_h, pul, pul_h, sems,
 ):
+    moves = [
+        (hid_in, hid), (hid_h_in, hid_h), (own_in, img.at[2:6, 2:10]), (own_h_in, own_h),
+        (slope_in, slope_ref), (slope_h_in, slope_h),
+    ]
+    copies = [pltpu.make_async_copy(x, y, sems.at[i]) for i, (x, y) in enumerate(moves)]
+    for copy in copies:
+        copy.start()
+    for copy in copies[:2]:
+        copy.wait()
     wide = lax.broadcasted_iota(jnp.int32, (2 * CH, LANES), 1)
     wide8 = wide & 7
     gx, gy, gz = place[0], place[1], place[2]
@@ -306,7 +355,7 @@
         def put_halo(v):
             store_halo(img_h, m, merge(v) * (halo_in * x_in))
 
-        convolve_layer(w_ref[0], rows_of(hid), lambda t: hid_h[t], m, pairs, put, put_halo)
+        convolve_layer(w_ref[1], rows_of(hid), lambda t: hid_h[t], m, pairs, put, put_halo)
 
     def stage_ends(i, carry):
         m = jnp.where(i < 2, i, i + 4)
@@ -316,9 +365,11 @@
 
     lax.fori_loop(0, 4, stage_ends, 0)
 
+    for copy in copies[2:]:
+        copy.wait()
+
     def stage_rim(i, carry):
         m = i + 2
-        img[m, 2:10] = own_ref[i]
         outer = (wide < 8) | (wide >= 40)
         image_layer(m, 1.0, (0, 5), lambda v: jnp.where(outer, v, own_h[i]))
         return carry
@@ -333,7 +384,7 @@
         def put_halo(v):
             store_halo(pul_h, m, slope_h[m] * v)
 
-        convolve_layer(w_ref[1], rows_of(img), lambda t: img_h[t], m, range(5), put, put_halo)
+        convolve_layer(w_ref[2], rows_of(img), lambda t: img_h[t], m, range(5), put, put_halo)
         return carry
 
     lax.fori_loop(0, 6, stage_pulled, 0)
@@ -342,37 +393,58 @@
         def put(p, v):
             out_ref[m, pl.ds(2 * p, 2)] = v.reshape(2, CH, LANES)
 
-        convolve_layer(w_ref[2], rows_of(pul), lambda t: pul_h[t], m, range(4), put, None)
+        convolve_layer(w_ref[3], rows_of(pul), lambda t: pul_h[t], m, range(4), put, None)
         return carry
 
     lax.fori_loop(0, 4, stage_out, 0)
 
 
-def second_convs(place, fields, weights):
+def second_convs(place, fields, weights, after):
     return pl.pallas_call(
         second_kernel_body,
         out_shape=jax.ShapeDtypeStruct((4, 8, CH, LANES), jnp.float32),
         in_specs=[pl.BlockSpec(memory_space=pltpu.SMEM)]
-        + [pl.BlockSpec(memory_space=pltpu.VMEM)] * 7,
+        + [pl.BlockSpec(memory_space=pl.ANY)] * 6
+        + [pl.BlockSpec(memory_space=pltpu.VMEM)] * 2,
         scratch_shapes=[
+            *[pltpu.VMEM(f.shape, f.dtype) for i, f in enumerate(fields) if i != 2],
             pltpu.VMEM((8, 12, CH, LANES), jnp.bfloat16),
             pltpu.VMEM((8, 4 * CH, LANES), jnp.bfloat16),
             pltpu.VMEM((6, 10, CH, LANES), jnp.bfloat16),
             pltpu.VMEM((6, 4 * CH, LANES), jnp.bfloat16),
+            pltpu.SemaphoreType.DMA((6,)),
         ],
-        compiler_params=pltpu.CompilerParams(vmem_limit_bytes=16 << 20),
+        compiler_params=pltpu.CompilerParams(vmem_limit_bytes=62 << 20),
         cost_estimate=pl.CostEstimate(flops=8 << 30, bytes_accessed=4 << 20, transcendentals=0),
         name="second_convs",
-    )(place, *fields, weights)
-
-
-def pair_matrix(kernel):
-    taps = kernel.reshape(3, 3, 3, CH, CH)
-    none = ((0, 0), (0, 0), (0, 0), (0, 0))
-    top = jnp.pad(taps, (none[0], (0, 1)) + none[:3])
-    low = jnp.pad(taps, (none[0], (1, 0)) + none[:3])
-    both = jnp.stack([top, low])
-    return both.transpose(3, 0, 4, 1, 2, 5).reshape(6 * CH, 12 * CH)
+    )(place, *fields, weights, after)
+
+
+def weights_kernel(k1_ref, k2_ref, w_ref):
+    w_ref[...] = jnp.zeros_like(w_ref)
+    for which, (ref, adjoint) in enumerate(
+        ((k1_ref, False), (k2_ref, False), (k2_ref, True), (k1_ref, True))
+    ):
+        for tap in range(27):
+            a, b, c = tap // 9, tap // 3 % 3, tap % 3
+            if adjoint:
+                block = ref[26 - tap].astype(jnp.float32).T.astype(jnp.bfloat16)
+            else:
+                block = ref[tap]
+            for row in range(2):
+                top = (2 * c + row) * CH
+                left = (4 * a + b + row) * CH
+                w_ref[which, top : top + CH, left : left + CH] = block
+
+
+def pair_matrices(first_kernel, second_kernel):
+    return pl.pallas_call(
+        weights_kernel,
+        out_shape=jax.ShapeDtypeStruct((4, 6 * CH, 12 * CH), jnp.bfloat16),
+        compiler_params=pltpu.CompilerParams(vmem_limit_bytes=8 << 20),
+        cost_estimate=pl.CostEstimate(flops=0, bytes_accessed=4 << 20, transcendentals=0),
+        name="pair_matrices",
+    )(first_kernel, second_kernel)
 
 
 def on_device(tangent, slopes, first_kernel, second_kernel):
@@ -381,33 +453,26 @@
     mine = jnp.concatenate([s[0:3], t, s[3:4]], axis=0)
     prev, following = shift_pair(mine[1:8], mine[0:7], "gx")
     a1, b1 = shift_pair(mine[:, 4:8], mine[:, 0:4], "gy")
-    to_below = jnp.concatenate([prev[:, 4:8], following[:, 4:8]], axis=0)
-    to_above = jnp.concatenate([prev[:, 0:4], following[:, 0:4]], axis=0)
-    a2, b2 = shift_pair(to_below, to_above, "gy")
-    tiles = pack_mid(prev, mine, following)
-    left_edge, right_edge = pack_edges(a1, b1, a2, b2, tiles)
+    prev, following, a1, b1 = lax.optimization_barrier((prev, following, a1, b1))
+    low, top = edge_rows(prev, following)
+    a2, b2 = shift_pair(low, top, "gy")
+    weights = pair_matrices(first_kernel, second_kernel)
+    left_edge, right_edge = pack_edges(a2, b2, pack_mid(prev, mine, following, a1, b1))
     rl, rr = shift_pair(right_edge, left_edge, "gz")
-
-    adjoint = lambda k: k[::-1].transpose(0, 2, 1)
-    second = pair_matrix(second_kernel)
-    forward = jnp.stack([pair_matrix(first_kernel), second])
-    backward = jnp.stack(
-        [second, pair_matrix(adjoint(second_kernel)), pair_matrix(adjoint(first_kernel))]
-    )
+    plane = lax.axis_size(("gy", "gz"))
+    pieces = (prev, mine, following, a1, b1, a2, b2)
+    *fields, spread = first_convs(pieces, rl, rr, weights, plane)
+
+    def collect(v, axes):
+        return jnp.sum(lax.all_to_all(v, axes, 0, 0, tiled=True), axis=0, keepdims=True)
+
     place = jnp.stack(
         [lax.axis_index(a) for a in ALL] + [jnp.int32(lax.axis_size(a) - 1) for a in ALL]
     ).astype(jnp.int32)
-    *fields, squares = first_convs((prev, mine, following, a1, b1, a2, b2), rl, rr, forward)
-
-    def exchange(part, axes):
-        count = lax.axis_size(axes)
-        spread = jnp.broadcast_to(part, (count, LANES))
-        return jnp.sum(lax.all_to_all(spread, axes, 0, 0, tiled=True), axis=0, keepdims=True)
-
-    part = exchange(jnp.sum(squares, axis=0, keepdims=True), ("gy", "gz"))
-    part, *fields = lax.optimization_barrier((part, *fields))
-    result = second_convs(place, fields, backward)
-    part = exchange(part, "gx")
+    part = collect(spread, ("gy", "gz"))
+    result = second_convs(place, fields, weights, part)
+    count = lax.axis_size("gx")
+    part = collect(jnp.broadcast_to(part, (count, 1, LANES)), "gx")
     jvp_norm = jnp.sqrt(jnp.sum(part) + 1e-06)
     next_vector = result.transpose(2, 0, 1, 3) / jvp_norm
     return (next_vector, jvp_norm.reshape(1))

time: 124 us -> 118 us (0.952)
  local copies, waits for them, and re-layouts: 22.7 us -> 5.11 us
  waiting for transfers between devices: 15.9 us -> 27.9 us
  other arithmetic: 7.99 us -> 1.85 us
  Pallas kernels: 25.4 us -> 30.8 us
    another operation x9 -> x1, local copies, waits for them, and re-layouts: 7.77 us -> 0.01 us  [the longest x2 3.22 us: on_device(): forward = jnp.stack([pair_matrix(first_kernel), second])]
    ppermute x4, waiting for transfers between devices: 3.85 us -> 9.74 us  [shift_pair(): from_next = lax.ppermute(down, axis, [(i + 1, i) for i in range(ends)])]
    unnamed x31, local copies, waits for them, and re-layouts: 9.55 us -> 3.8 us
    ppermute x4, waiting for transfers between devices: 7.78 us -> 12.2 us  [shift_pair(): from_prev = lax.ppermute(up, axis, [(i, i + 1) for i in range(ends)])]
    transpose x4 -> x0, other arithmetic: 3.59 us -> none  [pair_matrix(): return both.transpose(3, 0, 4, 1, 2, 5).reshape(6 * CH, 12 * CH)]
    pallas_call x1 -> x3, Pallas kernels: 11.1 us -> 14.3 us  [the longest x1 13.3 us: first_convs(): pl.pallas_call(first_kernel_body, out_shape=(*fields, shape((spread, 1, L...]
    pallas_call x1, Pallas kernels: 9.69 us -> 12.4 us  [second_convs(): pl.pallas_call(second_kernel_body, out_shape=jax.ShapeDtypeStruct((4, 8,...]
    all_to_all x2, waiting for transfers between devices: 4.26 us -> 5.99 us  [collect(): lax.all_to_all(v, axes, 0, 0, tiled=True)]
  transfers between devices with their start and end apart: 10 -> 10, of which waited for: 3 -> 8; matrix products, arithmetic and copies ran while one was open for 15% -> 1% of each run, Pallas kernels for 9% -> 13%
where the time goes in v3:
time: 118 us; the launch traced here: 117 us
  starting transfers between devices  49 us (42%)
  Pallas kernels  30.8 us (26%)
  waiting for transfers between devices  27.9 us (24%)
  local copies, waits for them, and re-layouts  5.11 us (4%)
  between operations  2.76 us (2%)
  other arithmetic  1.85 us (2%)
    all_to_all x2, starting transfers between devices, collect(): lax.all_to_all(v, axes, 0, 0, tiled=True)  24.6 us
    ppermute x4, starting transfers between devices, shift_pair(): from_prev = lax.ppermute(up, axis, [(i, i + 1) for i in range(ends)])  18.6 us
    pallas_call x1, Pallas kernels, first_convs(): pl.pallas_call(first_kernel_body, out_shape=(*fields, shape((spread, 1, L...  13.3 us
    pallas_call x1, Pallas kernels, second_convs(): pl.pallas_call(second_kernel_body, out_shape=jax.ShapeDtypeStruct((4, 8,...  12.4 us
    ppermute x4, waiting for transfers between devices, shift_pair(): from_prev = lax.ppermute(up, axis, [(i, i + 1) for i in range(ends)])  12.2 us
    ppermute x4, waiting for transfers between devices, shift_pair(): from_next = lax.ppermute(down, axis, [(i + 1, i) for i in range(ends)])  9.74 us
    all_to_all x2, waiting for transfers between devices, collect(): lax.all_to_all(v, axes, 0, 0, tiled=True)  5.99 us
    ppermute x4, starting transfers between devices, shift_pair(): from_next = lax.ppermute(down, axis, [(i + 1, i) for i in range(ends)])  5.8 us
  transfers between devices with their start and end apart: 10, of which 8 were waited for; matrix products, arithmetic and copies ran while one was open for 1% of the time, Pallas kernels for 13%

profile of v3, /device:TPU:1, one launch (start us, length us, event | category | flops | bytes accessed | tf_op | source)
XLA Modules:
  0.0 117.4 jit_solution(15330736481212101396)
XLA Ops:
  0.6 0.0 copy-start.10
  0.6 1.1 copy.19
  1.8 0.0 copy-done.10
  1.8 0.1 copy.18
  1.9 0.1 pad_maximum_fusion.mine_ref.mine
  2.0 0.0 copy-start
  2.0 5.5 %collective-permute-start = (bf16[7,8,32,128]{3,2,1,0:T(8,128)(2,1)S(1)}, bf16[7,8,32,128]{3,2,1,0:T(8,128)(2,1)S(1)}, u32[]{:S(2)}, u32[]{:S(2)}) collective-permute-start(bf16[7,8,32,128]{3,2,1,0:T(8,128)(2,1)S(1)} %slice.24), channel_id=1, source_target_pairs={{0,16},{16,32},{32,48},{48,64},{64,80},{80,96},{96,112},{112,128},... | collective-permute-start | bytes 1376264 | tf_op jit(solution)/shard_map/ppermute | solution.py:15
  7.6 1.3 %collective-permute-start.1 = (bf16[7,8,32,128]{3,2,1,0:T(8,128)(2,1)S(1)}, bf16[7,8,32,128]{3,2,1,0:T(8,128)(2,1)S(1)}, u32[]{:S(2)}, u32[]{:S(2)}) collective-permute-start(bf16[7,8,32,128]{3,2,1,0:T(8,128)(2,1)S(1)} %pad_maximum_fusion.1), channel_id=1, source_target_pairs={{16,0},{32,16},{48,32},{64,48},{80,64},{96,80},{112,96},{128,112},... | collective-permute-start | bytes 1376264 | tf_op jit(solution)/shard_map/ppermute | solution.py:16
  8.9 3.2 %collective-permute-start.2 = (bf16[8,4,32,128]{3,2,1,0:T(8,128)(2,1)S(1)}, bf16[8,4,32,128]{3,2,1,0:T(8,128)(2,1)S(1)}, u32[]{:S(2)}, u32[]{:S(2)}) collective-permute-start(bf16[8,4,32,128]{3,2,1,0:T(8,128)(2,1)S(1)} %get-tuple-element.39), channel_id=1, source_target_pairs={{0,4},{4,8},{8,12},{1,5},{5,9},{9,13},{2,6},{6,10},{10,14},{3,7},{... | collective-permute-start | bytes 786440 | tf_op jit(solution)/shard_map/ppermute | solution.py:15
  12.2 1.3 %collective-permute-start.3 = (bf16[8,4,32,128]{3,2,1,0:T(8,128)(2,1)S(1)}, bf16[8,4,32,128]{3,2,1,0:T(8,128)(2,1)S(1)}, u32[]{:S(2)}, u32[]{:S(2)}) collective-permute-start(bf16[8,4,32,128]{3,2,1,0:T(8,128)(2,1)S(1)} %get-tuple-element.38), channel_id=1, source_target_pairs={{4,0},{8,4},{12,8},{5,1},{9,5},{13,9},{6,2},{10,6},{14,10},{7,3},{... | collective-permute-start | bytes 786440 | tf_op jit(solution)/shard_map/ppermute | solution.py:16
  13.5 3.3 %collective-permute-done.2.a1 = bf16[8,4,32,128]{3,2,1,0:T(8,128)(2,1)S(1)} collective-permute-done((bf16[8,4,32,128]{3,2,1,0:T(8,128)(2,1)S(1)}, bf16[8,4,32,128]{3,2,1,0:T(8,128)(2,1)S(1)}, u32[]{:S(2)}, u32[]{:S(2)}) %collective-permute-start.2) | collective-permute-done | bytes 262176 | tf_op jit(solution)/shard_map/ppermute | solution.py:15
  16.8 0.0 copy-start.6
  16.8 3.8 %collective-permute-done.3.b1 = bf16[8,4,32,128]{3,2,1,0:T(8,128)(2,1)S(1)} collective-permute-done((bf16[8,4,32,128]{3,2,1,0:T(8,128)(2,1)S(1)}, bf16[8,4,32,128]{3,2,1,0:T(8,128)(2,1)S(1)}, u32[]{:S(2)}, u32[]{:S(2)}) %collective-permute-start.3) | collective-permute-done | bytes 262176 | tf_op jit(solution)/shard_map/ppermute | solution.py:16
  20.6 0.0 copy-start.7
  20.6 4.1 %collective-permute-done.prev_ref.prev = bf16[7,8,32,128]{3,2,1,0:T(8,128)(2,1)S(1)} collective-permute-done((bf16[7,8,32,128]{3,2,1,0:T(8,128)(2,1)S(1)}, bf16[7,8,32,128]{3,2,1,0:T(8,128)(2,1)S(1)}, u32[]{:S(2)}, u32[]{:S(2)}) %collective-permute-start) | collective-permute-done | bytes 458784 | tf_op jit(solution)/shard_map/ppermute | solution.py:15
  24.7 0.0 copy-start.1
  24.7 0.0 collective-permute-done.1.next_ref.following
  24.7 0.0 copy-start.2
  24.7 0.1 edge_rows.1
  24.8 5.0 %collective-permute-start.4 = (bf16[14,4,32,128]{3,2,1,0:T(8,128)(2,1)S(1)}, bf16[14,4,32,128]{3,2,1,0:T(8,128)(2,1)S(1)}, u32[]{:S(2)}, u32[]{:S(2)}) collective-permute-start(bf16[14,4,32,128]{3,2,1,0:T(8,128)(2,1)S(1)} %get-tuple-element.21), channel_id=1, source_target_pairs={{0,4},{4,8},{8,12},{1,5},{5,9},{9,13},{2,6},{6,10},{10,14},{3,7},{... | collective-permute-start | bytes 1376264 | tf_op jit(solution)/shard_map/ppermute | solution.py:15
  29.8 1.3 %collective-permute-start.5 = (bf16[14,4,32,128]{3,2,1,0:T(8,128)(2,1)S(1)}, bf16[14,4,32,128]{3,2,1,0:T(8,128)(2,1)S(1)}, u32[]{:S(2)}, u32[]{:S(2)}) collective-permute-start(bf16[14,4,32,128]{3,2,1,0:T(8,128)(2,1)S(1)} %get-tuple-element.22), channel_id=1, source_target_pairs={{4,0},{8,4},{12,8},{5,1},{9,5},{13,9},{6,2},{10,6},{14,10},{7,3},{... | collective-permute-start | bytes 1376264 | tf_op jit(solution)/shard_map/ppermute | solution.py:16
  31.1 0.0 copy-done
  31.1 2.1 %pack_mid.1.tile_ref = f32[22,32,128]{2,1,0:T(8,128)S(1)} custom-call(bf16[7,8,32,128]{3,2,1,0:T(8,128)(2,1)S(1)} %collective-permute-done.prev_ref.prev, bf16[8,8,32,128]{3,2,1,0:T(8,128)(2,1)S(1)} %pad_maximum_fusion.mine_ref.mine, bf16[7,8,32,128]{3,2,1,0:T(8,128)(2,1)S(1)} %collective-permute-done.1.next_ref.following, ...), custom_call_target="tpu_custom_call" | custom-call | bytes 2097152 | tf_op jit(solution)/shard_map/pack_mid/pallas_call | solution.py:83
  33.2 0.0 copy-done.6
  33.2 0.0 copy-done.7
  33.2 0.0 copy-done.1
  33.2 0.0 copy-done.2
  33.2 0.0 copy-start.8
  33.3 0.0 copy-start.9
  33.3 4.8 %collective-permute-done.4.a2 = bf16[14,4,32,128]{3,2,1,0:T(8,128)(2,1)S(1)} collective-permute-done((bf16[14,4,32,128]{3,2,1,0:T(8,128)(2,1)S(1)}, bf16[14,4,32,128]{3,2,1,0:T(8,128)(2,1)S(1)}, u32[]{:S(2)}, u32[]{:S(2)}) %collective-permute-start.4) | collective-permute-done | bytes 458784 | tf_op jit(solution)/shard_map/ppermute | solution.py:15
  38.0 0.0 copy-start.4
  38.0 3.9 %collective-permute-done.5.b2 = bf16[14,4,32,128]{3,2,1,0:T(8,128)(2,1)S(1)} collective-permute-done((bf16[14,4,32,128]{3,2,1,0:T(8,128)(2,1)S(1)}, bf16[14,4,32,128]{3,2,1,0:T(8,128)(2,1)S(1)}, u32[]{:S(2)}, u32[]{:S(2)}) %collective-permute-start.5) | collective-permute-done | bytes 458784 | tf_op jit(solution)/shard_map/ppermute | solution.py:16
  41.9 0.0 copy-start.5
  41.9 2.0 %pack_edges.1 = (bf16[11,32,128]{2,1,0:T(8,128)(2,1)S(1)}, bf16[11,32,128]{2,1,0:T(8,128)(2,1)S(1)}) custom-call(bf16[14,4,32,128]{3,2,1,0:T(8,128)(2,1)S(1)} %collective-permute-done.4.a2, bf16[14,4,32,128]{3,2,1,0:T(8,128)(2,1)S(1)} %collective-permute-done.5.b2, f32[22,32,128]{2,1,0:T(8,128)S(1)} %pack_mid.1.tile_ref), custom_call_target="tpu_custom_call" | custom-call | bytes 2097152 | tf_op jit(solution)/shard_map/pack_edges/pallas_call | solution.py:116
  43.9 4.9 %collective-permute-start.6 = (bf16[11,32,128]{2,1,0:T(8,128)(2,1)S(1)}, bf16[11,32,128]{2,1,0:T(8,128)(2,1)S(1)}, u32[]{:S(2)}, u32[]{:S(2)}) collective-permute-start(bf16[11,32,128]{2,1,0:T(8,128)(2,1)S(1)} %get-tuple-element.23), channel_id=1, source_target_pairs={{0,1},{1,2},{2,3},{4,5},{5,6},{6,7},{8,9},{9,10},{10,11},{12,13},{... | collective-permute-start | bytes 270344 | tf_op jit(solution)/shard_map/ppermute | solution.py:15
  48.8 1.9 %collective-permute-start.7 = (bf16[11,32,128]{2,1,0:T(8,128)(2,1)S(1)}, bf16[11,32,128]{2,1,0:T(8,128)(2,1)S(1)}, u32[]{:S(2)}, u32[]{:S(2)}) collective-permute-start(bf16[11,32,128]{2,1,0:T(8,128)(2,1)S(1)} %get-tuple-element.24), channel_id=1, source_target_pairs={{1,0},{2,1},{3,2},{5,4},{6,5},{7,6},{9,8},{10,9},{11,10},{13,12},{... | collective-permute-start | bytes 270344 | tf_op jit(solution)/shard_map/ppermute | solution.py:16
  50.7 0.0 copy-done.8
  50.7 0.0 copy-done.9
  50.8 1.0 pair_matrices.1.w_ref
  51.8 0.0 copy-done.4
  51.8 0.0 copy-done.5
  51.8 0.0 copy-start.3
  51.8 0.8 copy-done.3
  52.6 0.0 collective-permute-done.6.rl_ref
  52.6 0.0 copy-start.12
  52.6 2.0 %collective-permute-done.7.rr_ref = bf16[11,32,128]{2,1,0:T(8,128)(2,1)S(1)} collective-permute-done((bf16[11,32,128]{2,1,0:T(8,128)(2,1)S(1)}, bf16[11,32,128]{2,1,0:T(8,128)(2,1)S(1)}, u32[]{:S(2)}, u32[]{:S(2)}) %collective-permute-start.7) | collective-permute-done | bytes 90144 | tf_op jit(solution)/shard_map/ppermute | solution.py:16
  54.7 0.0 copy-done.12
  54.7 0.0 copy-start.13
  54.7 0.6 copy-done.13
  55.3 13.3 %first_convs.1 = (bf16[10,14,32,128]{3,2,1,0:T(8,128)(2,1)}, bf16[10,128,128]{2,1,0:T(8,128)(2,1)}, bf16[4,8,32,128]{3,2,1,0:T(8,128)(2,1)}, f32[4,64,128]{2,1,0...) custom-call(bf16[7,8,32,128]{3,2,1,0:T(8,128)(2,1)} %copy-done.1, ...), custom_call_target="tpu_custom_call" | custom-call | flops 8589934592 | bytes 8388608 | tf_op jit(solution)/shard_map/first_convs/pallas_call | solution.py:307
  68.6 4.3 %all-to-all-start = ((f32[16,1,128]{2,1,0:T(1,128)}), f32[16,1,128]{2,1,0:T(1,128)S(1)}, u32[]{:S(2)}, u32[]{:S(2)}) async-start(f32[16,1,128]{2,1,0:T(1,128)} %get-tuple-element.31), calls=%async_computation | async-start | bytes 16384 | tf_op jit(solution)/shard_map/all_to_all | solution.py:467
  72.9 0.6 stack.15.place
  73.5 4.9 %all-to-all-done = f32[16,1,128]{2,1,0:T(1,128)S(1)} async-done(((f32[16,1,128]{2,1,0:T(1,128)}), f32[16,1,128]{2,1,0:T(1,128)S(1)}, u32[]{:S(2)}, u32[]{:S(2)}) %all-to-all-start) | async-done | bytes 8224 | tf_op jit(solution)/shard_map/all_to_all | solution.py:467
  78.4 0.0 copy-start.11
  78.4 0.6 broadcast_in_dim.10
  79.0 20.2 %all-to-all-start.1 = ((f32[32,1,128]{2,1,0:T(1,128)}), f32[32,1,128]{2,1,0:T(1,128)S(1)}, u32[]{:S(2)}, u32[]{:S(2)}) async-start(f32[32,1,128]{2,1,0:T(1,128)} %broadcast_in_dim.10), calls=%async_computation.1 | async-start | bytes 32768 | tf_op jit(solution)/shard_map/all_to_all | solution.py:467
  99.3 0.0 copy-done.11
  99.3 12.4 %second_convs.1 = f32[4,8,32,128]{3,2,1,0:T(8,128)} custom-call(s32[6]{0:T(128)} %stack.15.place, bf16[10,14,32,128]{3,2,1,0:T(8,128)(2,1)} %get-tuple-element.25.hid_in, bf16[10,128,128]{2,1,0:T(8,128)(2,1)} %get-tuple-element.26.hid_h_in, bf16[4,8,32,128]{3,2,1,0:T(8,128)(2,1)} %get-tuple-element.27.own_in, f32[4,64,128]{2,1,0:T(8,128)} %get-tuple-element.28.own_h_in, ...), custom_call_target="tpu_custom_call" | custom-call | flops 8589934592 | bytes 4194304 | tf_op jit(solution)/shard_map/second_convs/pallas_call | solution.py:403
  111.7 1.1 all-to-all-done.1
  112.8 0.6 reduce_sum.20
  114.1 1.1 divide_bitcast_fusion
  115.2 1.1 copy.15
  (7 shorter events, 0.2 us)
Async XLA Ops:
  0.6 1.1 copy-start.10
  2.0 29.1 %copy-start = (bf16[8,8,32,128]{3,2,1,0:T(8,128)(2,1)}, bf16[8,8,32,128]{3,2,1,0:T(8,128)(2,1)S(1)}, u32[]{:S(2)}) copy-start(bf16[8,8,32,128]{3,2,1,0:T(8,128)(2,1)S(1)} %pad_maximum_fusion.mine_ref.mine) | copy-start | bytes 1572868
  2.0 22.7 %collective-permute-start = (bf16[7,8,32,128]{3,2,1,0:T(8,128)(2,1)S(1)}, bf16[7,8,32,128]{3,2,1,0:T(8,128)(2,1)S(1)}, u32[]{:S(2)}, u32[]{:S(2)}) collective-permute-start(bf16[7,8,32,128]{3,2,1,0:T(8,128)(2,1)S(1)} %slice.24), channel_id=1, source_target_pairs={{0,16},{16,32},{32,48},{48,64},{64,80},{80,96},{96,112},{112,128},... | collective-permute-start | bytes 1376264 | tf_op jit(solution)/shard_map/ppermute | solution.py:15
  7.6 17.1 %collective-permute-start.1 = (bf16[7,8,32,128]{3,2,1,0:T(8,128)(2,1)S(1)}, bf16[7,8,32,128]{3,2,1,0:T(8,128)(2,1)S(1)}, u32[]{:S(2)}, u32[]{:S(2)}) collective-permute-start(bf16[7,8,32,128]{3,2,1,0:T(8,128)(2,1)S(1)} %pad_maximum_fusion.1), channel_id=1, source_target_pairs={{16,0},{32,16},{48,32},{64,48},{80,64},{96,80},{112,96},{128,112},... | collective-permute-start | bytes 1376264 | tf_op jit(solution)/shard_map/ppermute | solution.py:16
  8.9 7.8 %collective-permute-start.2 = (bf16[8,4,32,128]{3,2,1,0:T(8,128)(2,1)S(1)}, bf16[8,4,32,128]{3,2,1,0:T(8,128)(2,1)S(1)}, u32[]{:S(2)}, u32[]{:S(2)}) collective-permute-start(bf16[8,4,32,128]{3,2,1,0:T(8,128)(2,1)S(1)} %get-tuple-element.39), channel_id=1, source_target_pairs={{0,4},{4,8},{8,12},{1,5},{5,9},{9,13},{2,6},{6,10},{10,14},{3,7},{... | collective-permute-start | bytes 786440 | tf_op jit(solution)/shard_map/ppermute | solution.py:15
  12.2 8.5 %collective-permute-start.3 = (bf16[8,4,32,128]{3,2,1,0:T(8,128)(2,1)S(1)}, bf16[8,4,32,128]{3,2,1,0:T(8,128)(2,1)S(1)}, u32[]{:S(2)}, u32[]{:S(2)}) collective-permute-start(bf16[8,4,32,128]{3,2,1,0:T(8,128)(2,1)S(1)} %get-tuple-element.38), channel_id=1, source_target_pairs={{4,0},{8,4},{12,8},{5,1},{9,5},{13,9},{6,2},{10,6},{14,10},{7,3},{... | collective-permute-start | bytes 786440 | tf_op jit(solution)/shard_map/ppermute | solution.py:16
  16.8 16.4 %copy-start.6 = (bf16[8,4,32,128]{3,2,1,0:T(8,128)(2,1)}, bf16[8,4,32,128]{3,2,1,0:T(8,128)(2,1)S(1)}, u32[]{:S(2)}) copy-start(bf16[8,4,32,128]{3,2,1,0:T(8,128)(2,1)S(1)} %collective-permute-done.2.a1) | copy-start | bytes 786436
  20.6 12.6 %copy-start.7 = (bf16[8,4,32,128]{3,2,1,0:T(8,128)(2,1)}, bf16[8,4,32,128]{3,2,1,0:T(8,128)(2,1)S(1)}, u32[]{:S(2)}) copy-start(bf16[8,4,32,128]{3,2,1,0:T(8,128)(2,1)S(1)} %collective-permute-done.3.b1) | copy-start | bytes 786436
  24.7 8.5 %copy-start.1 = (bf16[7,8,32,128]{3,2,1,0:T(8,128)(2,1)}, bf16[7,8,32,128]{3,2,1,0:T(8,128)(2,1)S(1)}, u32[]{:S(2)}) copy-start(bf16[7,8,32,128]{3,2,1,0:T(8,128)(2,1)S(1)} %collective-permute-done.prev_ref.prev) | copy-start | bytes 1376260
  24.7 8.5 %copy-start.2 = (bf16[7,8,32,128]{3,2,1,0:T(8,128)(2,1)}, bf16[7,8,32,128]{3,2,1,0:T(8,128)(2,1)S(1)}, u32[]{:S(2)}) copy-start(bf16[7,8,32,128]{3,2,1,0:T(8,128)(2,1)S(1)} %collective-permute-done.1.next_ref.following) | copy-start | bytes 1376260
  24.8 13.2 %collective-permute-start.4 = (bf16[14,4,32,128]{3,2,1,0:T(8,128)(2,1)S(1)}, bf16[14,4,32,128]{3,2,1,0:T(8,128)(2,1)S(1)}, u32[]{:S(2)}, u32[]{:S(2)}) collective-permute-start(bf16[14,4,32,128]{3,2,1,0:T(8,128)(2,1)S(1)} %get-tuple-element.21), channel_id=1, source_target_pairs={{0,4},{4,8},{8,12},{1,5},{5,9},{9,13},{2,6},{6,10},{10,14},{3,7},{... | collective-permute-start | bytes 1376264 | tf_op jit(solution)/shard_map/ppermute | solution.py:15
  29.8 12.1 %collective-permute-start.5 = (bf16[14,4,32,128]{3,2,1,0:T(8,128)(2,1)S(1)}, bf16[14,4,32,128]{3,2,1,0:T(8,128)(2,1)S(1)}, u32[]{:S(2)}, u32[]{:S(2)}) collective-permute-start(bf16[14,4,32,128]{3,2,1,0:T(8,128)(2,1)S(1)} %get-tuple-element.22), channel_id=1, source_target_pairs={{4,0},{8,4},{12,8},{5,1},{9,5},{13,9},{6,2},{10,6},{14,10},{7,3},{... | collective-permute-start | bytes 1376264 | tf_op jit(solution)/shard_map/ppermute | solution.py:16
  33.2 17.5 %copy-start.8 = (bf16[27,32,32]{2,1,0:T(8,128)(2,1)S(1)}, bf16[27,32,32]{2,1,0:T(8,128)(2,1)}, u32[]{:S(2)}) copy-start(bf16[27,32,32]{2,1,0:T(8,128)(2,1)} %k1_ref.1) | copy-start | bytes 165892
  33.3 17.5 %copy-start.9 = (bf16[27,32,32]{2,1,0:T(8,128)(2,1)S(1)}, bf16[27,32,32]{2,1,0:T(8,128)(2,1)}, u32[]{:S(2)}) copy-start(bf16[27,32,32]{2,1,0:T(8,128)(2,1)} %k2_ref.1) | copy-start | bytes 165892
  38.0 13.7 %copy-start.4 = (bf16[14,4,32,128]{3,2,1,0:T(8,128)(2,1)}, bf16[14,4,32,128]{3,2,1,0:T(8,128)(2,1)S(1)}, u32[]{:S(2)}) copy-start(bf16[14,4,32,128]{3,2,1,0:T(8,128)(2,1)S(1)} %collective-permute-done.4.a2) | copy-start | bytes 1376260
  41.9 9.9 %copy-start.5 = (bf16[14,4,32,128]{3,2,1,0:T(8,128)(2,1)}, bf16[14,4,32,128]{3,2,1,0:T(8,128)(2,1)S(1)}, u32[]{:S(2)}) copy-start(bf16[14,4,32,128]{3,2,1,0:T(8,128)(2,1)S(1)} %collective-permute-done.5.b2) | copy-start | bytes 1376260
  43.9 8.7 %collective-permute-start.6 = (bf16[11,32,128]{2,1,0:T(8,128)(2,1)S(1)}, bf16[11,32,128]{2,1,0:T(8,128)(2,1)S(1)}, u32[]{:S(2)}, u32[]{:S(2)}) collective-permute-start(bf16[11,32,128]{2,1,0:T(8,128)(2,1)S(1)} %get-tuple-element.23), channel_id=1, source_target_pairs={{0,1},{1,2},{2,3},{4,5},{5,6},{6,7},{8,9},{9,10},{10,11},{12,13},{... | collective-permute-start | bytes 270344 | tf_op jit(solution)/shard_map/ppermute | solution.py:15
  48.8 5.8 %collective-permute-start.7 = (bf16[11,32,128]{2,1,0:T(8,128)(2,1)S(1)}, bf16[11,32,128]{2,1,0:T(8,128)(2,1)S(1)}, u32[]{:S(2)}, u32[]{:S(2)}) collective-permute-start(bf16[11,32,128]{2,1,0:T(8,128)(2,1)S(1)} %get-tuple-element.24), channel_id=1, source_target_pairs={{1,0},{2,1},{3,2},{5,4},{6,5},{7,6},{9,8},{10,9},{11,10},{13,12},{... | collective-permute-start | bytes 270344 | tf_op jit(solution)/shard_map/ppermute | solution.py:16
  51.8 0.8 copy-start.3
  52.6 2.1 %copy-start.12 = (bf16[11,32,128]{2,1,0:T(8,128)(2,1)}, bf16[11,32,128]{2,1,0:T(8,128)(2,1)S(1)}, u32[]{:S(2)}) copy-start(bf16[11,32,128]{2,1,0:T(8,128)(2,1)S(1)} %collective-permute-done.6.rl_ref) | copy-start | bytes 270340
  54.7 0.6 copy-start.13
  68.6 9.8 %all-to-all-start = ((f32[16,1,128]{2,1,0:T(1,128)}), f32[16,1,128]{2,1,0:T(1,128)S(1)}, u32[]{:S(2)}, u32[]{:S(2)}) async-start(f32[16,1,128]{2,1,0:T(1,128)} %get-tuple-element.31), calls=%async_computation | async-start | bytes 16384 | tf_op jit(solution)/shard_map/all_to_all | solution.py:467
  78.4 20.8 %copy-start.11 = (f32[128]{0:T(128)}, f32[128]{0:T(128)S(1)}, u32[]{:S(2)}) copy-start(f32[128]{0:T(128)S(1)} %reduce_sum.16) | copy-start | bytes 1540
  79.0 33.8 %all-to-all-start.1 = ((f32[32,1,128]{2,1,0:T(1,128)}), f32[32,1,128]{2,1,0:T(1,128)S(1)}, u32[]{:S(2)}, u32[]{:S(2)}) async-start(f32[32,1,128]{2,1,0:T(1,128)} %broadcast_in_dim.10), calls=%async_computation.1 | async-start | bytes 32768 | tf_op jit(solution)/shard_map/all_to_all | solution.py:467

commit v4 on v3

--- a/solution.py
+++ b/solution.py
@@ -181,25 +181,30 @@
 
 
 def first_kernel_body(
-    prev, mine, following, a1, b1, a2, b2, rl_ref, rr_ref, w_ref,
+    prev, mine, following, a1, b1, a2, b2, rl_in, rr_in, w_in,
     hid_out, hid_h_out, own_out, own_h_out, slope_out, slope_h_out, sum_ref,
-    f_ref, edge, t_h, hid, hid_h, own_ref, own_h, slope_h, sum_acc, sems, out_sems,
+    f_ref, rl_ref, rr_ref, w_ref, edge, t_h, hid, hid_h, own_ref, own_h, slope_h, sum_acc, sems, out_sems,
 ):
     moves = [
+        (rl_in, rl_ref),
+        (rr_in, rr_ref),
+        (w_in.at[0:2], w_ref),
         (prev, f_ref.at[0:7, 4:12]),
+        (a2.at[0:7], f_ref.at[0:7, 0:4]),
+        (b2.at[0:7], f_ref.at[0:7, 12:16]),
         (mine, f_ref.at[7:15, 4:12]),
-        (following, f_ref.at[15:22, 4:12]),
         (a1, f_ref.at[7:15, 0:4]),
         (b1, f_ref.at[7:15, 12:16]),
-        (a2.at[0:7], f_ref.at[0:7, 0:4]),
+        (following, f_ref.at[15:22, 4:12]),
         (a2.at[7:14], f_ref.at[15:22, 0:4]),
-        (b2.at[0:7], f_ref.at[0:7, 12:16]),
         (b2.at[7:14], f_ref.at[15:22, 12:16]),
     ]
     copies = [pltpu.make_async_copy(x, y, sems.at[i]) for i, (x, y) in enumerate(moves)]
     for copy in copies:
         copy.start()
 
+    for copy in copies[:3]:
+        copy.wait()
     lane = lax.broadcasted_iota(jnp.int32, (CH, LANES), 1)
     low = (lane & 7) < 4
 
@@ -239,8 +244,6 @@
         return f_ref[t_layer(t), pl.ds(r, 4)].reshape(4 * CH, LANES)
 
     lax.fori_loop(0, 6, keep_slopes, 0)
-    for copy in copies:
-        copy.wait()
 
     def stage_hidden(m, carry):
         def put(p, v):
@@ -253,7 +256,10 @@
         convolve_layer(w_ref[0], field_rows, lambda t: t_h[t], m, range(7), put, put_halo)
         return carry
 
-    lax.fori_loop(0, 10, stage_hidden, 0)
+    for start, end, arrived in ((0, 2, 3), (2, 6, 6), (6, 10, 9)):
+        for copy in copies[arrived : arrived + 3]:
+            copy.wait()
+        lax.fori_loop(start, end, stage_hidden, 0)
     early = [
         (hid, hid_out), (hid_h, hid_h_out), (slope_h, slope_h_out),
         (f_ref.at[6:10, 3:13], slope_out.at[0:4]), (f_ref.at[14:16, 3:13], slope_out.at[4:6]),
@@ -307,15 +313,18 @@
     return pl.pallas_call(
         first_kernel_body,
         out_shape=(*fields, shape((spread, 1, LANES), jnp.float32)),
-        in_specs=[anywhere] * 7 + [local] * 3,
+        in_specs=[anywhere] * 10,
         out_specs=(*([anywhere] * 6), local),
         scratch_shapes=[
             pltpu.VMEM((22, 16, CH, LANES), jnp.bfloat16),
+            pltpu.VMEM(rl.shape, rl.dtype),
+            pltpu.VMEM(rr.shape, rr.dtype),
+            pltpu.VMEM((2, *weights.shape[1:]), weights.dtype),
             pltpu.VMEM((22, CH, LANES), jnp.float32),
             pltpu.VMEM((12, 4 * CH, LANES), jnp.bfloat16),
             *keep,
             pltpu.VMEM((8, LANES), jnp.float32),
-            pltpu.SemaphoreType.DMA((9,)),
+            pltpu.SemaphoreType.DMA((12,)),
             pltpu.SemaphoreType.DMA((7,)),
         ],
         compiler_params=pltpu.CompilerParams(vmem_limit_bytes=62 << 20),
@@ -325,17 +334,17 @@
 
 
 def second_kernel_body(
-    place, hid_in, hid_h_in, own_in, own_h_in, slope_in, slope_h_in, w_ref, after, out_ref,
-    hid, hid_h, own_h, slope_ref, slope_h, img, img_h, pul, pul_h, sems,
+    place, hid_in, hid_h_in, own_in, own_h_in, slope_in, slope_h_in, w_in, after, out_ref,
+    w_ref, hid, hid_h, own_h, slope_ref, slope_h, img, img_h, pul, pul_h, sems,
 ):
     moves = [
-        (hid_in, hid), (hid_h_in, hid_h), (own_in, img.at[2:6, 2:10]), (own_h_in, own_h),
+        (w_in, w_ref), (hid_in, hid), (hid_h_in, hid_h), (own_in, img.at[2:6, 2:10]), (own_h_in, own_h),
         (slope_in, slope_ref), (slope_h_in, slope_h),
     ]
     copies = [pltpu.make_async_copy(x, y, sems.at[i]) for i, (x, y) in enumerate(moves)]
     for copy in copies:
         copy.start()
-    for copy in copies[:2]:
+    for copy in copies[:3]:
         copy.wait()
     wide = lax.broadcasted_iota(jnp.int32, (2 * CH, LANES), 1)
     wide8 = wide & 7
@@ -365,7 +374,7 @@
 
     lax.fori_loop(0, 4, stage_ends, 0)
 
-    for copy in copies[2:]:
+    for copy in copies[3:]:
         copy.wait()
 
     def stage_rim(i, carry):
@@ -404,15 +413,15 @@
         second_kernel_body,
         out_shape=jax.ShapeDtypeStruct((4, 8, CH, LANES), jnp.float32),
         in_specs=[pl.BlockSpec(memory_space=pltpu.SMEM)]
-        + [pl.BlockSpec(memory_space=pl.ANY)] * 6
-        + [pl.BlockSpec(memory_space=pltpu.VMEM)] * 2,
+        + [pl.BlockSpec(memory_space=pl.ANY)] * 8,
         scratch_shapes=[
+            pltpu.VMEM(weights.shape, weights.dtype),
             *[pltpu.VMEM(f.shape, f.dtype) for i, f in enumerate(fields) if i != 2],
             pltpu.VMEM((8, 12, CH, LANES), jnp.bfloat16),
             pltpu.VMEM((8, 4 * CH, LANES), jnp.bfloat16),
             pltpu.VMEM((6, 10, CH, LANES), jnp.bfloat16),
             pltpu.VMEM((6, 4 * CH, LANES), jnp.bfloat16),
-            pltpu.SemaphoreType.DMA((6,)),
+            pltpu.SemaphoreType.DMA((7,)),
         ],
         compiler_params=pltpu.CompilerParams(vmem_limit_bytes=62 << 20),
         cost_estimate=pl.CostEstimate(flops=8 << 30, bytes_accessed=4 << 20, transcendentals=0),
@@ -447,35 +456,71 @@
     )(first_kernel, second_kernel)
 
 
+def finish_kernel(result, parts, out_ref, norm_ref, block, sems):
+    layers = block.shape[0]
+    copies = [pltpu.make_async_copy(result.at[x], block.at[x], sems.at[x]) for x in range(layers)]
+    for copy in copies:
+        copy.start()
+    total = jnp.sum(jnp.sum(parts[...], axis=0), axis=1, keepdims=True)
+    norm = jnp.sqrt(total + 1e-06)
+    norm_ref[0] = norm[0, 0]
+    scale = jnp.broadcast_to(norm, (8, LANES))
+    for x in range(layers):
+        copies[x].wait()
+        out_ref[:, x] = block[x].transpose(1, 0, 2) / scale
+
+
+def finish(result, parts):
+    return pl.pallas_call(
+        finish_kernel,
+        out_shape=(
+            jax.ShapeDtypeStruct((CH, 4, 8, LANES), jnp.float32),
+            jax.ShapeDtypeStruct((1,), jnp.float32),
+        ),
+        in_specs=[
+            pl.BlockSpec(memory_space=pl.ANY),
+            pl.BlockSpec(memory_space=pltpu.VMEM),
+        ],
+        out_specs=(
+            pl.BlockSpec(memory_space=pltpu.VMEM),
+            pl.BlockSpec(memory_space=pltpu.SMEM),
+        ),
+        scratch_shapes=[
+            pltpu.VMEM(result.shape, jnp.float32),
+            pltpu.SemaphoreType.DMA((result.shape[0],)),
+        ],
+        compiler_params=pltpu.CompilerParams(vmem_limit_bytes=62 << 20),
+        name="finish",
+    )(result, parts)
+
+
 def on_device(tangent, slopes, first_kernel, second_kernel):
     t = tangent.transpose(1, 2, 0, 3)
     s = slopes.transpose(1, 2, 0, 3)
     mine = jnp.concatenate([s[0:3], t, s[3:4]], axis=0)
     prev, following = shift_pair(mine[1:8], mine[0:7], "gx")
     a1, b1 = shift_pair(mine[:, 4:8], mine[:, 0:4], "gy")
-    prev, following, a1, b1 = lax.optimization_barrier((prev, following, a1, b1))
+    weights = pair_matrices(first_kernel, second_kernel)
+    prev, following, a1, b1, weights = lax.optimization_barrier(
+        (prev, following, a1, b1, weights)
+    )
     low, top = edge_rows(prev, following)
     a2, b2 = shift_pair(low, top, "gy")
-    weights = pair_matrices(first_kernel, second_kernel)
     left_edge, right_edge = pack_edges(a2, b2, pack_mid(prev, mine, following, a1, b1))
     rl, rr = shift_pair(right_edge, left_edge, "gz")
     plane = lax.axis_size(("gy", "gz"))
     pieces = (prev, mine, following, a1, b1, a2, b2)
     *fields, spread = first_convs(pieces, rl, rr, weights, plane)
 
-    def collect(v, axes):
-        return jnp.sum(lax.all_to_all(v, axes, 0, 0, tiled=True), axis=0, keepdims=True)
-
     place = jnp.stack(
         [lax.axis_index(a) for a in ALL] + [jnp.int32(lax.axis_size(a) - 1) for a in ALL]
     ).astype(jnp.int32)
-    part = collect(spread, ("gy", "gz"))
+    parts = lax.all_to_all(spread, ("gy", "gz"), 0, 0, tiled=True)
+    part = jnp.sum(parts, axis=0, keepdims=True)
     result = second_convs(place, fields, weights, part)
     count = lax.axis_size("gx")
-    part = collect(jnp.broadcast_to(part, (count, 1, LANES)), "gx")
-    jvp_norm = jnp.sqrt(jnp.sum(part) + 1e-06)
-    next_vector = result.transpose(2, 0, 1, 3) / jvp_norm
-    return (next_vector, jvp_norm.reshape(1))
+    parts = lax.all_to_all(jnp.broadcast_to(part, (count, 1, LANES)), "gx", 0, 0, tiled=True)
+    return finish(result, parts)
 
 
 def solution(mesh):

time: 118 us -> 117 us (level)
  Pallas kernels: 30.8 us -> 33.2 us
  between operations: 2.76 us -> 0.93 us
  other arithmetic: 1.85 us -> 0.15 us
    pallas_call x0 -> x1, Pallas kernels: none -> 2.69 us  [finish(): pl.pallas_call(finish_kernel, out_shape=(jax.ShapeDtypeStruct((CH, 4, 8,...]
    ppermute x4, waiting for transfers between devices: 12.2 us -> 10.3 us  [shift_pair(): from_prev = lax.ppermute(up, axis, [(i, i + 1) for i in range(ends)])]
    ppermute x4, waiting for transfers between devices: 9.74 us -> 11.6 us  [shift_pair(): from_next = lax.ppermute(down, axis, [(i + 1, i) for i in range(ends)])]
    unnamed x31 -> x32, local copies, waits for them, and re-layouts: 3.8 us -> 3.33 us
where the time goes in v4:
time: 117 us; the launch traced here: 116 us
  starting transfers between devices  49.1 us (42%)
  Pallas kernels  33.2 us (28%)
  waiting for transfers between devices  28.1 us (24%)
  local copies, waits for them, and re-layouts  4.65 us (4%)
    all_to_all x1, starting transfers between devices, on_device(): lax.all_to_all(jnp.broadcast_to(part, (count, 1, LANES)), 'gx', 0, 0, til...  20.2 us
    ppermute x4, starting transfers between devices, shift_pair(): from_prev = lax.ppermute(up, axis, [(i, i + 1) for i in range(ends)])  18.7 us
    pallas_call x1, Pallas kernels, first_convs(): pl.pallas_call(first_kernel_body, out_shape=(*fields, shape((spread, 1, L...  13.2 us
    pallas_call x1, Pallas kernels, second_convs(): pl.pallas_call(second_kernel_body, out_shape=jax.ShapeDtypeStruct((4, 8,...  12.2 us
    ppermute x4, waiting for transfers between devices, shift_pair(): from_next = lax.ppermute(down, axis, [(i + 1, i) for i in range(ends)])  11.6 us
    ppermute x4, waiting for transfers between devices, shift_pair(): from_prev = lax.ppermute(up, axis, [(i, i + 1) for i in range(ends)])  10.3 us
    ppermute x4, starting transfers between devices, shift_pair(): from_next = lax.ppermute(down, axis, [(i + 1, i) for i in range(ends)])  5.8 us
    all_to_all x1, waiting for transfers between devices, on_device(): parts = lax.all_to_all(spread, ('gy', 'gz'), 0, 0, tiled=True)  4.87 us
  transfers between devices with their start and end apart: 10, of which 8 were waited for; matrix products, arithmetic and copies ran while one was open for 1% of the time, Pallas kernels for 13%

profile of v4, /device:TPU:1, one launch (start us, length us, event | category | flops | bytes accessed | tf_op | source)
XLA Modules:
  0.0 116.1 jit_solution(4685210891080077847)
XLA Ops:
  0.6 0.0 copy-start.10
  0.6 1.1 copy.11
  1.8 0.0 copy-done.10
  1.8 0.1 copy.10
  1.9 0.1 pad_maximum_fusion.mine_ref.mine
  2.0 0.0 copy-start
  2.0 0.0 copy-start.8
  2.0 0.0 copy-start.9
  2.0 5.6 %collective-permute-start = (bf16[7,8,32,128]{3,2,1,0:T(8,128)(2,1)S(1)}, bf16[7,8,32,128]{3,2,1,0:T(8,128)(2,1)S(1)}, u32[]{:S(2)}, u32[]{:S(2)}) collective-permute-start(bf16[7,8,32,128]{3,2,1,0:T(8,128)(2,1)S(1)} %slice.24), channel_id=1, source_target_pairs={{0,16},{16,32},{32,48},{48,64},{64,80},{80,96},{96,112},{112,128},... | collective-permute-start | bytes 1376264 | tf_op jit(solution)/shard_map/ppermute | solution.py:15
  7.7 1.3 %collective-permute-start.1 = (bf16[7,8,32,128]{3,2,1,0:T(8,128)(2,1)S(1)}, bf16[7,8,32,128]{3,2,1,0:T(8,128)(2,1)S(1)}, u32[]{:S(2)}, u32[]{:S(2)}) collective-permute-start(bf16[7,8,32,128]{3,2,1,0:T(8,128)(2,1)S(1)} %pad_maximum_fusion.1), channel_id=1, source_target_pairs={{16,0},{32,16},{48,32},{64,48},{80,64},{96,80},{112,96},{128,112},... | collective-permute-start | bytes 1376264 | tf_op jit(solution)/shard_map/ppermute | solution.py:16
  9.1 3.2 %collective-permute-start.2 = (bf16[8,4,32,128]{3,2,1,0:T(8,128)(2,1)S(1)}, bf16[8,4,32,128]{3,2,1,0:T(8,128)(2,1)S(1)}, u32[]{:S(2)}, u32[]{:S(2)}) collective-permute-start(bf16[8,4,32,128]{3,2,1,0:T(8,128)(2,1)S(1)} %get-tuple-element.35), channel_id=1, source_target_pairs={{0,4},{4,8},{8,12},{1,5},{5,9},{9,13},{2,6},{6,10},{10,14},{3,7},{... | collective-permute-start | bytes 786440 | tf_op jit(solution)/shard_map/ppermute | solution.py:15
  12.3 1.3 %collective-permute-start.3 = (bf16[8,4,32,128]{3,2,1,0:T(8,128)(2,1)S(1)}, bf16[8,4,32,128]{3,2,1,0:T(8,128)(2,1)S(1)}, u32[]{:S(2)}, u32[]{:S(2)}) collective-permute-start(bf16[8,4,32,128]{3,2,1,0:T(8,128)(2,1)S(1)} %get-tuple-element.34), channel_id=1, source_target_pairs={{4,0},{8,4},{12,8},{5,1},{9,5},{13,9},{6,2},{10,6},{14,10},{7,3},{... | collective-permute-start | bytes 786440 | tf_op jit(solution)/shard_map/ppermute | solution.py:16
  13.6 0.0 copy-done.8
  13.6 0.0 copy-done.9
  13.6 1.0 pair_matrices.1.w_in
  14.6 0.0 copy-start.3
  14.6 0.8 copy-done.3
  15.5 1.4 %collective-permute-done.2.a1 = bf16[8,4,32,128]{3,2,1,0:T(8,128)(2,1)S(1)} collective-permute-done((bf16[8,4,32,128]{3,2,1,0:T(8,128)(2,1)S(1)}, bf16[8,4,32,128]{3,2,1,0:T(8,128)(2,1)S(1)}, u32[]{:S(2)}, u32[]{:S(2)}) %collective-permute-start.2) | collective-permute-done | bytes 262176 | tf_op jit(solution)/shard_map/ppermute | solution.py:15
  16.9 0.0 copy-start.6
  16.9 3.8 %collective-permute-done.3.b1 = bf16[8,4,32,128]{3,2,1,0:T(8,128)(2,1)S(1)} collective-permute-done((bf16[8,4,32,128]{3,2,1,0:T(8,128)(2,1)S(1)}, bf16[8,4,32,128]{3,2,1,0:T(8,128)(2,1)S(1)}, u32[]{:S(2)}, u32[]{:S(2)}) %collective-permute-start.3) | collective-permute-done | bytes 262176 | tf_op jit(solution)/shard_map/ppermute | solution.py:16
  20.8 0.0 copy-start.7
  20.8 4.1 %collective-permute-done.prev_ref.prev = bf16[7,8,32,128]{3,2,1,0:T(8,128)(2,1)S(1)} collective-permute-done((bf16[7,8,32,128]{3,2,1,0:T(8,128)(2,1)S(1)}, bf16[7,8,32,128]{3,2,1,0:T(8,128)(2,1)S(1)}, u32[]{:S(2)}, u32[]{:S(2)}) %collective-permute-start) | collective-permute-done | bytes 458784 | tf_op jit(solution)/shard_map/ppermute | solution.py:15
  24.9 0.0 copy-start.1
  24.9 0.0 collective-permute-done.1.next_ref.following
  24.9 0.0 copy-start.2
  24.9 0.1 edge_rows.1
  24.9 5.0 %collective-permute-start.4 = (bf16[14,4,32,128]{3,2,1,0:T(8,128)(2,1)S(1)}, bf16[14,4,32,128]{3,2,1,0:T(8,128)(2,1)S(1)}, u32[]{:S(2)}, u32[]{:S(2)}) collective-permute-start(bf16[14,4,32,128]{3,2,1,0:T(8,128)(2,1)S(1)} %get-tuple-element.22), channel_id=1, source_target_pairs={{0,4},{4,8},{8,12},{1,5},{5,9},{9,13},{2,6},{6,10},{10,14},{3,7},{... | collective-permute-start | bytes 1376264 | tf_op jit(solution)/shard_map/ppermute | solution.py:15
  30.0 1.3 %collective-permute-start.5 = (bf16[14,4,32,128]{3,2,1,0:T(8,128)(2,1)S(1)}, bf16[14,4,32,128]{3,2,1,0:T(8,128)(2,1)S(1)}, u32[]{:S(2)}, u32[]{:S(2)}) collective-permute-start(bf16[14,4,32,128]{3,2,1,0:T(8,128)(2,1)S(1)} %get-tuple-element.23), channel_id=1, source_target_pairs={{4,0},{8,4},{12,8},{5,1},{9,5},{13,9},{6,2},{10,6},{14,10},{7,3},{... | collective-permute-start | bytes 1376264 | tf_op jit(solution)/shard_map/ppermute | solution.py:16
  31.3 0.0 copy-done
  31.3 2.1 %pack_mid.1.tile_ref = f32[22,32,128]{2,1,0:T(8,128)S(1)} custom-call(bf16[7,8,32,128]{3,2,1,0:T(8,128)(2,1)S(1)} %collective-permute-done.prev_ref.prev, bf16[8,8,32,128]{3,2,1,0:T(8,128)(2,1)S(1)} %pad_maximum_fusion.mine_ref.mine, bf16[7,8,32,128]{3,2,1,0:T(8,128)(2,1)S(1)} %collective-permute-done.1.next_ref.following, ...), custom_call_target="tpu_custom_call" | custom-call | bytes 2097152 | tf_op jit(solution)/shard_map/pack_mid/pallas_call | solution.py:83
  33.4 0.0 copy-done.6
  33.4 0.0 copy-done.7
  33.4 0.0 copy-done.1
  33.4 0.0 copy-done.2
  33.4 4.8 %collective-permute-done.4.a2 = bf16[14,4,32,128]{3,2,1,0:T(8,128)(2,1)S(1)} collective-permute-done((bf16[14,4,32,128]{3,2,1,0:T(8,128)(2,1)S(1)}, bf16[14,4,32,128]{3,2,1,0:T(8,128)(2,1)S(1)}, u32[]{:S(2)}, u32[]{:S(2)}) %collective-permute-start.4) | collective-permute-done | bytes 458784 | tf_op jit(solution)/shard_map/ppermute | solution.py:15
  38.2 0.0 copy-start.4
  38.2 3.9 %collective-permute-done.5.b2 = bf16[14,4,32,128]{3,2,1,0:T(8,128)(2,1)S(1)} collective-permute-done((bf16[14,4,32,128]{3,2,1,0:T(8,128)(2,1)S(1)}, bf16[14,4,32,128]{3,2,1,0:T(8,128)(2,1)S(1)}, u32[]{:S(2)}, u32[]{:S(2)}) %collective-permute-start.5) | collective-permute-done | bytes 458784 | tf_op jit(solution)/shard_map/ppermute | solution.py:16
  42.1 0.0 copy-start.5
  42.1 2.0 %pack_edges.1 = (bf16[11,32,128]{2,1,0:T(8,128)(2,1)S(1)}, bf16[11,32,128]{2,1,0:T(8,128)(2,1)S(1)}) custom-call(bf16[14,4,32,128]{3,2,1,0:T(8,128)(2,1)S(1)} %collective-permute-done.4.a2, bf16[14,4,32,128]{3,2,1,0:T(8,128)(2,1)S(1)} %collective-permute-done.5.b2, f32[22,32,128]{2,1,0:T(8,128)S(1)} %pack_mid.1.tile_ref), custom_call_target="tpu_custom_call" | custom-call | bytes 2097152 | tf_op jit(solution)/shard_map/pack_edges/pallas_call | solution.py:116
  44.1 0.0 copy-done.5
  44.1 4.9 %collective-permute-start.6 = (bf16[11,32,128]{2,1,0:T(8,128)(2,1)S(1)}, bf16[11,32,128]{2,1,0:T(8,128)(2,1)S(1)}, u32[]{:S(2)}, u32[]{:S(2)}) collective-permute-start(bf16[11,32,128]{2,1,0:T(8,128)(2,1)S(1)} %get-tuple-element.24), channel_id=1, source_target_pairs={{0,1},{1,2},{2,3},{4,5},{5,6},{6,7},{8,9},{9,10},{10,11},{12,13},{... | collective-permute-start | bytes 270344 | tf_op jit(solution)/shard_map/ppermute | solution.py:15
  49.0 1.9 %collective-permute-start.7 = (bf16[11,32,128]{2,1,0:T(8,128)(2,1)S(1)}, bf16[11,32,128]{2,1,0:T(8,128)(2,1)S(1)}, u32[]{:S(2)}, u32[]{:S(2)}) collective-permute-start(bf16[11,32,128]{2,1,0:T(8,128)(2,1)S(1)} %get-tuple-element.25), channel_id=1, source_target_pairs={{1,0},{2,1},{3,2},{5,4},{6,5},{7,6},{9,8},{10,9},{11,10},{13,12},{... | collective-permute-start | bytes 270344 | tf_op jit(solution)/shard_map/ppermute | solution.py:16
  50.9 0.0 collective-permute-done.6.rl_in
  50.9 0.0 copy-start.13
  50.9 3.9 %collective-permute-done.7.rr_in = bf16[11,32,128]{2,1,0:T(8,128)(2,1)S(1)} collective-permute-done((bf16[11,32,128]{2,1,0:T(8,128)(2,1)S(1)}, bf16[11,32,128]{2,1,0:T(8,128)(2,1)S(1)}, u32[]{:S(2)}, u32[]{:S(2)}) %collective-permute-start.7) | collective-permute-done | bytes 90144 | tf_op jit(solution)/shard_map/ppermute | solution.py:16
  54.8 0.0 copy-done.4
  54.8 0.0 copy-done.13
  54.8 0.0 copy-start.14
  54.8 0.6 copy-done.14
  55.5 13.2 %first_convs.1 = (bf16[10,14,32,128]{3,2,1,0:T(8,128)(2,1)}, bf16[10,128,128]{2,1,0:T(8,128)(2,1)}, bf16[4,8,32,128]{3,2,1,0:T(8,128)(2,1)}, f32[4,64,128]{2,1,0...) custom-call(bf16[7,8,32,128]{3,2,1,0:T(8,128)(2,1)} %copy-done.1, ...), custom_call_target="tpu_custom_call" | custom-call | flops 8589934592 | bytes 8388608 | tf_op jit(solution)/shard_map/first_convs/pallas_call | solution.py:313
  68.7 4.3 %all-to-all-start = ((f32[16,1,128]{2,1,0:T(1,128)}), f32[16,1,128]{2,1,0:T(1,128)S(1)}, u32[]{:S(2)}, u32[]{:S(2)}) async-start(f32[16,1,128]{2,1,0:T(1,128)} %get-tuple-element.33), calls=%async_computation | async-start | bytes 16384 | tf_op jit(solution)/shard_map/all_to_all | solution.py:518
  73.0 0.6 stack.15.place
  73.6 4.9 %all-to-all-done = f32[16,1,128]{2,1,0:T(1,128)S(1)} async-done(((f32[16,1,128]{2,1,0:T(1,128)}), f32[16,1,128]{2,1,0:T(1,128)S(1)}, u32[]{:S(2)}, u32[]{:S(2)}) %all-to-all-start) | async-done | bytes 8224 | tf_op jit(solution)/shard_map/all_to_all | solution.py:518
  78.5 0.0 copy-start.12
  78.5 0.6 broadcast_in_dim.9
  79.1 20.2 %all-to-all-start.1 = ((f32[32,1,128]{2,1,0:T(1,128)}), f32[32,1,128]{2,1,0:T(1,128)S(1)}, u32[]{:S(2)}, u32[]{:S(2)}) async-start(f32[32,1,128]{2,1,0:T(1,128)} %broadcast_in_dim.9), calls=%async_computation.1 | async-start | bytes 32768 | tf_op jit(solution)/shard_map/all_to_all | solution.py:522
  99.3 0.0 copy-done.12
  99.3 12.2 %second_convs.1.result = f32[4,8,32,128]{3,2,1,0:T(8,128)} custom-call(s32[6]{0:T(128)} %stack.15.place, bf16[10,14,32,128]{3,2,1,0:T(8,128)(2,1)} %get-tuple-element.27.hid_in, bf16[10,128,128]{2,1,0:T(8,128)(2,1)} %get-tuple-element.28.hid_h_in, bf16[4,8,32,128]{3,2,1,0:T(8,128)(2,1)} %get-tuple-element.29.own_in, ...), custom_call_target="tpu_custom_call" | custom-call | flops 8589934592 | bytes 4194304 | tf_op jit(solution)/shard_map/second_convs/pallas_call | solution.py:412
  111.5 1.3 %all-to-all-done.1.parts = f32[32,1,128]{2,1,0:T(1,128)S(1)} async-done(((f32[32,1,128]{2,1,0:T(1,128)}), f32[32,1,128]{2,1,0:T(1,128)S(1)}, u32[]{:S(2)}, u32[]{:S(2)}) %all-to-all-start.1) | async-done | bytes 16416 | tf_op jit(solution)/shard_map/all_to_all | solution.py:522
  112.8 0.0 copy-start.11
  112.8 0.6 copy-done.11
  113.4 2.7 %finish.1 = (f32[32,4,8,128]{3,2,1,0:T(8,128)}, f32[1]{0:T(128)}) custom-call(f32[4,8,32,128]{3,2,1,0:T(8,128)} %second_convs.1.result, f32[32,1,128]{2,1,0:T(1,128)} %copy-done.11), custom_call_target="tpu_custom_call" | custom-call | tf_op jit(solution)/shard_map/finish/pallas_call | solution.py:474
  (7 shorter events, 0.2 us)
Async XLA Ops:
  0.6 1.1 copy-start.10
  2.0 29.3 %copy-start = (bf16[8,8,32,128]{3,2,1,0:T(8,128)(2,1)}, bf16[8,8,32,128]{3,2,1,0:T(8,128)(2,1)S(1)}, u32[]{:S(2)}) copy-start(bf16[8,8,32,128]{3,2,1,0:T(8,128)(2,1)S(1)} %pad_maximum_fusion.mine_ref.mine) | copy-start | bytes 1572868
  2.0 11.6 %copy-start.8 = (bf16[27,32,32]{2,1,0:T(8,128)(2,1)S(1)}, bf16[27,32,32]{2,1,0:T(8,128)(2,1)}, u32[]{:S(2)}) copy-start(bf16[27,32,32]{2,1,0:T(8,128)(2,1)} %k1_ref.1) | copy-start | bytes 165892
  2.0 11.6 %copy-start.9 = (bf16[27,32,32]{2,1,0:T(8,128)(2,1)S(1)}, bf16[27,32,32]{2,1,0:T(8,128)(2,1)}, u32[]{:S(2)}) copy-start(bf16[27,32,32]{2,1,0:T(8,128)(2,1)} %k2_ref.1) | copy-start | bytes 165892
  2.0 22.8 %collective-permute-start = (bf16[7,8,32,128]{3,2,1,0:T(8,128)(2,1)S(1)}, bf16[7,8,32,128]{3,2,1,0:T(8,128)(2,1)S(1)}, u32[]{:S(2)}, u32[]{:S(2)}) collective-permute-start(bf16[7,8,32,128]{3,2,1,0:T(8,128)(2,1)S(1)} %slice.24), channel_id=1, source_target_pairs={{0,16},{16,32},{32,48},{48,64},{64,80},{80,96},{96,112},{112,128},... | collective-permute-start | bytes 1376264 | tf_op jit(solution)/shard_map/ppermute | solution.py:15
  7.7 17.1 %collective-permute-start.1 = (bf16[7,8,32,128]{3,2,1,0:T(8,128)(2,1)S(1)}, bf16[7,8,32,128]{3,2,1,0:T(8,128)(2,1)S(1)}, u32[]{:S(2)}, u32[]{:S(2)}) collective-permute-start(bf16[7,8,32,128]{3,2,1,0:T(8,128)(2,1)S(1)} %pad_maximum_fusion.1), channel_id=1, source_target_pairs={{16,0},{32,16},{48,32},{64,48},{80,64},{96,80},{112,96},{128,112},... | collective-permute-start | bytes 1376264 | tf_op jit(solution)/shard_map/ppermute | solution.py:16
  9.1 7.8 %collective-permute-start.2 = (bf16[8,4,32,128]{3,2,1,0:T(8,128)(2,1)S(1)}, bf16[8,4,32,128]{3,2,1,0:T(8,128)(2,1)S(1)}, u32[]{:S(2)}, u32[]{:S(2)}) collective-permute-start(bf16[8,4,32,128]{3,2,1,0:T(8,128)(2,1)S(1)} %get-tuple-element.35), channel_id=1, source_target_pairs={{0,4},{4,8},{8,12},{1,5},{5,9},{9,13},{2,6},{6,10},{10,14},{3,7},{... | collective-permute-start | bytes 786440 | tf_op jit(solution)/shard_map/ppermute | solution.py:15
  12.3 8.5 %collective-permute-start.3 = (bf16[8,4,32,128]{3,2,1,0:T(8,128)(2,1)S(1)}, bf16[8,4,32,128]{3,2,1,0:T(8,128)(2,1)S(1)}, u32[]{:S(2)}, u32[]{:S(2)}) collective-permute-start(bf16[8,4,32,128]{3,2,1,0:T(8,128)(2,1)S(1)} %get-tuple-element.34), channel_id=1, source_target_pairs={{4,0},{8,4},{12,8},{5,1},{9,5},{13,9},{6,2},{10,6},{14,10},{7,3},{... | collective-permute-start | bytes 786440 | tf_op jit(solution)/shard_map/ppermute | solution.py:16
  14.6 0.9 copy-start.3
  16.9 16.4 %copy-start.6 = (bf16[8,4,32,128]{3,2,1,0:T(8,128)(2,1)}, bf16[8,4,32,128]{3,2,1,0:T(8,128)(2,1)S(1)}, u32[]{:S(2)}) copy-start(bf16[8,4,32,128]{3,2,1,0:T(8,128)(2,1)S(1)} %collective-permute-done.2.a1) | copy-start | bytes 786436
  20.8 12.6 %copy-start.7 = (bf16[8,4,32,128]{3,2,1,0:T(8,128)(2,1)}, bf16[8,4,32,128]{3,2,1,0:T(8,128)(2,1)S(1)}, u32[]{:S(2)}) copy-start(bf16[8,4,32,128]{3,2,1,0:T(8,128)(2,1)S(1)} %collective-permute-done.3.b1) | copy-start | bytes 786436
  24.9 8.5 %copy-start.1 = (bf16[7,8,32,128]{3,2,1,0:T(8,128)(2,1)}, bf16[7,8,32,128]{3,2,1,0:T(8,128)(2,1)S(1)}, u32[]{:S(2)}) copy-start(bf16[7,8,32,128]{3,2,1,0:T(8,128)(2,1)S(1)} %collective-permute-done.prev_ref.prev) | copy-start | bytes 1376260
  24.9 8.5 %copy-start.2 = (bf16[7,8,32,128]{3,2,1,0:T(8,128)(2,1)}, bf16[7,8,32,128]{3,2,1,0:T(8,128)(2,1)S(1)}, u32[]{:S(2)}) copy-start(bf16[7,8,32,128]{3,2,1,0:T(8,128)(2,1)S(1)} %collective-permute-done.1.next_ref.following) | copy-start | bytes 1376260
  24.9 13.2 %collective-permute-start.4 = (bf16[14,4,32,128]{3,2,1,0:T(8,128)(2,1)S(1)}, bf16[14,4,32,128]{3,2,1,0:T(8,128)(2,1)S(1)}, u32[]{:S(2)}, u32[]{:S(2)}) collective-permute-start(bf16[14,4,32,128]{3,2,1,0:T(8,128)(2,1)S(1)} %get-tuple-element.22), channel_id=1, source_target_pairs={{0,4},{4,8},{8,12},{1,5},{5,9},{9,13},{2,6},{6,10},{10,14},{3,7},{... | collective-permute-start | bytes 1376264 | tf_op jit(solution)/shard_map/ppermute | solution.py:15
  30.0 12.1 %collective-permute-start.5 = (bf16[14,4,32,128]{3,2,1,0:T(8,128)(2,1)S(1)}, bf16[14,4,32,128]{3,2,1,0:T(8,128)(2,1)S(1)}, u32[]{:S(2)}, u32[]{:S(2)}) collective-permute-start(bf16[14,4,32,128]{3,2,1,0:T(8,128)(2,1)S(1)} %get-tuple-element.23), channel_id=1, source_target_pairs={{4,0},{8,4},{12,8},{5,1},{9,5},{13,9},{6,2},{10,6},{14,10},{7,3},{... | collective-permute-start | bytes 1376264 | tf_op jit(solution)/shard_map/ppermute | solution.py:16
  38.2 16.6 %copy-start.4 = (bf16[14,4,32,128]{3,2,1,0:T(8,128)(2,1)}, bf16[14,4,32,128]{3,2,1,0:T(8,128)(2,1)S(1)}, u32[]{:S(2)}) copy-start(bf16[14,4,32,128]{3,2,1,0:T(8,128)(2,1)S(1)} %collective-permute-done.4.a2) | copy-start | bytes 1376260
  42.1 2.0 %copy-start.5 = (bf16[14,4,32,128]{3,2,1,0:T(8,128)(2,1)}, bf16[14,4,32,128]{3,2,1,0:T(8,128)(2,1)S(1)}, u32[]{:S(2)}) copy-start(bf16[14,4,32,128]{3,2,1,0:T(8,128)(2,1)S(1)} %collective-permute-done.5.b2) | copy-start | bytes 1376260
  44.1 6.8 %collective-permute-start.6 = (bf16[11,32,128]{2,1,0:T(8,128)(2,1)S(1)}, bf16[11,32,128]{2,1,0:T(8,128)(2,1)S(1)}, u32[]{:S(2)}, u32[]{:S(2)}) collective-permute-start(bf16[11,32,128]{2,1,0:T(8,128)(2,1)S(1)} %get-tuple-element.24), channel_id=1, source_target_pairs={{0,1},{1,2},{2,3},{4,5},{5,6},{6,7},{8,9},{9,10},{10,11},{12,13},{... | collective-permute-start | bytes 270344 | tf_op jit(solution)/shard_map/ppermute | solution.py:15
  49.0 5.8 %collective-permute-start.7 = (bf16[11,32,128]{2,1,0:T(8,128)(2,1)S(1)}, bf16[11,32,128]{2,1,0:T(8,128)(2,1)S(1)}, u32[]{:S(2)}, u32[]{:S(2)}) collective-permute-start(bf16[11,32,128]{2,1,0:T(8,128)(2,1)S(1)} %get-tuple-element.25), channel_id=1, source_target_pairs={{1,0},{2,1},{3,2},{5,4},{6,5},{7,6},{9,8},{10,9},{11,10},{13,12},{... | collective-permute-start | bytes 270344 | tf_op jit(solution)/shard_map/ppermute | solution.py:16
  50.9 3.9 %copy-start.13 = (bf16[11,32,128]{2,1,0:T(8,128)(2,1)}, bf16[11,32,128]{2,1,0:T(8,128)(2,1)S(1)}, u32[]{:S(2)}) copy-start(bf16[11,32,128]{2,1,0:T(8,128)(2,1)S(1)} %collective-permute-done.6.rl_in) | copy-start | bytes 270340
  54.8 0.6 copy-start.14
  68.7 9.8 %all-to-all-start = ((f32[16,1,128]{2,1,0:T(1,128)}), f32[16,1,128]{2,1,0:T(1,128)S(1)}, u32[]{:S(2)}, u32[]{:S(2)}) async-start(f32[16,1,128]{2,1,0:T(1,128)} %get-tuple-element.33), calls=%async_computation | async-start | bytes 16384 | tf_op jit(solution)/shard_map/all_to_all | solution.py:518
  78.5 20.9 %copy-start.12 = (f32[128]{0:T(128)}, f32[128]{0:T(128)S(1)}, u32[]{:S(2)}) copy-start(f32[128]{0:T(128)S(1)} %reduce_sum.9) | copy-start | bytes 1540
  79.1 33.7 %all-to-all-start.1 = ((f32[32,1,128]{2,1,0:T(1,128)}), f32[32,1,128]{2,1,0:T(1,128)S(1)}, u32[]{:S(2)}, u32[]{:S(2)}) async-start(f32[32,1,128]{2,1,0:T(1,128)} %broadcast_in_dim.9), calls=%async_computation.1 | async-start | bytes 32768 | tf_op jit(solution)/shard_map/all_to_all | solution.py:522
  112.8 0.6 copy-start.11

commit v5 on v4

--- a/solution.py
+++ b/solution.py
@@ -100,7 +100,7 @@
         full[at] = gather_edges(tile_ref[at], OUTER, load, lane)
         return carry
 
-    lax.fori_loop(0, 14, received, 0)
+    lax.fori_loop(0, 14, received, 0, unroll=True)
 
     def group(g, carry):
         one, two = full[2 * g], full[2 * g + 1]
@@ -108,7 +108,7 @@
         left_ref[g] = jnp.where(low, roll(two, -4), one).astype(jnp.bfloat16)
         return carry
 
-    lax.fori_loop(0, left_ref.shape[0], group, 0)
+    lax.fori_loop(0, left_ref.shape[0], group, 0, unroll=True)
 
 
 def pack_edges(a2, b2, tiles):
@@ -215,7 +215,7 @@
         edge[2 * g + 1] = jnp.where(low, roll(rl, -4), roll(rr, 4))
         return carry
 
-    lax.fori_loop(0, rl_ref.shape[0], unpack, 0)
+    lax.fori_loop(0, rl_ref.shape[0], unpack, 0, unroll=True)
 
     def t_layer(t):
         return t + 2 + 4 * lax.shift_right_logical(t, 2)
@@ -229,7 +229,7 @@
             t_h[t, q * CH : (q + 1) * CH] = roll(tile, shift).astype(jnp.bfloat16)
         return carry
 
-    lax.fori_loop(0, 12, t_halo, 0)
+    lax.fori_loop(0, 12, t_halo, 0, unroll=True)
 
     def slope_halo(m, row):
         tile = edge[s_layer(m)]
@@ -243,7 +243,7 @@
     def field_rows(t, r):
         return f_ref[t_layer(t), pl.ds(r, 4)].reshape(4 * CH, LANES)
 
-    lax.fori_loop(0, 6, keep_slopes, 0)
+    lax.fori_loop(0, 6, keep_slopes, 0, unroll=True)
 
     def stage_hidden(m, carry):
         def put(p, v):
@@ -259,7 +259,7 @@
     for start, end, arrived in ((0, 2, 3), (2, 6, 6), (6, 10, 9)):
         for copy in copies[arrived : arrived + 3]:
             copy.wait()
-        lax.fori_loop(start, end, stage_hidden, 0)
+        lax.fori_loop(start, end, stage_hidden, 0, unroll=True)
     early = [
         (hid, hid_out), (hid_h, hid_h_out), (slope_h, slope_h_out),
         (f_ref.at[6:10, 3:13], slope_out.at[0:4]), (f_ref.at[14:16, 3:13], slope_out.at[4:6]),
@@ -287,7 +287,7 @@
         )
         return carry
 
-    lax.fori_loop(0, 4, stage_own, 0)
+    lax.fori_loop(0, 4, stage_own, 0, unroll=True)
     for copy in writes[5:]:
         copy.start()
     total = jnp.sum(sum_acc[...], axis=0, keepdims=True)
@@ -372,7 +372,7 @@
         image_layer(m, x_in, range(6), lambda v: v)
         return carry
 
-    lax.fori_loop(0, 4, stage_ends, 0)
+    lax.fori_loop(0, 4, stage_ends, 0, unroll=True)
 
     for copy in copies[3:]:
         copy.wait()
@@ -383,7 +383,7 @@
         image_layer(m, 1.0, (0, 5), lambda v: jnp.where(outer, v, own_h[i]))
         return carry
 
-    lax.fori_loop(0, 4, stage_rim, 0)
+    lax.fori_loop(0, 4, stage_rim, 0, unroll=True)
 
     def stage_pulled(m, carry):
         def put(p, v):
@@ -396,7 +396,7 @@
         convolve_layer(w_ref[2], rows_of(img), lambda t: img_h[t], m, range(5), put, put_halo)
         return carry
 
-    lax.fori_loop(0, 6, stage_pulled, 0)
+    lax.fori_loop(0, 6, stage_pulled, 0, unroll=True)
 
     def stage_out(m, carry):
         def put(p, v):
@@ -405,7 +405,7 @@
         convolve_layer(w_ref[3], rows_of(pul), lambda t: pul_h[t], m, range(4), put, None)
         return carry
 
-    lax.fori_loop(0, 4, stage_out, 0)
+    lax.fori_loop(0, 4, stage_out, 0, unroll=True)
 
 
 def second_convs(place, fields, weights, after):
@@ -456,18 +456,13 @@
     )(first_kernel, second_kernel)
 
 
-def finish_kernel(result, parts, out_ref, norm_ref, block, sems):
-    layers = block.shape[0]
-    copies = [pltpu.make_async_copy(result.at[x], block.at[x], sems.at[x]) for x in range(layers)]
-    for copy in copies:
-        copy.start()
+def finish_kernel(result, parts, out_ref, norm_ref):
     total = jnp.sum(jnp.sum(parts[...], axis=0), axis=1, keepdims=True)
     norm = jnp.sqrt(total + 1e-06)
     norm_ref[0] = norm[0, 0]
     scale = jnp.broadcast_to(norm, (8, LANES))
-    for x in range(layers):
-        copies[x].wait()
-        out_ref[:, x] = block[x].transpose(1, 0, 2) / scale
+    for x in range(result.shape[0]):
+        out_ref[:, x] = result[x].transpose(1, 0, 2) / scale
 
 
 def finish(result, parts):
@@ -477,19 +472,11 @@
             jax.ShapeDtypeStruct((CH, 4, 8, LANES), jnp.float32),
             jax.ShapeDtypeStruct((1,), jnp.float32),
         ),
-        in_specs=[
-            pl.BlockSpec(memory_space=pl.ANY),
-            pl.BlockSpec(memory_space=pltpu.VMEM),
-        ],
         out_specs=(
             pl.BlockSpec(memory_space=pltpu.VMEM),
             pl.BlockSpec(memory_space=pltpu.SMEM),
         ),
-        scratch_shapes=[
-            pltpu.VMEM(result.shape, jnp.float32),
-            pltpu.SemaphoreType.DMA((result.shape[0],)),
-        ],
-        compiler_params=pltpu.CompilerParams(vmem_limit_bytes=62 << 20),
+        compiler_params=pltpu.CompilerParams(vmem_limit_bytes=16 << 20),
         name="finish",
     )(result, parts)
 

time: 117 us -> 110 us (0.940)
  Pallas kernels: 33.2 us -> 20.4 us
  waiting for transfers between devices: 28.1 us -> 32.8 us
    pallas_call x1, Pallas kernels: 12.2 us -> 7.38 us  [second_convs(): pl.pallas_call(second_kernel_body, out_shape=jax.ShapeDtypeStruct((4, 8,...]
    pallas_call x1, Pallas kernels: 13.2 us -> 8.48 us  [first_convs(): pl.pallas_call(first_kernel_body, out_shape=(*fields, shape((spread, 1, L...]
    all_to_all x1, waiting for transfers between devices: 1.28 us -> 5.97 us  [on_device(): lax.all_to_all(jnp.broadcast_to(part, (count, 1, LANES)), 'gx', 0, 0, til...]
    pallas_call x1, Pallas kernels: 2.69 us -> 1.01 us  [finish(): pl.pallas_call(finish_kernel, out_shape=(jax.ShapeDtypeStruct((CH, 4, 8,...]
    pallas_call x1, Pallas kernels: 2.04 us -> 0.38 us  [pack_edges(): pl.pallas_call(pack_kernel, out_shape=(out, out), scratch_shapes=[pltpu.V...]
  transfers between devices with their start and end apart: 10 -> 10, of which waited for: 8 -> 8; matrix products, arithmetic and copies ran while one was open for 1% -> 1% of each run, Pallas kernels for 13% -> 10%
where the time goes in v5:
time: 110 us; the launch traced here: 109 us
  starting transfers between devices  49.2 us (45%)
  waiting for transfers between devices  32.8 us (30%)
  Pallas kernels  20.4 us (19%)
  local copies, waits for them, and re-layouts  5.47 us (5%)
    all_to_all x1, starting transfers between devices, on_device(): lax.all_to_all(jnp.broadcast_to(part, (count, 1, LANES)), 'gx', 0, 0, til...  20.4 us
    ppermute x4, starting transfers between devices, shift_pair(): from_prev = lax.ppermute(up, axis, [(i, i + 1) for i in range(ends)])  18.7 us
    ppermute x4, waiting for transfers between devices, shift_pair(): from_next = lax.ppermute(down, axis, [(i + 1, i) for i in range(ends)])  11.6 us
    ppermute x4, waiting for transfers between devices, shift_pair(): from_prev = lax.ppermute(up, axis, [(i, i + 1) for i in range(ends)])  10.4 us
    pallas_call x1, Pallas kernels, first_convs(): pl.pallas_call(first_kernel_body, out_shape=(*fields, shape((spread, 1, L...  8.48 us
    pallas_call x1, Pallas kernels, second_convs(): pl.pallas_call(second_kernel_body, out_shape=jax.ShapeDtypeStruct((4, 8,...  7.38 us
    all_to_all x1, waiting for transfers between devices, on_device(): lax.all_to_all(jnp.broadcast_to(part, (count, 1, LANES)), 'gx', 0, 0, til...  5.97 us
    ppermute x4, starting transfers between devices, shift_pair(): from_next = lax.ppermute(down, axis, [(i + 1, i) for i in range(ends)])  5.8 us
  transfers between devices with their start and end apart: 10, of which 8 were waited for; matrix products, arithmetic and copies ran while one was open for 1% of the time, Pallas kernels for 10%

profile of v5, /device:TPU:1, one launch (start us, length us, event | category | flops | bytes accessed | tf_op | source)
XLA Modules:
  0.0 109.1 jit_solution(15699332729939143636)
XLA Ops:
  0.6 0.0 copy-start.11
  0.6 1.1 %copy.11 = bf16[32,4,8,128]{3,0,2,1:T(8,128)(2,1)S(1)} copy(bf16[32,4,8,128]{3,2,1,0:T(8,128)(2,1)} %param.5) | data formatting | bytes 524288 | tf_op args[1]
  1.8 0.0 copy-done.11
  1.8 0.1 copy.10
  1.9 0.1 pad_maximum_fusion.mine_ref.mine
  2.0 0.0 copy-start
  2.0 0.0 copy-start.9
  2.0 0.0 copy-start.10
  2.0 5.6 %collective-permute-start = (bf16[7,8,32,128]{3,2,1,0:T(8,128)(2,1)S(1)}, bf16[7,8,32,128]{3,2,1,0:T(8,128)(2,1)S(1)}, u32[]{:S(2)}, u32[]{:S(2)}) collective-permute-start(bf16[7,8,32,128]{3,2,1,0:T(8,128)(2,1)S(1)} %slice.24), channel_id=1, source_target_pairs={{0,16},{16,32},{32,48},{48,64},{64,80},{80,96},{96,112},{112,128},... | collective-permute-start | bytes 1376264 | tf_op jit(solution)/shard_map/ppermute | solution.py:15
  7.7 1.3 %collective-permute-start.1 = (bf16[7,8,32,128]{3,2,1,0:T(8,128)(2,1)S(1)}, bf16[7,8,32,128]{3,2,1,0:T(8,128)(2,1)S(1)}, u32[]{:S(2)}, u32[]{:S(2)}) collective-permute-start(bf16[7,8,32,128]{3,2,1,0:T(8,128)(2,1)S(1)} %pad_maximum_fusion.1), channel_id=1, source_target_pairs={{16,0},{32,16},{48,32},{64,48},{80,64},{96,80},{112,96},{128,112},... | collective-permute-start | bytes 1376264 | tf_op jit(solution)/shard_map/ppermute | solution.py:16
  9.1 3.2 %collective-permute-start.2 = (bf16[8,4,32,128]{3,2,1,0:T(8,128)(2,1)S(1)}, bf16[8,4,32,128]{3,2,1,0:T(8,128)(2,1)S(1)}, u32[]{:S(2)}, u32[]{:S(2)}) collective-permute-start(bf16[8,4,32,128]{3,2,1,0:T(8,128)(2,1)S(1)} %get-tuple-element.35), channel_id=1, source_target_pairs={{0,4},{4,8},{8,12},{1,5},{5,9},{9,13},{2,6},{6,10},{10,14},{3,7},{... | collective-permute-start | bytes 786440 | tf_op jit(solution)/shard_map/ppermute | solution.py:15
  12.3 1.3 %collective-permute-start.3 = (bf16[8,4,32,128]{3,2,1,0:T(8,128)(2,1)S(1)}, bf16[8,4,32,128]{3,2,1,0:T(8,128)(2,1)S(1)}, u32[]{:S(2)}, u32[]{:S(2)}) collective-permute-start(bf16[8,4,32,128]{3,2,1,0:T(8,128)(2,1)S(1)} %get-tuple-element.34), channel_id=1, source_target_pairs={{4,0},{8,4},{12,8},{5,1},{9,5},{13,9},{6,2},{10,6},{14,10},{7,3},{... | collective-permute-start | bytes 786440 | tf_op jit(solution)/shard_map/ppermute | solution.py:16
  13.6 0.0 copy-done.9
  13.6 0.0 copy-done.10
  13.6 1.0 pair_matrices.1.w_in
  14.6 0.0 copy-start.3
  14.6 0.8 copy-done.3
  15.5 1.5 %collective-permute-done.2.a1 = bf16[8,4,32,128]{3,2,1,0:T(8,128)(2,1)S(1)} collective-permute-done((bf16[8,4,32,128]{3,2,1,0:T(8,128)(2,1)S(1)}, bf16[8,4,32,128]{3,2,1,0:T(8,128)(2,1)S(1)}, u32[]{:S(2)}, u32[]{:S(2)}) %collective-permute-start.2) | collective-permute-done | bytes 262176 | tf_op jit(solution)/shard_map/ppermute | solution.py:15
  16.9 0.0 copy-start.7
  16.9 3.8 %collective-permute-done.3.b1 = bf16[8,4,32,128]{3,2,1,0:T(8,128)(2,1)S(1)} collective-permute-done((bf16[8,4,32,128]{3,2,1,0:T(8,128)(2,1)S(1)}, bf16[8,4,32,128]{3,2,1,0:T(8,128)(2,1)S(1)}, u32[]{:S(2)}, u32[]{:S(2)}) %collective-permute-start.3) | collective-permute-done | bytes 262176 | tf_op jit(solution)/shard_map/ppermute | solution.py:16
  20.8 0.0 copy-start.8
  20.8 4.1 %collective-permute-done.prev_ref.prev = bf16[7,8,32,128]{3,2,1,0:T(8,128)(2,1)S(1)} collective-permute-done((bf16[7,8,32,128]{3,2,1,0:T(8,128)(2,1)S(1)}, bf16[7,8,32,128]{3,2,1,0:T(8,128)(2,1)S(1)}, u32[]{:S(2)}, u32[]{:S(2)}) %collective-permute-start) | collective-permute-done | bytes 458784 | tf_op jit(solution)/shard_map/ppermute | solution.py:15
  24.9 0.0 copy-start.1
  24.9 0.0 collective-permute-done.1.next_ref.following
  24.9 0.0 copy-start.2
  24.9 0.1 edge_rows.1
  24.9 5.0 %collective-permute-start.4 = (bf16[14,4,32,128]{3,2,1,0:T(8,128)(2,1)S(1)}, bf16[14,4,32,128]{3,2,1,0:T(8,128)(2,1)S(1)}, u32[]{:S(2)}, u32[]{:S(2)}) collective-permute-start(bf16[14,4,32,128]{3,2,1,0:T(8,128)(2,1)S(1)} %get-tuple-element.22), channel_id=1, source_target_pairs={{0,4},{4,8},{8,12},{1,5},{5,9},{9,13},{2,6},{6,10},{10,14},{3,7},{... | collective-permute-start | bytes 1376264 | tf_op jit(solution)/shard_map/ppermute | solution.py:15
  30.0 1.3 %collective-permute-start.5 = (bf16[14,4,32,128]{3,2,1,0:T(8,128)(2,1)S(1)}, bf16[14,4,32,128]{3,2,1,0:T(8,128)(2,1)S(1)}, u32[]{:S(2)}, u32[]{:S(2)}) collective-permute-start(bf16[14,4,32,128]{3,2,1,0:T(8,128)(2,1)S(1)} %get-tuple-element.23), channel_id=1, source_target_pairs={{4,0},{8,4},{12,8},{5,1},{9,5},{13,9},{6,2},{10,6},{14,10},{7,3},{... | collective-permute-start | bytes 1376264 | tf_op jit(solution)/shard_map/ppermute | solution.py:16
  31.3 0.0 copy-done
  31.3 2.1 %pack_mid.1.tile_ref = f32[22,32,128]{2,1,0:T(8,128)S(1)} custom-call(bf16[7,8,32,128]{3,2,1,0:T(8,128)(2,1)S(1)} %collective-permute-done.prev_ref.prev, bf16[8,8,32,128]{3,2,1,0:T(8,128)(2,1)S(1)} %pad_maximum_fusion.mine_ref.mine, bf16[7,8,32,128]{3,2,1,0:T(8,128)(2,1)S(1)} %collective-permute-done.1.next_ref.following, ...), custom_call_target="tpu_custom_call" | custom-call | bytes 2097152 | tf_op jit(solution)/shard_map/pack_mid/pallas_call | solution.py:83
  33.4 0.0 copy-done.7
  33.4 0.0 copy-done.8
  33.4 0.0 copy-done.1
  33.4 0.0 copy-done.2
  33.4 4.8 %collective-permute-done.4.a2 = bf16[14,4,32,128]{3,2,1,0:T(8,128)(2,1)S(1)} collective-permute-done((bf16[14,4,32,128]{3,2,1,0:T(8,128)(2,1)S(1)}, bf16[14,4,32,128]{3,2,1,0:T(8,128)(2,1)S(1)}, u32[]{:S(2)}, u32[]{:S(2)}) %collective-permute-start.4) | collective-permute-done | bytes 458784 | tf_op jit(solution)/shard_map/ppermute | solution.py:15
  38.2 0.0 copy-start.5
  38.2 3.9 %collective-permute-done.5.b2 = bf16[14,4,32,128]{3,2,1,0:T(8,128)(2,1)S(1)} collective-permute-done((bf16[14,4,32,128]{3,2,1,0:T(8,128)(2,1)S(1)}, bf16[14,4,32,128]{3,2,1,0:T(8,128)(2,1)S(1)}, u32[]{:S(2)}, u32[]{:S(2)}) %collective-permute-start.5) | collective-permute-done | bytes 458784 | tf_op jit(solution)/shard_map/ppermute | solution.py:16
  42.1 0.0 copy-start.6
  42.1 0.4 pack_edges.1
  42.4 0.4 copy-done.6
  42.8 4.8 %collective-permute-start.6 = (bf16[11,32,128]{2,1,0:T(8,128)(2,1)S(1)}, bf16[11,32,128]{2,1,0:T(8,128)(2,1)S(1)}, u32[]{:S(2)}, u32[]{:S(2)}) collective-permute-start(bf16[11,32,128]{2,1,0:T(8,128)(2,1)S(1)} %get-tuple-element.24), channel_id=1, source_target_pairs={{0,1},{1,2},{2,3},{4,5},{5,6},{6,7},{8,9},{9,10},{10,11},{12,13},{... | collective-permute-start | bytes 270344 | tf_op jit(solution)/shard_map/ppermute | solution.py:15
  47.7 1.9 %collective-permute-start.7 = (bf16[11,32,128]{2,1,0:T(8,128)(2,1)S(1)}, bf16[11,32,128]{2,1,0:T(8,128)(2,1)S(1)}, u32[]{:S(2)}, u32[]{:S(2)}) collective-permute-start(bf16[11,32,128]{2,1,0:T(8,128)(2,1)S(1)} %get-tuple-element.25), channel_id=1, source_target_pairs={{1,0},{2,1},{3,2},{5,4},{6,5},{7,6},{9,8},{10,9},{11,10},{13,12},{... | collective-permute-start | bytes 270344 | tf_op jit(solution)/shard_map/ppermute | solution.py:16
  49.6 0.0 collective-permute-done.6.rl_in
  49.6 0.0 copy-start.13
  49.6 3.9 %collective-permute-done.7.rr_in = bf16[11,32,128]{2,1,0:T(8,128)(2,1)S(1)} collective-permute-done((bf16[11,32,128]{2,1,0:T(8,128)(2,1)S(1)}, bf16[11,32,128]{2,1,0:T(8,128)(2,1)S(1)}, u32[]{:S(2)}, u32[]{:S(2)}) %collective-permute-start.7) | collective-permute-done | bytes 90144 | tf_op jit(solution)/shard_map/ppermute | solution.py:16
  53.5 0.0 copy-done.5
  53.5 0.0 copy-done.13
  53.5 0.0 copy-start.14
  53.5 0.6 copy-done.14
  54.2 8.5 %first_convs.1 = (bf16[10,14,32,128]{3,2,1,0:T(8,128)(2,1)}, bf16[10,128,128]{2,1,0:T(8,128)(2,1)}, bf16[4,8,32,128]{3,2,1,0:T(8,128)(2,1)}, f32[4,64,128]{2,1,0...) custom-call(bf16[7,8,32,128]{3,2,1,0:T(8,128)(2,1)} %copy-done.1, ...), custom_call_target="tpu_custom_call" | custom-call | flops 8589934592 | bytes 8388608 | tf_op jit(solution)/shard_map/first_convs/pallas_call | solution.py:313
  62.7 4.3 %all-to-all-start = ((f32[16,1,128]{2,1,0:T(1,128)}), f32[16,1,128]{2,1,0:T(1,128)S(1)}, u32[]{:S(2)}, u32[]{:S(2)}) async-start(f32[16,1,128]{2,1,0:T(1,128)} %get-tuple-element.33), calls=%async_computation | async-start | bytes 16384 | tf_op jit(solution)/shard_map/all_to_all | solution.py:505
  67.0 0.6 stack.15.place
  67.6 4.9 %all-to-all-done = f32[16,1,128]{2,1,0:T(1,128)S(1)} async-done(((f32[16,1,128]{2,1,0:T(1,128)}), f32[16,1,128]{2,1,0:T(1,128)S(1)}, u32[]{:S(2)}, u32[]{:S(2)}) %all-to-all-start) | async-done | bytes 8224 | tf_op jit(solution)/shard_map/all_to_all | solution.py:505
  72.5 0.0 copy-start.12
  72.5 0.6 broadcast_in_dim.9
  73.1 20.4 %all-to-all-start.1 = ((f32[32,1,128]{2,1,0:T(1,128)}), f32[32,1,128]{2,1,0:T(1,128)S(1)}, u32[]{:S(2)}, u32[]{:S(2)}) async-start(f32[32,1,128]{2,1,0:T(1,128)} %broadcast_in_dim.9), calls=%async_computation.1 | async-start | bytes 32768 | tf_op jit(solution)/shard_map/all_to_all | solution.py:509
  93.5 0.0 copy-done.12
  93.5 7.4 %second_convs.1.result = f32[4,8,32,128]{3,2,1,0:T(8,128)} custom-call(s32[6]{0:T(128)} %stack.15.place, bf16[10,14,32,128]{3,2,1,0:T(8,128)(2,1)} %get-tuple-element.27.hid_in, bf16[10,128,128]{2,1,0:T(8,128)(2,1)} %get-tuple-element.28.hid_h_in, bf16[4,8,32,128]{3,2,1,0:T(8,128)(2,1)} %get-tuple-element.29.own_in, ...), custom_call_target="tpu_custom_call" | custom-call | flops 8589934592 | bytes 4194304 | tf_op jit(solution)/shard_map/second_convs/pallas_call | solution.py:412
  100.9 6.0 %all-to-all-done.1.parts = f32[32,1,128]{2,1,0:T(1,128)S(1)} async-done(((f32[32,1,128]{2,1,0:T(1,128)}), f32[32,1,128]{2,1,0:T(1,128)S(1)}, u32[]{:S(2)}, u32[]{:S(2)}) %all-to-all-start.1) | async-done | bytes 16416 | tf_op jit(solution)/shard_map/all_to_all | solution.py:509
  106.9 0.0 copy-start.4
  106.9 1.0 copy-done.4
  107.9 1.0 finish.1
  (7 shorter events, 0.2 us)
Async XLA Ops:
  0.6 1.1 %copy-start.11 = (bf16[32,4,8,128]{3,2,1,0:T(8,128)(2,1)S(1)}, bf16[32,4,8,128]{3,2,1,0:T(8,128)(2,1)}, u32[]{:S(2)}) copy-start(bf16[32,4,8,128]{3,2,1,0:T(8,128)(2,1)} %param.4) | copy-start | bytes 786436
  2.0 29.3 %copy-start = (bf16[8,8,32,128]{3,2,1,0:T(8,128)(2,1)}, bf16[8,8,32,128]{3,2,1,0:T(8,128)(2,1)S(1)}, u32[]{:S(2)}) copy-start(bf16[8,8,32,128]{3,2,1,0:T(8,128)(2,1)S(1)} %pad_maximum_fusion.mine_ref.mine) | copy-start | bytes 1572868
  2.0 11.6 %copy-start.9 = (bf16[27,32,32]{2,1,0:T(8,128)(2,1)S(1)}, bf16[27,32,32]{2,1,0:T(8,128)(2,1)}, u32[]{:S(2)}) copy-start(bf16[27,32,32]{2,1,0:T(8,128)(2,1)} %k1_ref.1) | copy-start | bytes 165892
  2.0 11.6 %copy-start.10 = (bf16[27,32,32]{2,1,0:T(8,128)(2,1)S(1)}, bf16[27,32,32]{2,1,0:T(8,128)(2,1)}, u32[]{:S(2)}) copy-start(bf16[27,32,32]{2,1,0:T(8,128)(2,1)} %k2_ref.1) | copy-start | bytes 165892
  2.0 22.8 %collective-permute-start = (bf16[7,8,32,128]{3,2,1,0:T(8,128)(2,1)S(1)}, bf16[7,8,32,128]{3,2,1,0:T(8,128)(2,1)S(1)}, u32[]{:S(2)}, u32[]{:S(2)}) collective-permute-start(bf16[7,8,32,128]{3,2,1,0:T(8,128)(2,1)S(1)} %slice.24), channel_id=1, source_target_pairs={{0,16},{16,32},{32,48},{48,64},{64,80},{80,96},{96,112},{112,128},... | collective-permute-start | bytes 1376264 | tf_op jit(solution)/shard_map/ppermute | solution.py:15
  7.7 17.1 %collective-permute-start.1 = (bf16[7,8,32,128]{3,2,1,0:T(8,128)(2,1)S(1)}, bf16[7,8,32,128]{3,2,1,0:T(8,128)(2,1)S(1)}, u32[]{:S(2)}, u32[]{:S(2)}) collective-permute-start(bf16[7,8,32,128]{3,2,1,0:T(8,128)(2,1)S(1)} %pad_maximum_fusion.1), channel_id=1, source_target_pairs={{16,0},{32,16},{48,32},{64,48},{80,64},{96,80},{112,96},{128,112},... | collective-permute-start | bytes 1376264 | tf_op jit(solution)/shard_map/ppermute | solution.py:16
  9.1 7.8 %collective-permute-start.2 = (bf16[8,4,32,128]{3,2,1,0:T(8,128)(2,1)S(1)}, bf16[8,4,32,128]{3,2,1,0:T(8,128)(2,1)S(1)}, u32[]{:S(2)}, u32[]{:S(2)}) collective-permute-start(bf16[8,4,32,128]{3,2,1,0:T(8,128)(2,1)S(1)} %get-tuple-element.35), channel_id=1, source_target_pairs={{0,4},{4,8},{8,12},{1,5},{5,9},{9,13},{2,6},{6,10},{10,14},{3,7},{... | collective-permute-start | bytes 786440 | tf_op jit(solution)/shard_map/ppermute | solution.py:15
  12.3 8.5 %collective-permute-start.3 = (bf16[8,4,32,128]{3,2,1,0:T(8,128)(2,1)S(1)}, bf16[8,4,32,128]{3,2,1,0:T(8,128)(2,1)S(1)}, u32[]{:S(2)}, u32[]{:S(2)}) collective-permute-start(bf16[8,4,32,128]{3,2,1,0:T(8,128)(2,1)S(1)} %get-tuple-element.34), channel_id=1, source_target_pairs={{4,0},{8,4},{12,8},{5,1},{9,5},{13,9},{6,2},{10,6},{14,10},{7,3},{... | collective-permute-start | bytes 786440 | tf_op jit(solution)/shard_map/ppermute | solution.py:16
  14.6 0.8 copy-start.3
  16.9 16.4 %copy-start.7 = (bf16[8,4,32,128]{3,2,1,0:T(8,128)(2,1)}, bf16[8,4,32,128]{3,2,1,0:T(8,128)(2,1)S(1)}, u32[]{:S(2)}) copy-start(bf16[8,4,32,128]{3,2,1,0:T(8,128)(2,1)S(1)} %collective-permute-done.2.a1) | copy-start | bytes 786436
  20.8 12.6 %copy-start.8 = (bf16[8,4,32,128]{3,2,1,0:T(8,128)(2,1)}, bf16[8,4,32,128]{3,2,1,0:T(8,128)(2,1)S(1)}, u32[]{:S(2)}) copy-start(bf16[8,4,32,128]{3,2,1,0:T(8,128)(2,1)S(1)} %collective-permute-done.3.b1) | copy-start | bytes 786436
  24.9 8.5 %copy-start.1 = (bf16[7,8,32,128]{3,2,1,0:T(8,128)(2,1)}, bf16[7,8,32,128]{3,2,1,0:T(8,128)(2,1)S(1)}, u32[]{:S(2)}) copy-start(bf16[7,8,32,128]{3,2,1,0:T(8,128)(2,1)S(1)} %collective-permute-done.prev_ref.prev) | copy-start | bytes 1376260
  24.9 8.5 %copy-start.2 = (bf16[7,8,32,128]{3,2,1,0:T(8,128)(2,1)}, bf16[7,8,32,128]{3,2,1,0:T(8,128)(2,1)S(1)}, u32[]{:S(2)}) copy-start(bf16[7,8,32,128]{3,2,1,0:T(8,128)(2,1)S(1)} %collective-permute-done.1.next_ref.following) | copy-start | bytes 1376260
  24.9 13.2 %collective-permute-start.4 = (bf16[14,4,32,128]{3,2,1,0:T(8,128)(2,1)S(1)}, bf16[14,4,32,128]{3,2,1,0:T(8,128)(2,1)S(1)}, u32[]{:S(2)}, u32[]{:S(2)}) collective-permute-start(bf16[14,4,32,128]{3,2,1,0:T(8,128)(2,1)S(1)} %get-tuple-element.22), channel_id=1, source_target_pairs={{0,4},{4,8},{8,12},{1,5},{5,9},{9,13},{2,6},{6,10},{10,14},{3,7},{... | collective-permute-start | bytes 1376264 | tf_op jit(solution)/shard_map/ppermute | solution.py:15
  30.0 12.1 %collective-permute-start.5 = (bf16[14,4,32,128]{3,2,1,0:T(8,128)(2,1)S(1)}, bf16[14,4,32,128]{3,2,1,0:T(8,128)(2,1)S(1)}, u32[]{:S(2)}, u32[]{:S(2)}) collective-permute-start(bf16[14,4,32,128]{3,2,1,0:T(8,128)(2,1)S(1)} %get-tuple-element.23), channel_id=1, source_target_pairs={{4,0},{8,4},{12,8},{5,1},{9,5},{13,9},{6,2},{10,6},{14,10},{7,3},{... | collective-permute-start | bytes 1376264 | tf_op jit(solution)/shard_map/ppermute | solution.py:16
  38.2 15.3 %copy-start.5 = (bf16[14,4,32,128]{3,2,1,0:T(8,128)(2,1)}, bf16[14,4,32,128]{3,2,1,0:T(8,128)(2,1)S(1)}, u32[]{:S(2)}) copy-start(bf16[14,4,32,128]{3,2,1,0:T(8,128)(2,1)S(1)} %collective-permute-done.4.a2) | copy-start | bytes 1376260
  42.1 0.8 copy-start.6
  42.8 6.8 %collective-permute-start.6 = (bf16[11,32,128]{2,1,0:T(8,128)(2,1)S(1)}, bf16[11,32,128]{2,1,0:T(8,128)(2,1)S(1)}, u32[]{:S(2)}, u32[]{:S(2)}) collective-permute-start(bf16[11,32,128]{2,1,0:T(8,128)(2,1)S(1)} %get-tuple-element.24), channel_id=1, source_target_pairs={{0,1},{1,2},{2,3},{4,5},{5,6},{6,7},{8,9},{9,10},{10,11},{12,13},{... | collective-permute-start | bytes 270344 | tf_op jit(solution)/shard_map/ppermute | solution.py:15
  47.7 5.8 %collective-permute-start.7 = (bf16[11,32,128]{2,1,0:T(8,128)(2,1)S(1)}, bf16[11,32,128]{2,1,0:T(8,128)(2,1)S(1)}, u32[]{:S(2)}, u32[]{:S(2)}) collective-permute-start(bf16[11,32,128]{2,1,0:T(8,128)(2,1)S(1)} %get-tuple-element.25), channel_id=1, source_target_pairs={{1,0},{2,1},{3,2},{5,4},{6,5},{7,6},{9,8},{10,9},{11,10},{13,12},{... | collective-permute-start | bytes 270344 | tf_op jit(solution)/shard_map/ppermute | solution.py:16
  49.6 3.9 %copy-start.13 = (bf16[11,32,128]{2,1,0:T(8,128)(2,1)}, bf16[11,32,128]{2,1,0:T(8,128)(2,1)S(1)}, u32[]{:S(2)}) copy-start(bf16[11,32,128]{2,1,0:T(8,128)(2,1)S(1)} %collective-permute-done.6.rl_in) | copy-start | bytes 270340
  53.5 0.6 copy-start.14
  62.7 9.8 %all-to-all-start = ((f32[16,1,128]{2,1,0:T(1,128)}), f32[16,1,128]{2,1,0:T(1,128)S(1)}, u32[]{:S(2)}, u32[]{:S(2)}) async-start(f32[16,1,128]{2,1,0:T(1,128)} %get-tuple-element.33), calls=%async_computation | async-start | bytes 16384 | tf_op jit(solution)/shard_map/all_to_all | solution.py:505
  72.5 21.0 %copy-start.12 = (f32[128]{0:T(128)}, f32[128]{0:T(128)S(1)}, u32[]{:S(2)}) copy-start(f32[128]{0:T(128)S(1)} %reduce_sum.9) | copy-start | bytes 1540
  73.1 33.8 %all-to-all-start.1 = ((f32[32,1,128]{2,1,0:T(1,128)}), f32[32,1,128]{2,1,0:T(1,128)S(1)}, u32[]{:S(2)}, u32[]{:S(2)}) async-start(f32[32,1,128]{2,1,0:T(1,128)} %broadcast_in_dim.9), calls=%async_computation.1 | async-start | bytes 32768 | tf_op jit(solution)/shard_map/all_to_all | solution.py:509
  106.9 1.0 copy-start.4

commit v6 on v5

--- a/solution.py
+++ b/solution.py
@@ -180,10 +180,13 @@
     return lambda t, r: ref[t, pl.ds(r, 4)].reshape(4 * CH, LANES)
 
 
+OUTER_LAYERS = (0, 1, 8, 9)
+
+
 def first_kernel_body(
     prev, mine, following, a1, b1, a2, b2, rl_in, rr_in, w_in,
-    hid_out, hid_h_out, own_out, own_h_out, slope_out, slope_h_out, sum_ref,
-    f_ref, rl_ref, rr_ref, w_ref, edge, t_h, hid, hid_h, own_ref, own_h, slope_h, sum_acc, sems, out_sems,
+    hid_out, hid_h_out, own_out, own_h_out, slope_out, slope_h_out, t_h_out, far_h_out, sum_ref,
+    f_ref, rl_ref, rr_ref, w_ref, edge, t_h, hid, hid_h, own_ref, own_h, slope_h, far_h, sum_acc, sems, out_sems,
 ):
     moves = [
         (rl_in, rl_ref),
@@ -244,6 +247,8 @@
         return f_ref[t_layer(t), pl.ds(r, 4)].reshape(4 * CH, LANES)
 
     lax.fori_loop(0, 6, keep_slopes, 0, unroll=True)
+    for i, m in enumerate(OUTER_LAYERS):
+        far_h[i] = slope_halo(m, 1)
 
     def stage_hidden(m, carry):
         def put(p, v):
@@ -256,17 +261,18 @@
         convolve_layer(w_ref[0], field_rows, lambda t: t_h[t], m, range(7), put, put_halo)
         return carry
 
-    for start, end, arrived in ((0, 2, 3), (2, 6, 6), (6, 10, 9)):
-        for copy in copies[arrived : arrived + 3]:
+    for start, end, first, last in ((2, 6, 3, 9), (6, 8, 9, 12)):
+        for copy in copies[first:last]:
             copy.wait()
         lax.fori_loop(start, end, stage_hidden, 0, unroll=True)
     early = [
-        (hid, hid_out), (hid_h, hid_h_out), (slope_h, slope_h_out),
+        (hid.at[2:8], hid_out.at[2:8]), (hid_h.at[2:8], hid_h_out.at[2:8]),
+        (slope_h, slope_h_out), (t_h, t_h_out), (far_h, far_h_out),
         (f_ref.at[6:10, 3:13], slope_out.at[0:4]), (f_ref.at[14:16, 3:13], slope_out.at[4:6]),
     ]
     late = [(own_ref, own_out), (own_h, own_h_out)]
     writes = [pltpu.make_async_copy(x, y, out_sems.at[i]) for i, (x, y) in enumerate(early + late)]
-    for copy in writes[:5]:
+    for copy in writes[:7]:
         copy.start()
     sum_acc[...] = jnp.zeros_like(sum_acc)
 
@@ -288,7 +294,7 @@
         return carry
 
     lax.fori_loop(0, 4, stage_own, 0, unroll=True)
-    for copy in writes[5:]:
+    for copy in writes[7:]:
         copy.start()
     total = jnp.sum(sum_acc[...], axis=0, keepdims=True)
     for i in range(sum_ref.shape[0]):
@@ -308,13 +314,15 @@
         shape((4, 2 * CH, LANES), jnp.float32),
         shape((6, 10, CH, LANES), jnp.bfloat16),
         shape((6, 2 * CH, LANES), jnp.float32),
+        shape((12, 4 * CH, LANES), jnp.bfloat16),
+        shape((4, 2 * CH, LANES), jnp.float32),
     )
-    keep = [pltpu.VMEM(fields[i].shape, fields[i].dtype) for i in (0, 1, 2, 3, 5)]
+    keep = [pltpu.VMEM(fields[i].shape, fields[i].dtype) for i in (0, 1, 2, 3, 5, 7)]
     return pl.pallas_call(
         first_kernel_body,
         out_shape=(*fields, shape((spread, 1, LANES), jnp.float32)),
         in_specs=[anywhere] * 10,
-        out_specs=(*([anywhere] * 6), local),
+        out_specs=(*([anywhere] * 8), local),
         scratch_shapes=[
             pltpu.VMEM((22, 16, CH, LANES), jnp.bfloat16),
             pltpu.VMEM(rl.shape, rl.dtype),
@@ -325,7 +333,7 @@
             *keep,
             pltpu.VMEM((8, LANES), jnp.float32),
             pltpu.SemaphoreType.DMA((12,)),
-            pltpu.SemaphoreType.DMA((7,)),
+            pltpu.SemaphoreType.DMA((9,)),
         ],
         compiler_params=pltpu.CompilerParams(vmem_limit_bytes=62 << 20),
         cost_estimate=pl.CostEstimate(flops=8 << 30, bytes_accessed=8 << 20, transcendentals=0),
@@ -334,17 +342,44 @@
 
 
 def second_kernel_body(
-    place, hid_in, hid_h_in, own_in, own_h_in, slope_in, slope_h_in, w_in, after, out_ref,
-    w_ref, hid, hid_h, own_h, slope_ref, slope_h, img, img_h, pul, pul_h, sems,
+    place, hid_in, hid_h_in, own_in, own_h_in, slope_in, slope_h_in, t_h_in, far_h_in,
+    prev, following, a2, b2, w_in, after, out_ref,
+    f_ref, w_ref, hid, hid_h, own_h, slope_ref, slope_h, t_h, far_h, img, img_h, pul, pul_h, sems,
 ):
     moves = [
-        (w_in, w_ref), (hid_in, hid), (hid_h_in, hid_h), (own_in, img.at[2:6, 2:10]), (own_h_in, own_h),
+        (w_in, w_ref),
+        (t_h_in, t_h), (far_h_in, far_h),
+        (prev, f_ref.at[0:7, 4:12]),
+        (a2.at[0:7], f_ref.at[0:7, 0:4]),
+        (b2.at[0:7], f_ref.at[0:7, 12:16]),
+        (following, f_ref.at[7:14, 4:12]),
+        (a2.at[7:14], f_ref.at[7:14, 0:4]),
+        (b2.at[7:14], f_ref.at[7:14, 12:16]),
+        (hid_in.at[2:8], hid.at[2:8]), (hid_h_in.at[2:8], hid_h.at[2:8]),
+        (own_in, img.at[2:6, 2:10]), (own_h_in, own_h),
         (slope_in, slope_ref), (slope_h_in, slope_h),
     ]
     copies = [pltpu.make_async_copy(x, y, sems.at[i]) for i, (x, y) in enumerate(moves)]
     for copy in copies:
         copy.start()
-    for copy in copies[:3]:
+    for copy in copies[:9]:
+        copy.wait()
+
+    def field_rows(t, r):
+        return f_ref[t + 2, pl.ds(r, 4)].reshape(4 * CH, LANES)
+
+    for i, m in enumerate(OUTER_LAYERS):
+
+        def put(p, v):
+            slope = f_ref[m, pl.ds(2 * p + 1, 2)].reshape(2 * CH, LANES)
+            store(hid, m, p, slope.astype(jnp.float32) * v)
+
+        def put_halo(v):
+            store_halo(hid_h, m, far_h[i] * v)
+
+        convolve_layer(w_ref[0], field_rows, lambda t: t_h[t], m, range(7), put, put_halo)
+
+    for copy in copies[9:11]:
         copy.wait()
     wide = lax.broadcasted_iota(jnp.int32, (2 * CH, LANES), 1)
     wide8 = wide & 7
@@ -374,7 +409,7 @@
 
     lax.fori_loop(0, 4, stage_ends, 0, unroll=True)
 
-    for copy in copies[3:]:
+    for copy in copies[11:]:
         copy.wait()
 
     def stage_rim(i, carry):
@@ -408,25 +443,26 @@
     lax.fori_loop(0, 4, stage_out, 0, unroll=True)
 
 
-def second_convs(place, fields, weights, after):
+def second_convs(place, fields, outer, weights, after):
     return pl.pallas_call(
         second_kernel_body,
         out_shape=jax.ShapeDtypeStruct((4, 8, CH, LANES), jnp.float32),
         in_specs=[pl.BlockSpec(memory_space=pltpu.SMEM)]
-        + [pl.BlockSpec(memory_space=pl.ANY)] * 8,
+        + [pl.BlockSpec(memory_space=pl.ANY)] * 14,
         scratch_shapes=[
+            pltpu.VMEM((14, 16, CH, LANES), jnp.bfloat16),
             pltpu.VMEM(weights.shape, weights.dtype),
             *[pltpu.VMEM(f.shape, f.dtype) for i, f in enumerate(fields) if i != 2],
             pltpu.VMEM((8, 12, CH, LANES), jnp.bfloat16),
             pltpu.VMEM((8, 4 * CH, LANES), jnp.bfloat16),
             pltpu.VMEM((6, 10, CH, LANES), jnp.bfloat16),
             pltpu.VMEM((6, 4 * CH, LANES), jnp.bfloat16),
-            pltpu.SemaphoreType.DMA((7,)),
+            pltpu.SemaphoreType.DMA((15,)),
         ],
         compiler_params=pltpu.CompilerParams(vmem_limit_bytes=62 << 20),
         cost_estimate=pl.CostEstimate(flops=8 << 30, bytes_accessed=4 << 20, transcendentals=0),
         name="second_convs",
-    )(place, *fields, weights, after)
+    )(place, *fields, *outer, weights, after)
 
 
 def weights_kernel(k1_ref, k2_ref, w_ref):
@@ -504,7 +540,7 @@
     ).astype(jnp.int32)
     parts = lax.all_to_all(spread, ("gy", "gz"), 0, 0, tiled=True)
     part = jnp.sum(parts, axis=0, keepdims=True)
-    result = second_convs(place, fields, weights, part)
+    result = second_convs(place, fields, (prev, following, a2, b2), weights, part)
     count = lax.axis_size("gx")
     parts = lax.all_to_all(jnp.broadcast_to(part, (count, 1, LANES)), "gx", 0, 0, tiled=True)
     return finish(result, parts)

time: 110 us -> 108 us (0.982)
  waiting for transfers between devices: 32.8 us -> 30.6 us
    pallas_call x1, Pallas kernels: 7.38 us -> 9.47 us  [second_convs(): pl.pallas_call(second_kernel_body, out_shape=jax.ShapeDtypeStruct((4, 8,...]
    all_to_all x1, waiting for transfers between devices: 5.97 us -> 3.89 us  [on_device(): lax.all_to_all(jnp.broadcast_to(part, (count, 1, LANES)), 'gx', 0, 0, til...]
    pallas_call x1, Pallas kernels: 8.48 us -> 6.96 us  [first_convs(): pl.pallas_call(first_kernel_body, out_shape=(*fields, shape((spread, 1, L...]
  transfers between devices with their start and end apart: 10 -> 10, of which waited for: 8 -> 8; matrix products, arithmetic and copies ran while one was open for 1% -> 1% of each run, Pallas kernels for 10% -> 12%
where the time goes in v6:
time: 108 us
  starting transfers between devices  49.2 us (46%)
  waiting for transfers between devices  30.6 us (28%)
  Pallas kernels  20.9 us (19%)
  local copies, waits for them, and re-layouts  5.53 us (5%)
  between operations  1.09 us (1%)
    all_to_all x1, starting transfers between devices, on_device(): lax.all_to_all(jnp.broadcast_to(part, (count, 1, LANES)), 'gx', 0, 0, til...  20.4 us
    ppermute x4, starting transfers between devices, shift_pair(): from_prev = lax.ppermute(up, axis, [(i, i + 1) for i in range(ends)])  18.7 us
    ppermute x4, waiting for transfers between devices, shift_pair(): from_next = lax.ppermute(down, axis, [(i + 1, i) for i in range(ends)])  11.6 us
    ppermute x4, waiting for transfers between devices, shift_pair(): from_prev = lax.ppermute(up, axis, [(i, i + 1) for i in range(ends)])  10.4 us
    pallas_call x1, Pallas kernels, second_convs(): pl.pallas_call(second_kernel_body, out_shape=jax.ShapeDtypeStruct((4, 8,...  9.47 us
    pallas_call x1, Pallas kernels, first_convs(): pl.pallas_call(first_kernel_body, out_shape=(*fields, shape((spread, 1, L...  6.96 us
    ppermute x4, starting transfers between devices, shift_pair(): from_next = lax.ppermute(down, axis, [(i + 1, i) for i in range(ends)])  5.8 us
    all_to_all x1, waiting for transfers between devices, on_device(): parts = lax.all_to_all(spread, ('gy', 'gz'), 0, 0, tiled=True)  4.81 us
  transfers between devices with their start and end apart: 10, of which 8 were waited for; matrix products, arithmetic and copies ran while one was open for 1% of the time, Pallas kernels for 12%

profile of v6, /device:TPU:1, one launch (start us, length us, event | category | flops | bytes accessed | tf_op | source)
XLA Modules:
  0.0 107.6 jit_solution(12017713352642032871)
XLA Ops:
  0.6 0.0 copy-start.11
  0.6 1.1 %copy.11 = bf16[32,4,8,128]{3,0,2,1:T(8,128)(2,1)S(1)} copy(bf16[32,4,8,128]{3,2,1,0:T(8,128)(2,1)} %param.5) | data formatting | bytes 524288 | tf_op args[1]
  1.8 0.0 copy-done.11
  1.8 0.1 copy.10
  1.9 0.1 pad_maximum_fusion.mine_ref.mine
  2.0 0.0 copy-start
  2.0 0.0 copy-start.9
  2.0 0.0 copy-start.10
  2.0 5.6 %collective-permute-start = (bf16[7,8,32,128]{3,2,1,0:T(8,128)(2,1)S(1)}, bf16[7,8,32,128]{3,2,1,0:T(8,128)(2,1)S(1)}, u32[]{:S(2)}, u32[]{:S(2)}) collective-permute-start(bf16[7,8,32,128]{3,2,1,0:T(8,128)(2,1)S(1)} %slice.24), channel_id=1, source_target_pairs={{0,16},{16,32},{32,48},{48,64},{64,80},{80,96},{96,112},{112,128},... | collective-permute-start | bytes 1376264 | tf_op jit(solution)/shard_map/ppermute | solution.py:15
  7.7 1.3 %collective-permute-start.1 = (bf16[7,8,32,128]{3,2,1,0:T(8,128)(2,1)S(1)}, bf16[7,8,32,128]{3,2,1,0:T(8,128)(2,1)S(1)}, u32[]{:S(2)}, u32[]{:S(2)}) collective-permute-start(bf16[7,8,32,128]{3,2,1,0:T(8,128)(2,1)S(1)} %pad_maximum_fusion.1), channel_id=1, source_target_pairs={{16,0},{32,16},{48,32},{64,48},{80,64},{96,80},{112,96},{128,112},... | collective-permute-start | bytes 1376264 | tf_op jit(solution)/shard_map/ppermute | solution.py:16
  9.1 3.2 %collective-permute-start.2 = (bf16[8,4,32,128]{3,2,1,0:T(8,128)(2,1)S(1)}, bf16[8,4,32,128]{3,2,1,0:T(8,128)(2,1)S(1)}, u32[]{:S(2)}, u32[]{:S(2)}) collective-permute-start(bf16[8,4,32,128]{3,2,1,0:T(8,128)(2,1)S(1)} %get-tuple-element.39), channel_id=1, source_target_pairs={{0,4},{4,8},{8,12},{1,5},{5,9},{9,13},{2,6},{6,10},{10,14},{3,7},{... | collective-permute-start | bytes 786440 | tf_op jit(solution)/shard_map/ppermute | solution.py:15
  12.3 1.3 %collective-permute-start.3 = (bf16[8,4,32,128]{3,2,1,0:T(8,128)(2,1)S(1)}, bf16[8,4,32,128]{3,2,1,0:T(8,128)(2,1)S(1)}, u32[]{:S(2)}, u32[]{:S(2)}) collective-permute-start(bf16[8,4,32,128]{3,2,1,0:T(8,128)(2,1)S(1)} %get-tuple-element.38), channel_id=1, source_target_pairs={{4,0},{8,4},{12,8},{5,1},{9,5},{13,9},{6,2},{10,6},{14,10},{7,3},{... | collective-permute-start | bytes 786440 | tf_op jit(solution)/shard_map/ppermute | solution.py:16
  13.6 0.0 copy-done.9
  13.6 0.0 copy-done.10
  13.6 1.0 pair_matrices.1.w_in
  14.6 0.0 copy-start.3
  14.6 0.8 copy-done.3
  15.5 1.5 %collective-permute-done.2.a1 = bf16[8,4,32,128]{3,2,1,0:T(8,128)(2,1)S(1)} collective-permute-done((bf16[8,4,32,128]{3,2,1,0:T(8,128)(2,1)S(1)}, bf16[8,4,32,128]{3,2,1,0:T(8,128)(2,1)S(1)}, u32[]{:S(2)}, u32[]{:S(2)}) %collective-permute-start.2) | collective-permute-done | bytes 262176 | tf_op jit(solution)/shard_map/ppermute | solution.py:15
  16.9 0.0 copy-start.7
  16.9 3.8 %collective-permute-done.3.b1 = bf16[8,4,32,128]{3,2,1,0:T(8,128)(2,1)S(1)} collective-permute-done((bf16[8,4,32,128]{3,2,1,0:T(8,128)(2,1)S(1)}, bf16[8,4,32,128]{3,2,1,0:T(8,128)(2,1)S(1)}, u32[]{:S(2)}, u32[]{:S(2)}) %collective-permute-start.3) | collective-permute-done | bytes 262176 | tf_op jit(solution)/shard_map/ppermute | solution.py:16
  20.8 0.0 copy-start.8
  20.8 4.1 %collective-permute-done.prev_ref.prev = bf16[7,8,32,128]{3,2,1,0:T(8,128)(2,1)S(1)} collective-permute-done((bf16[7,8,32,128]{3,2,1,0:T(8,128)(2,1)S(1)}, bf16[7,8,32,128]{3,2,1,0:T(8,128)(2,1)S(1)}, u32[]{:S(2)}, u32[]{:S(2)}) %collective-permute-start) | collective-permute-done | bytes 458784 | tf_op jit(solution)/shard_map/ppermute | solution.py:15
  24.9 0.0 copy-start.1
  24.9 0.0 collective-permute-done.1.next_ref.following
  24.9 0.0 copy-start.2
  24.9 0.1 edge_rows.1
  24.9 5.0 %collective-permute-start.4 = (bf16[14,4,32,128]{3,2,1,0:T(8,128)(2,1)S(1)}, bf16[14,4,32,128]{3,2,1,0:T(8,128)(2,1)S(1)}, u32[]{:S(2)}, u32[]{:S(2)}) collective-permute-start(bf16[14,4,32,128]{3,2,1,0:T(8,128)(2,1)S(1)} %get-tuple-element.24), channel_id=1, source_target_pairs={{0,4},{4,8},{8,12},{1,5},{5,9},{9,13},{2,6},{6,10},{10,14},{3,7},{... | collective-permute-start | bytes 1376264 | tf_op jit(solution)/shard_map/ppermute | solution.py:15
  30.0 1.3 %collective-permute-start.5 = (bf16[14,4,32,128]{3,2,1,0:T(8,128)(2,1)S(1)}, bf16[14,4,32,128]{3,2,1,0:T(8,128)(2,1)S(1)}, u32[]{:S(2)}, u32[]{:S(2)}) collective-permute-start(bf16[14,4,32,128]{3,2,1,0:T(8,128)(2,1)S(1)} %get-tuple-element.25), channel_id=1, source_target_pairs={{4,0},{8,4},{12,8},{5,1},{9,5},{13,9},{6,2},{10,6},{14,10},{7,3},{... | collective-permute-start | bytes 1376264 | tf_op jit(solution)/shard_map/ppermute | solution.py:16
  31.3 0.0 copy-done
  31.3 2.1 %pack_mid.1.tile_ref = f32[22,32,128]{2,1,0:T(8,128)S(1)} custom-call(bf16[7,8,32,128]{3,2,1,0:T(8,128)(2,1)S(1)} %collective-permute-done.prev_ref.prev, bf16[8,8,32,128]{3,2,1,0:T(8,128)(2,1)S(1)} %pad_maximum_fusion.mine_ref.mine, bf16[7,8,32,128]{3,2,1,0:T(8,128)(2,1)S(1)} %collective-permute-done.1.next_ref.following, ...), custom_call_target="tpu_custom_call" | custom-call | bytes 2097152 | tf_op jit(solution)/shard_map/pack_mid/pallas_call | solution.py:83
  33.4 0.0 copy-done.7
  33.4 0.0 copy-done.8
  33.4 0.0 copy-done.1
  33.4 0.0 copy-done.2
  33.4 4.8 %collective-permute-done.4.a2 = bf16[14,4,32,128]{3,2,1,0:T(8,128)(2,1)S(1)} collective-permute-done((bf16[14,4,32,128]{3,2,1,0:T(8,128)(2,1)S(1)}, bf16[14,4,32,128]{3,2,1,0:T(8,128)(2,1)S(1)}, u32[]{:S(2)}, u32[]{:S(2)}) %collective-permute-start.4) | collective-permute-done | bytes 458784 | tf_op jit(solution)/shard_map/ppermute | solution.py:15
  38.2 0.0 copy-start.5
  38.2 3.9 %collective-permute-done.5.b2 = bf16[14,4,32,128]{3,2,1,0:T(8,128)(2,1)S(1)} collective-permute-done((bf16[14,4,32,128]{3,2,1,0:T(8,128)(2,1)S(1)}, bf16[14,4,32,128]{3,2,1,0:T(8,128)(2,1)S(1)}, u32[]{:S(2)}, u32[]{:S(2)}) %collective-permute-start.5) | collective-permute-done | bytes 458784 | tf_op jit(solution)/shard_map/ppermute | solution.py:16
  42.1 0.0 copy-start.6
  42.1 0.4 pack_edges.1
  42.4 0.4 copy-done.6
  42.8 4.8 %collective-permute-start.6 = (bf16[11,32,128]{2,1,0:T(8,128)(2,1)S(1)}, bf16[11,32,128]{2,1,0:T(8,128)(2,1)S(1)}, u32[]{:S(2)}, u32[]{:S(2)}) collective-permute-start(bf16[11,32,128]{2,1,0:T(8,128)(2,1)S(1)} %get-tuple-element.26), channel_id=1, source_target_pairs={{0,1},{1,2},{2,3},{4,5},{5,6},{6,7},{8,9},{9,10},{10,11},{12,13},{... | collective-permute-start | bytes 270344 | tf_op jit(solution)/shard_map/ppermute | solution.py:15
  47.7 1.9 %collective-permute-start.7 = (bf16[11,32,128]{2,1,0:T(8,128)(2,1)S(1)}, bf16[11,32,128]{2,1,0:T(8,128)(2,1)S(1)}, u32[]{:S(2)}, u32[]{:S(2)}) collective-permute-start(bf16[11,32,128]{2,1,0:T(8,128)(2,1)S(1)} %get-tuple-element.27), channel_id=1, source_target_pairs={{1,0},{2,1},{3,2},{5,4},{6,5},{7,6},{9,8},{10,9},{11,10},{13,12},{... | collective-permute-start | bytes 270344 | tf_op jit(solution)/shard_map/ppermute | solution.py:16
  49.6 0.0 collective-permute-done.6.rl_in
  49.6 0.0 copy-start.13
  49.6 3.9 %collective-permute-done.7.rr_in = bf16[11,32,128]{2,1,0:T(8,128)(2,1)S(1)} collective-permute-done((bf16[11,32,128]{2,1,0:T(8,128)(2,1)S(1)}, bf16[11,32,128]{2,1,0:T(8,128)(2,1)S(1)}, u32[]{:S(2)}, u32[]{:S(2)}) %collective-permute-start.7) | collective-permute-done | bytes 90144 | tf_op jit(solution)/shard_map/ppermute | solution.py:16
  53.5 0.0 copy-done.5
  53.5 0.0 copy-done.13
  53.5 0.0 copy-start.14
  53.5 0.6 copy-done.14
  54.2 7.0 %first_convs.1 = (bf16[10,14,32,128]{3,2,1,0:T(8,128)(2,1)}, bf16[10,128,128]{2,1,0:T(8,128)(2,1)}, bf16[4,8,32,128]{3,2,1,0:T(8,128)(2,1)}, f32[4,64,128]{2,1,0...) custom-call(bf16[7,8,32,128]{3,2,1,0:T(8,128)(2,1)} %copy-done.1, ...), custom_call_target="tpu_custom_call" | custom-call | flops 8589934592 | bytes 8388608 | tf_op jit(solution)/shard_map/first_convs/pallas_call | solution.py:321
  61.1 4.3 %all-to-all-start = ((f32[16,1,128]{2,1,0:T(1,128)}), f32[16,1,128]{2,1,0:T(1,128)S(1)}, u32[]{:S(2)}, u32[]{:S(2)}) async-start(f32[16,1,128]{2,1,0:T(1,128)} %get-tuple-element.37), calls=%async_computation | async-start | bytes 16384 | tf_op jit(solution)/shard_map/all_to_all | solution.py:541
  65.4 0.7 stack.15.place
  66.1 4.8 %all-to-all-done = f32[16,1,128]{2,1,0:T(1,128)S(1)} async-done(((f32[16,1,128]{2,1,0:T(1,128)}), f32[16,1,128]{2,1,0:T(1,128)S(1)}, u32[]{:S(2)}, u32[]{:S(2)}) %all-to-all-start) | async-done | bytes 8224 | tf_op jit(solution)/shard_map/all_to_all | solution.py:541
  70.9 0.0 copy-start.12
  70.9 0.6 broadcast_in_dim.9
  71.6 20.4 %all-to-all-start.1 = ((f32[32,1,128]{2,1,0:T(1,128)}), f32[32,1,128]{2,1,0:T(1,128)S(1)}, u32[]{:S(2)}, u32[]{:S(2)}) async-start(f32[32,1,128]{2,1,0:T(1,128)} %broadcast_in_dim.9), calls=%async_computation.1 | async-start | bytes 32768 | tf_op jit(solution)/shard_map/all_to_all | solution.py:545
  92.0 0.0 copy-done.12
  92.0 9.5 %second_convs.1.result = f32[4,8,32,128]{3,2,1,0:T(8,128)} custom-call(s32[6]{0:T(128)} %stack.15.place, bf16[10,14,32,128]{3,2,1,0:T(8,128)(2,1)} %get-tuple-element.29.hid_in, bf16[10,128,128]{2,1,0:T(8,128)(2,1)} %get-tuple-element.30.hid_h_in, bf16[4,8,32,128]{3,2,1,0:T(8,128)(2,1)} %get-tuple-element.31.own_in, ...), custom_call_target="tpu_custom_call" | custom-call | flops 8589934592 | bytes 4194304 | tf_op jit(solution)/shard_map/second_convs/pallas_call | solution.py:447
  101.5 3.9 %all-to-all-done.1.parts = f32[32,1,128]{2,1,0:T(1,128)S(1)} async-done(((f32[32,1,128]{2,1,0:T(1,128)}), f32[32,1,128]{2,1,0:T(1,128)S(1)}, u32[]{:S(2)}, u32[]{:S(2)}) %all-to-all-start.1) | async-done | bytes 16416 | tf_op jit(solution)/shard_map/all_to_all | solution.py:545
  105.3 0.0 copy-start.4
  105.4 1.0 copy-done.4
  106.4 1.0 finish.1
  (7 shorter events, 0.2 us)
Async XLA Ops:
  0.6 1.1 %copy-start.11 = (bf16[32,4,8,128]{3,2,1,0:T(8,128)(2,1)S(1)}, bf16[32,4,8,128]{3,2,1,0:T(8,128)(2,1)}, u32[]{:S(2)}) copy-start(bf16[32,4,8,128]{3,2,1,0:T(8,128)(2,1)} %param.4) | copy-start | bytes 786436
  2.0 29.3 %copy-start = (bf16[8,8,32,128]{3,2,1,0:T(8,128)(2,1)}, bf16[8,8,32,128]{3,2,1,0:T(8,128)(2,1)S(1)}, u32[]{:S(2)}) copy-start(bf16[8,8,32,128]{3,2,1,0:T(8,128)(2,1)S(1)} %pad_maximum_fusion.mine_ref.mine) | copy-start | bytes 1572868
  2.0 11.6 %copy-start.9 = (bf16[27,32,32]{2,1,0:T(8,128)(2,1)S(1)}, bf16[27,32,32]{2,1,0:T(8,128)(2,1)}, u32[]{:S(2)}) copy-start(bf16[27,32,32]{2,1,0:T(8,128)(2,1)} %k1_ref.1) | copy-start | bytes 165892
  2.0 11.6 %copy-start.10 = (bf16[27,32,32]{2,1,0:T(8,128)(2,1)S(1)}, bf16[27,32,32]{2,1,0:T(8,128)(2,1)}, u32[]{:S(2)}) copy-start(bf16[27,32,32]{2,1,0:T(8,128)(2,1)} %k2_ref.1) | copy-start | bytes 165892
  2.0 22.8 %collective-permute-start = (bf16[7,8,32,128]{3,2,1,0:T(8,128)(2,1)S(1)}, bf16[7,8,32,128]{3,2,1,0:T(8,128)(2,1)S(1)}, u32[]{:S(2)}, u32[]{:S(2)}) collective-permute-start(bf16[7,8,32,128]{3,2,1,0:T(8,128)(2,1)S(1)} %slice.24), channel_id=1, source_target_pairs={{0,16},{16,32},{32,48},{48,64},{64,80},{80,96},{96,112},{112,128},... | collective-permute-start | bytes 1376264 | tf_op jit(solution)/shard_map/ppermute | solution.py:15
  7.7 17.1 %collective-permute-start.1 = (bf16[7,8,32,128]{3,2,1,0:T(8,128)(2,1)S(1)}, bf16[7,8,32,128]{3,2,1,0:T(8,128)(2,1)S(1)}, u32[]{:S(2)}, u32[]{:S(2)}) collective-permute-start(bf16[7,8,32,128]{3,2,1,0:T(8,128)(2,1)S(1)} %pad_maximum_fusion.1), channel_id=1, source_target_pairs={{16,0},{32,16},{48,32},{64,48},{80,64},{96,80},{112,96},{128,112},... | collective-permute-start | bytes 1376264 | tf_op jit(solution)/shard_map/ppermute | solution.py:16
  9.1 7.8 %collective-permute-start.2 = (bf16[8,4,32,128]{3,2,1,0:T(8,128)(2,1)S(1)}, bf16[8,4,32,128]{3,2,1,0:T(8,128)(2,1)S(1)}, u32[]{:S(2)}, u32[]{:S(2)}) collective-permute-start(bf16[8,4,32,128]{3,2,1,0:T(8,128)(2,1)S(1)} %get-tuple-element.39), channel_id=1, source_target_pairs={{0,4},{4,8},{8,12},{1,5},{5,9},{9,13},{2,6},{6,10},{10,14},{3,7},{... | collective-permute-start | bytes 786440 | tf_op jit(solution)/shard_map/ppermute | solution.py:15
  12.3 8.5 %collective-permute-start.3 = (bf16[8,4,32,128]{3,2,1,0:T(8,128)(2,1)S(1)}, bf16[8,4,32,128]{3,2,1,0:T(8,128)(2,1)S(1)}, u32[]{:S(2)}, u32[]{:S(2)}) collective-permute-start(bf16[8,4,32,128]{3,2,1,0:T(8,128)(2,1)S(1)} %get-tuple-element.38), channel_id=1, source_target_pairs={{4,0},{8,4},{12,8},{5,1},{9,5},{13,9},{6,2},{10,6},{14,10},{7,3},{... | collective-permute-start | bytes 786440 | tf_op jit(solution)/shard_map/ppermute | solution.py:16
  14.6 0.8 copy-start.3
  16.9 16.4 %copy-start.7 = (bf16[8,4,32,128]{3,2,1,0:T(8,128)(2,1)}, bf16[8,4,32,128]{3,2,1,0:T(8,128)(2,1)S(1)}, u32[]{:S(2)}) copy-start(bf16[8,4,32,128]{3,2,1,0:T(8,128)(2,1)S(1)} %collective-permute-done.2.a1) | copy-start | bytes 786436
  20.8 12.6 %copy-start.8 = (bf16[8,4,32,128]{3,2,1,0:T(8,128)(2,1)}, bf16[8,4,32,128]{3,2,1,0:T(8,128)(2,1)S(1)}, u32[]{:S(2)}) copy-start(bf16[8,4,32,128]{3,2,1,0:T(8,128)(2,1)S(1)} %collective-permute-done.3.b1) | copy-start | bytes 786436
  24.9 8.5 %copy-start.1 = (bf16[7,8,32,128]{3,2,1,0:T(8,128)(2,1)}, bf16[7,8,32,128]{3,2,1,0:T(8,128)(2,1)S(1)}, u32[]{:S(2)}) copy-start(bf16[7,8,32,128]{3,2,1,0:T(8,128)(2,1)S(1)} %collective-permute-done.prev_ref.prev) | copy-start | bytes 1376260
  24.9 8.5 %copy-start.2 = (bf16[7,8,32,128]{3,2,1,0:T(8,128)(2,1)}, bf16[7,8,32,128]{3,2,1,0:T(8,128)(2,1)S(1)}, u32[]{:S(2)}) copy-start(bf16[7,8,32,128]{3,2,1,0:T(8,128)(2,1)S(1)} %collective-permute-done.1.next_ref.following) | copy-start | bytes 1376260
  24.9 13.2 %collective-permute-start.4 = (bf16[14,4,32,128]{3,2,1,0:T(8,128)(2,1)S(1)}, bf16[14,4,32,128]{3,2,1,0:T(8,128)(2,1)S(1)}, u32[]{:S(2)}, u32[]{:S(2)}) collective-permute-start(bf16[14,4,32,128]{3,2,1,0:T(8,128)(2,1)S(1)} %get-tuple-element.24), channel_id=1, source_target_pairs={{0,4},{4,8},{8,12},{1,5},{5,9},{9,13},{2,6},{6,10},{10,14},{3,7},{... | collective-permute-start | bytes 1376264 | tf_op jit(solution)/shard_map/ppermute | solution.py:15
  30.0 12.1 %collective-permute-start.5 = (bf16[14,4,32,128]{3,2,1,0:T(8,128)(2,1)S(1)}, bf16[14,4,32,128]{3,2,1,0:T(8,128)(2,1)S(1)}, u32[]{:S(2)}, u32[]{:S(2)}) collective-permute-start(bf16[14,4,32,128]{3,2,1,0:T(8,128)(2,1)S(1)} %get-tuple-element.25), channel_id=1, source_target_pairs={{4,0},{8,4},{12,8},{5,1},{9,5},{13,9},{6,2},{10,6},{14,10},{7,3},{... | collective-permute-start | bytes 1376264 | tf_op jit(solution)/shard_map/ppermute | solution.py:16
  38.2 15.3 %copy-start.5 = (bf16[14,4,32,128]{3,2,1,0:T(8,128)(2,1)}, bf16[14,4,32,128]{3,2,1,0:T(8,128)(2,1)S(1)}, u32[]{:S(2)}) copy-start(bf16[14,4,32,128]{3,2,1,0:T(8,128)(2,1)S(1)} %collective-permute-done.4.a2) | copy-start | bytes 1376260
  42.1 0.8 copy-start.6
  42.8 6.8 %collective-permute-start.6 = (bf16[11,32,128]{2,1,0:T(8,128)(2,1)S(1)}, bf16[11,32,128]{2,1,0:T(8,128)(2,1)S(1)}, u32[]{:S(2)}, u32[]{:S(2)}) collective-permute-start(bf16[11,32,128]{2,1,0:T(8,128)(2,1)S(1)} %get-tuple-element.26), channel_id=1, source_target_pairs={{0,1},{1,2},{2,3},{4,5},{5,6},{6,7},{8,9},{9,10},{10,11},{12,13},{... | collective-permute-start | bytes 270344 | tf_op jit(solution)/shard_map/ppermute | solution.py:15
  47.7 5.8 %collective-permute-start.7 = (bf16[11,32,128]{2,1,0:T(8,128)(2,1)S(1)}, bf16[11,32,128]{2,1,0:T(8,128)(2,1)S(1)}, u32[]{:S(2)}, u32[]{:S(2)}) collective-permute-start(bf16[11,32,128]{2,1,0:T(8,128)(2,1)S(1)} %get-tuple-element.27), channel_id=1, source_target_pairs={{1,0},{2,1},{3,2},{5,4},{6,5},{7,6},{9,8},{10,9},{11,10},{13,12},{... | collective-permute-start | bytes 270344 | tf_op jit(solution)/shard_map/ppermute | solution.py:16
  49.6 3.9 %copy-start.13 = (bf16[11,32,128]{2,1,0:T(8,128)(2,1)}, bf16[11,32,128]{2,1,0:T(8,128)(2,1)S(1)}, u32[]{:S(2)}) copy-start(bf16[11,32,128]{2,1,0:T(8,128)(2,1)S(1)} %collective-permute-done.6.rl_in) | copy-start | bytes 270340
  53.5 0.6 copy-start.14
  61.1 9.8 %all-to-all-start = ((f32[16,1,128]{2,1,0:T(1,128)}), f32[16,1,128]{2,1,0:T(1,128)S(1)}, u32[]{:S(2)}, u32[]{:S(2)}) async-start(f32[16,1,128]{2,1,0:T(1,128)} %get-tuple-element.37), calls=%async_computation | async-start | bytes 16384 | tf_op jit(solution)/shard_map/all_to_all | solution.py:541
  70.9 21.0 %copy-start.12 = (f32[128]{0:T(128)}, f32[128]{0:T(128)S(1)}, u32[]{:S(2)}) copy-start(f32[128]{0:T(128)S(1)} %reduce_sum.9) | copy-start | bytes 1540
  71.6 33.8 %all-to-all-start.1 = ((f32[32,1,128]{2,1,0:T(1,128)}), f32[32,1,128]{2,1,0:T(1,128)S(1)}, u32[]{:S(2)}, u32[]{:S(2)}) async-start(f32[32,1,128]{2,1,0:T(1,128)} %broadcast_in_dim.9), calls=%async_computation.1 | async-start | bytes 32768 | tf_op jit(solution)/shard_map/all_to_all | solution.py:545
  105.3 1.0 copy-start.4

commit v7 on v6

--- a/solution.py
+++ b/solution.py
@@ -492,20 +492,33 @@
     )(first_kernel, second_kernel)
 
 
-def finish_kernel(result, parts, out_ref, norm_ref):
+def turn_kernel(result, out_ref):
+    for x in range(result.shape[0]):
+        out_ref[:, x] = result[x].transpose(1, 0, 2)
+
+
+def turn(result):
+    return pl.pallas_call(
+        turn_kernel,
+        out_shape=jax.ShapeDtypeStruct((CH, 4, 8, LANES), jnp.float32),
+        compiler_params=pltpu.CompilerParams(vmem_limit_bytes=16 << 20),
+        cost_estimate=pl.CostEstimate(flops=0, bytes_accessed=4 << 20, transcendentals=0),
+        name="turn",
+    )(result)
+
+
+def finish_kernel(block, parts, out_ref, norm_ref):
     total = jnp.sum(jnp.sum(parts[...], axis=0), axis=1, keepdims=True)
     norm = jnp.sqrt(total + 1e-06)
     norm_ref[0] = norm[0, 0]
-    scale = jnp.broadcast_to(norm, (8, LANES))
-    for x in range(result.shape[0]):
-        out_ref[:, x] = result[x].transpose(1, 0, 2) / scale
-
-
-def finish(result, parts):
+    out_ref[...] = block[...] / jnp.broadcast_to(norm, (8, LANES))
+
+
+def finish(block, parts):
     return pl.pallas_call(
         finish_kernel,
         out_shape=(
-            jax.ShapeDtypeStruct((CH, 4, 8, LANES), jnp.float32),
+            jax.ShapeDtypeStruct(block.shape, jnp.float32),
             jax.ShapeDtypeStruct((1,), jnp.float32),
         ),
         out_specs=(
@@ -514,7 +527,7 @@
         ),
         compiler_params=pltpu.CompilerParams(vmem_limit_bytes=16 << 20),
         name="finish",
-    )(result, parts)
+    )(block, parts)
 
 
 def on_device(tangent, slopes, first_kernel, second_kernel):
@@ -540,7 +553,7 @@
     ).astype(jnp.int32)
     parts = lax.all_to_all(spread, ("gy", "gz"), 0, 0, tiled=True)
     part = jnp.sum(parts, axis=0, keepdims=True)
-    result = second_convs(place, fields, (prev, following, a2, b2), weights, part)
+    result = turn(second_convs(place, fields, (prev, following, a2, b2), weights, part))
     count = lax.axis_size("gx")
     parts = lax.all_to_all(jnp.broadcast_to(part, (count, 1, LANES)), "gx", 0, 0, tiled=True)
     return finish(result, parts)

time: 108 us -> 107 us (level)
  waiting for transfers between devices: 30.6 us -> 29.5 us
    all_to_all x1, waiting for transfers between devices: 3.89 us -> 2.74 us  [on_device(): lax.all_to_all(jnp.broadcast_to(part, (count, 1, LANES)), 'gx', 0, 0, til...]
where the time goes in v7:
time: 107 us; the launch traced here: 106 us
  starting transfers between devices  49.2 us (46%)
  waiting for transfers between devices  29.5 us (28%)
  Pallas kernels  21 us (20%)
  local copies, waits for them, and re-layouts  5.52 us (5%)
  between operations  1.1 us (1%)
    all_to_all x1, starting transfers between devices, on_device(): lax.all_to_all(jnp.broadcast_to(part, (count, 1, LANES)), 'gx', 0, 0, til...  20.4 us
    ppermute x4, starting transfers between devices, shift_pair(): from_prev = lax.ppermute(up, axis, [(i, i + 1) for i in range(ends)])  18.7 us
    ppermute x4, waiting for transfers between devices, shift_pair(): from_next = lax.ppermute(down, axis, [(i + 1, i) for i in range(ends)])  11.6 us
    ppermute x4, waiting for transfers between devices, shift_pair(): from_prev = lax.ppermute(up, axis, [(i, i + 1) for i in range(ends)])  10.4 us
    pallas_call x1, Pallas kernels, second_convs(): pl.pallas_call(second_kernel_body, out_shape=jax.ShapeDtypeStruct((4, 8,...  9.47 us
    pallas_call x1, Pallas kernels, first_convs(): pl.pallas_call(first_kernel_body, out_shape=(*fields, shape((spread, 1, L...  6.96 us
    ppermute x4, starting transfers between devices, shift_pair(): from_next = lax.ppermute(down, axis, [(i + 1, i) for i in range(ends)])  5.8 us
    all_to_all x1, waiting for transfers between devices, on_device(): parts = lax.all_to_all(spread, ('gy', 'gz'), 0, 0, tiled=True)  4.81 us
  transfers between devices with their start and end apart: 10, of which 8 were waited for; matrix products, arithmetic and copies ran while one was open for 1% of the time, Pallas kernels for 12%

profile of v7, /device:TPU:1, one launch (start us, length us, event | category | flops | bytes accessed | tf_op | source)
XLA Modules:
  0.0 106.5 jit_solution(4474162134497389490)
XLA Ops:
  0.6 0.0 copy-start.11
  0.6 1.1 %copy.11 = bf16[32,4,8,128]{3,0,2,1:T(8,128)(2,1)S(1)} copy(bf16[32,4,8,128]{3,2,1,0:T(8,128)(2,1)} %param.5) | data formatting | bytes 524288 | tf_op args[1]
  1.8 0.0 copy-done.11
  1.8 0.1 copy.10
  1.9 0.1 pad_maximum_fusion.mine_ref.mine
  2.0 0.0 copy-start
  2.0 0.0 copy-start.9
  2.0 0.0 copy-start.10
  2.0 5.6 %collective-permute-start = (bf16[7,8,32,128]{3,2,1,0:T(8,128)(2,1)S(1)}, bf16[7,8,32,128]{3,2,1,0:T(8,128)(2,1)S(1)}, u32[]{:S(2)}, u32[]{:S(2)}) collective-permute-start(bf16[7,8,32,128]{3,2,1,0:T(8,128)(2,1)S(1)} %slice.24), channel_id=1, source_target_pairs={{0,16},{16,32},{32,48},{48,64},{64,80},{80,96},{96,112},{112,128},... | collective-permute-start | bytes 1376264 | tf_op jit(solution)/shard_map/ppermute | solution.py:15
  7.7 1.3 %collective-permute-start.1 = (bf16[7,8,32,128]{3,2,1,0:T(8,128)(2,1)S(1)}, bf16[7,8,32,128]{3,2,1,0:T(8,128)(2,1)S(1)}, u32[]{:S(2)}, u32[]{:S(2)}) collective-permute-start(bf16[7,8,32,128]{3,2,1,0:T(8,128)(2,1)S(1)} %pad_maximum_fusion.1), channel_id=1, source_target_pairs={{16,0},{32,16},{48,32},{64,48},{80,64},{96,80},{112,96},{128,112},... | collective-permute-start | bytes 1376264 | tf_op jit(solution)/shard_map/ppermute | solution.py:16
  9.1 3.2 %collective-permute-start.2 = (bf16[8,4,32,128]{3,2,1,0:T(8,128)(2,1)S(1)}, bf16[8,4,32,128]{3,2,1,0:T(8,128)(2,1)S(1)}, u32[]{:S(2)}, u32[]{:S(2)}) collective-permute-start(bf16[8,4,32,128]{3,2,1,0:T(8,128)(2,1)S(1)} %get-tuple-element.39), channel_id=1, source_target_pairs={{0,4},{4,8},{8,12},{1,5},{5,9},{9,13},{2,6},{6,10},{10,14},{3,7},{... | collective-permute-start | bytes 786440 | tf_op jit(solution)/shard_map/ppermute | solution.py:15
  12.3 1.3 %collective-permute-start.3 = (bf16[8,4,32,128]{3,2,1,0:T(8,128)(2,1)S(1)}, bf16[8,4,32,128]{3,2,1,0:T(8,128)(2,1)S(1)}, u32[]{:S(2)}, u32[]{:S(2)}) collective-permute-start(bf16[8,4,32,128]{3,2,1,0:T(8,128)(2,1)S(1)} %get-tuple-element.38), channel_id=1, source_target_pairs={{4,0},{8,4},{12,8},{5,1},{9,5},{13,9},{6,2},{10,6},{14,10},{7,3},{... | collective-permute-start | bytes 786440 | tf_op jit(solution)/shard_map/ppermute | solution.py:16
  13.6 0.0 copy-done.9
  13.6 0.0 copy-done.10
  13.6 1.0 pair_matrices.1.w_in
  14.6 0.0 copy-start.3
  14.6 0.8 copy-done.3
  15.5 1.5 %collective-permute-done.2.a1 = bf16[8,4,32,128]{3,2,1,0:T(8,128)(2,1)S(1)} collective-permute-done((bf16[8,4,32,128]{3,2,1,0:T(8,128)(2,1)S(1)}, bf16[8,4,32,128]{3,2,1,0:T(8,128)(2,1)S(1)}, u32[]{:S(2)}, u32[]{:S(2)}) %collective-permute-start.2) | collective-permute-done | bytes 262176 | tf_op jit(solution)/shard_map/ppermute | solution.py:15
  16.9 0.0 copy-start.7
  16.9 3.8 %collective-permute-done.3.b1 = bf16[8,4,32,128]{3,2,1,0:T(8,128)(2,1)S(1)} collective-permute-done((bf16[8,4,32,128]{3,2,1,0:T(8,128)(2,1)S(1)}, bf16[8,4,32,128]{3,2,1,0:T(8,128)(2,1)S(1)}, u32[]{:S(2)}, u32[]{:S(2)}) %collective-permute-start.3) | collective-permute-done | bytes 262176 | tf_op jit(solution)/shard_map/ppermute | solution.py:16
  20.8 0.0 copy-start.8
  20.8 4.1 %collective-permute-done.prev_ref.prev = bf16[7,8,32,128]{3,2,1,0:T(8,128)(2,1)S(1)} collective-permute-done((bf16[7,8,32,128]{3,2,1,0:T(8,128)(2,1)S(1)}, bf16[7,8,32,128]{3,2,1,0:T(8,128)(2,1)S(1)}, u32[]{:S(2)}, u32[]{:S(2)}) %collective-permute-start) | collective-permute-done | bytes 458784 | tf_op jit(solution)/shard_map/ppermute | solution.py:15
  24.9 0.0 copy-start.1
  24.9 0.0 collective-permute-done.1.next_ref.following
  24.9 0.0 copy-start.2
  24.9 0.1 edge_rows.1
  24.9 5.0 %collective-permute-start.4 = (bf16[14,4,32,128]{3,2,1,0:T(8,128)(2,1)S(1)}, bf16[14,4,32,128]{3,2,1,0:T(8,128)(2,1)S(1)}, u32[]{:S(2)}, u32[]{:S(2)}) collective-permute-start(bf16[14,4,32,128]{3,2,1,0:T(8,128)(2,1)S(1)} %get-tuple-element.24), channel_id=1, source_target_pairs={{0,4},{4,8},{8,12},{1,5},{5,9},{9,13},{2,6},{6,10},{10,14},{3,7},{... | collective-permute-start | bytes 1376264 | tf_op jit(solution)/shard_map/ppermute | solution.py:15
  30.0 1.3 %collective-permute-start.5 = (bf16[14,4,32,128]{3,2,1,0:T(8,128)(2,1)S(1)}, bf16[14,4,32,128]{3,2,1,0:T(8,128)(2,1)S(1)}, u32[]{:S(2)}, u32[]{:S(2)}) collective-permute-start(bf16[14,4,32,128]{3,2,1,0:T(8,128)(2,1)S(1)} %get-tuple-element.25), channel_id=1, source_target_pairs={{4,0},{8,4},{12,8},{5,1},{9,5},{13,9},{6,2},{10,6},{14,10},{7,3},{... | collective-permute-start | bytes 1376264 | tf_op jit(solution)/shard_map/ppermute | solution.py:16
  31.3 0.0 copy-done
  31.3 2.1 %pack_mid.1.tile_ref = f32[22,32,128]{2,1,0:T(8,128)S(1)} custom-call(bf16[7,8,32,128]{3,2,1,0:T(8,128)(2,1)S(1)} %collective-permute-done.prev_ref.prev, bf16[8,8,32,128]{3,2,1,0:T(8,128)(2,1)S(1)} %pad_maximum_fusion.mine_ref.mine, bf16[7,8,32,128]{3,2,1,0:T(8,128)(2,1)S(1)} %collective-permute-done.1.next_ref.following, ...), custom_call_target="tpu_custom_call" | custom-call | bytes 2097152 | tf_op jit(solution)/shard_map/pack_mid/pallas_call | solution.py:83
  33.4 0.0 copy-done.7
  33.4 0.0 copy-done.8
  33.4 0.0 copy-done.1
  33.4 0.0 copy-done.2
  33.4 4.8 %collective-permute-done.4.a2 = bf16[14,4,32,128]{3,2,1,0:T(8,128)(2,1)S(1)} collective-permute-done((bf16[14,4,32,128]{3,2,1,0:T(8,128)(2,1)S(1)}, bf16[14,4,32,128]{3,2,1,0:T(8,128)(2,1)S(1)}, u32[]{:S(2)}, u32[]{:S(2)}) %collective-permute-start.4) | collective-permute-done | bytes 458784 | tf_op jit(solution)/shard_map/ppermute | solution.py:15
  38.2 0.0 copy-start.5
  38.2 3.9 %collective-permute-done.5.b2 = bf16[14,4,32,128]{3,2,1,0:T(8,128)(2,1)S(1)} collective-permute-done((bf16[14,4,32,128]{3,2,1,0:T(8,128)(2,1)S(1)}, bf16[14,4,32,128]{3,2,1,0:T(8,128)(2,1)S(1)}, u32[]{:S(2)}, u32[]{:S(2)}) %collective-permute-start.5) | collective-permute-done | bytes 458784 | tf_op jit(solution)/shard_map/ppermute | solution.py:16
  42.1 0.0 copy-start.6
  42.1 0.4 pack_edges.1
  42.4 0.4 copy-done.6
  42.8 4.8 %collective-permute-start.6 = (bf16[11,32,128]{2,1,0:T(8,128)(2,1)S(1)}, bf16[11,32,128]{2,1,0:T(8,128)(2,1)S(1)}, u32[]{:S(2)}, u32[]{:S(2)}) collective-permute-start(bf16[11,32,128]{2,1,0:T(8,128)(2,1)S(1)} %get-tuple-element.26), channel_id=1, source_target_pairs={{0,1},{1,2},{2,3},{4,5},{5,6},{6,7},{8,9},{9,10},{10,11},{12,13},{... | collective-permute-start | bytes 270344 | tf_op jit(solution)/shard_map/ppermute | solution.py:15
  47.7 1.9 %collective-permute-start.7 = (bf16[11,32,128]{2,1,0:T(8,128)(2,1)S(1)}, bf16[11,32,128]{2,1,0:T(8,128)(2,1)S(1)}, u32[]{:S(2)}, u32[]{:S(2)}) collective-permute-start(bf16[11,32,128]{2,1,0:T(8,128)(2,1)S(1)} %get-tuple-element.27), channel_id=1, source_target_pairs={{1,0},{2,1},{3,2},{5,4},{6,5},{7,6},{9,8},{10,9},{11,10},{13,12},{... | collective-permute-start | bytes 270344 | tf_op jit(solution)/shard_map/ppermute | solution.py:16
  49.6 0.0 collective-permute-done.6.rl_in
  49.6 0.0 copy-start.13
  49.6 3.9 %collective-permute-done.7.rr_in = bf16[11,32,128]{2,1,0:T(8,128)(2,1)S(1)} collective-permute-done((bf16[11,32,128]{2,1,0:T(8,128)(2,1)S(1)}, bf16[11,32,128]{2,1,0:T(8,128)(2,1)S(1)}, u32[]{:S(2)}, u32[]{:S(2)}) %collective-permute-start.7) | collective-permute-done | bytes 90144 | tf_op jit(solution)/shard_map/ppermute | solution.py:16
  53.5 0.0 copy-done.5
  53.5 0.0 copy-done.13
  53.5 0.0 copy-start.14
  53.5 0.6 copy-done.14
  54.2 7.0 %first_convs.1 = (bf16[10,14,32,128]{3,2,1,0:T(8,128)(2,1)}, bf16[10,128,128]{2,1,0:T(8,128)(2,1)}, bf16[4,8,32,128]{3,2,1,0:T(8,128)(2,1)}, f32[4,64,128]{2,1,0...) custom-call(bf16[7,8,32,128]{3,2,1,0:T(8,128)(2,1)} %copy-done.1, ...), custom_call_target="tpu_custom_call" | custom-call | flops 8589934592 | bytes 8388608 | tf_op jit(solution)/shard_map/first_convs/pallas_call | solution.py:321
  61.1 4.3 %all-to-all-start = ((f32[16,1,128]{2,1,0:T(1,128)}), f32[16,1,128]{2,1,0:T(1,128)S(1)}, u32[]{:S(2)}, u32[]{:S(2)}) async-start(f32[16,1,128]{2,1,0:T(1,128)} %get-tuple-element.37), calls=%async_computation | async-start | bytes 16384 | tf_op jit(solution)/shard_map/all_to_all | solution.py:554
  65.4 0.7 stack.15.place
  66.1 4.8 %all-to-all-done = f32[16,1,128]{2,1,0:T(1,128)S(1)} async-done(((f32[16,1,128]{2,1,0:T(1,128)}), f32[16,1,128]{2,1,0:T(1,128)S(1)}, u32[]{:S(2)}, u32[]{:S(2)}) %all-to-all-start) | async-done | bytes 8224 | tf_op jit(solution)/shard_map/all_to_all | solution.py:554
  70.9 0.0 copy-start.12
  70.9 0.6 broadcast_in_dim.9
  71.6 20.4 %all-to-all-start.1 = ((f32[32,1,128]{2,1,0:T(1,128)}), f32[32,1,128]{2,1,0:T(1,128)S(1)}, u32[]{:S(2)}, u32[]{:S(2)}) async-start(f32[32,1,128]{2,1,0:T(1,128)} %broadcast_in_dim.9), calls=%async_computation.1 | async-start | bytes 32768 | tf_op jit(solution)/shard_map/all_to_all | solution.py:558
  92.0 0.0 copy-done.12
  92.0 9.5 %second_convs.1.result = f32[4,8,32,128]{3,2,1,0:T(8,128)} custom-call(s32[6]{0:T(128)} %stack.15.place, bf16[10,14,32,128]{3,2,1,0:T(8,128)(2,1)} %get-tuple-element.29.hid_in, bf16[10,128,128]{2,1,0:T(8,128)(2,1)} %get-tuple-element.30.hid_h_in, bf16[4,8,32,128]{3,2,1,0:T(8,128)(2,1)} %get-tuple-element.31.own_in, ...), custom_call_target="tpu_custom_call" | custom-call | flops 8589934592 | bytes 4194304 | tf_op jit(solution)/shard_map/second_convs/pallas_call | solution.py:447
  101.5 0.0 copy-start.4
  101.5 1.0 copy-done.4
  102.5 0.1 turn.1.block
  102.6 2.7 %all-to-all-done.1.parts = f32[32,1,128]{2,1,0:T(1,128)S(1)} async-done(((f32[32,1,128]{2,1,0:T(1,128)}), f32[32,1,128]{2,1,0:T(1,128)S(1)}, u32[]{:S(2)}, u32[]{:S(2)}) %all-to-all-start.1) | async-done | bytes 16416 | tf_op jit(solution)/shard_map/all_to_all | solution.py:558
  105.3 1.0 finish.1
  (7 shorter events, 0.2 us)
Async XLA Ops:
  0.6 1.1 %copy-start.11 = (bf16[32,4,8,128]{3,2,1,0:T(8,128)(2,1)S(1)}, bf16[32,4,8,128]{3,2,1,0:T(8,128)(2,1)}, u32[]{:S(2)}) copy-start(bf16[32,4,8,128]{3,2,1,0:T(8,128)(2,1)} %param.4) | copy-start | bytes 786436
  2.0 29.3 %copy-start = (bf16[8,8,32,128]{3,2,1,0:T(8,128)(2,1)}, bf16[8,8,32,128]{3,2,1,0:T(8,128)(2,1)S(1)}, u32[]{:S(2)}) copy-start(bf16[8,8,32,128]{3,2,1,0:T(8,128)(2,1)S(1)} %pad_maximum_fusion.mine_ref.mine) | copy-start | bytes 1572868
  2.0 11.6 %copy-start.9 = (bf16[27,32,32]{2,1,0:T(8,128)(2,1)S(1)}, bf16[27,32,32]{2,1,0:T(8,128)(2,1)}, u32[]{:S(2)}) copy-start(bf16[27,32,32]{2,1,0:T(8,128)(2,1)} %k1_ref.1) | copy-start | bytes 165892
  2.0 11.6 %copy-start.10 = (bf16[27,32,32]{2,1,0:T(8,128)(2,1)S(1)}, bf16[27,32,32]{2,1,0:T(8,128)(2,1)}, u32[]{:S(2)}) copy-start(bf16[27,32,32]{2,1,0:T(8,128)(2,1)} %k2_ref.1) | copy-start | bytes 165892
  2.0 22.8 %collective-permute-start = (bf16[7,8,32,128]{3,2,1,0:T(8,128)(2,1)S(1)}, bf16[7,8,32,128]{3,2,1,0:T(8,128)(2,1)S(1)}, u32[]{:S(2)}, u32[]{:S(2)}) collective-permute-start(bf16[7,8,32,128]{3,2,1,0:T(8,128)(2,1)S(1)} %slice.24), channel_id=1, source_target_pairs={{0,16},{16,32},{32,48},{48,64},{64,80},{80,96},{96,112},{112,128},... | collective-permute-start | bytes 1376264 | tf_op jit(solution)/shard_map/ppermute | solution.py:15
  7.7 17.1 %collective-permute-start.1 = (bf16[7,8,32,128]{3,2,1,0:T(8,128)(2,1)S(1)}, bf16[7,8,32,128]{3,2,1,0:T(8,128)(2,1)S(1)}, u32[]{:S(2)}, u32[]{:S(2)}) collective-permute-start(bf16[7,8,32,128]{3,2,1,0:T(8,128)(2,1)S(1)} %pad_maximum_fusion.1), channel_id=1, source_target_pairs={{16,0},{32,16},{48,32},{64,48},{80,64},{96,80},{112,96},{128,112},... | collective-permute-start | bytes 1376264 | tf_op jit(solution)/shard_map/ppermute | solution.py:16
  9.1 7.8 %collective-permute-start.2 = (bf16[8,4,32,128]{3,2,1,0:T(8,128)(2,1)S(1)}, bf16[8,4,32,128]{3,2,1,0:T(8,128)(2,1)S(1)}, u32[]{:S(2)}, u32[]{:S(2)}) collective-permute-start(bf16[8,4,32,128]{3,2,1,0:T(8,128)(2,1)S(1)} %get-tuple-element.39), channel_id=1, source_target_pairs={{0,4},{4,8},{8,12},{1,5},{5,9},{9,13},{2,6},{6,10},{10,14},{3,7},{... | collective-permute-start | bytes 786440 | tf_op jit(solution)/shard_map/ppermute | solution.py:15
  12.3 8.5 %collective-permute-start.3 = (bf16[8,4,32,128]{3,2,1,0:T(8,128)(2,1)S(1)}, bf16[8,4,32,128]{3,2,1,0:T(8,128)(2,1)S(1)}, u32[]{:S(2)}, u32[]{:S(2)}) collective-permute-start(bf16[8,4,32,128]{3,2,1,0:T(8,128)(2,1)S(1)} %get-tuple-element.38), channel_id=1, source_target_pairs={{4,0},{8,4},{12,8},{5,1},{9,5},{13,9},{6,2},{10,6},{14,10},{7,3},{... | collective-permute-start | bytes 786440 | tf_op jit(solution)/shard_map/ppermute | solution.py:16
  14.6 0.8 copy-start.3
  16.9 16.4 %copy-start.7 = (bf16[8,4,32,128]{3,2,1,0:T(8,128)(2,1)}, bf16[8,4,32,128]{3,2,1,0:T(8,128)(2,1)S(1)}, u32[]{:S(2)}) copy-start(bf16[8,4,32,128]{3,2,1,0:T(8,128)(2,1)S(1)} %collective-permute-done.2.a1) | copy-start | bytes 786436
  20.8 12.6 %copy-start.8 = (bf16[8,4,32,128]{3,2,1,0:T(8,128)(2,1)}, bf16[8,4,32,128]{3,2,1,0:T(8,128)(2,1)S(1)}, u32[]{:S(2)}) copy-start(bf16[8,4,32,128]{3,2,1,0:T(8,128)(2,1)S(1)} %collective-permute-done.3.b1) | copy-start | bytes 786436
  24.9 8.5 %copy-start.1 = (bf16[7,8,32,128]{3,2,1,0:T(8,128)(2,1)}, bf16[7,8,32,128]{3,2,1,0:T(8,128)(2,1)S(1)}, u32[]{:S(2)}) copy-start(bf16[7,8,32,128]{3,2,1,0:T(8,128)(2,1)S(1)} %collective-permute-done.prev_ref.prev) | copy-start | bytes 1376260
  24.9 8.5 %copy-start.2 = (bf16[7,8,32,128]{3,2,1,0:T(8,128)(2,1)}, bf16[7,8,32,128]{3,2,1,0:T(8,128)(2,1)S(1)}, u32[]{:S(2)}) copy-start(bf16[7,8,32,128]{3,2,1,0:T(8,128)(2,1)S(1)} %collective-permute-done.1.next_ref.following) | copy-start | bytes 1376260
  24.9 13.2 %collective-permute-start.4 = (bf16[14,4,32,128]{3,2,1,0:T(8,128)(2,1)S(1)}, bf16[14,4,32,128]{3,2,1,0:T(8,128)(2,1)S(1)}, u32[]{:S(2)}, u32[]{:S(2)}) collective-permute-start(bf16[14,4,32,128]{3,2,1,0:T(8,128)(2,1)S(1)} %get-tuple-element.24), channel_id=1, source_target_pairs={{0,4},{4,8},{8,12},{1,5},{5,9},{9,13},{2,6},{6,10},{10,14},{3,7},{... | collective-permute-start | bytes 1376264 | tf_op jit(solution)/shard_map/ppermute | solution.py:15
  30.0 12.1 %collective-permute-start.5 = (bf16[14,4,32,128]{3,2,1,0:T(8,128)(2,1)S(1)}, bf16[14,4,32,128]{3,2,1,0:T(8,128)(2,1)S(1)}, u32[]{:S(2)}, u32[]{:S(2)}) collective-permute-start(bf16[14,4,32,128]{3,2,1,0:T(8,128)(2,1)S(1)} %get-tuple-element.25), channel_id=1, source_target_pairs={{4,0},{8,4},{12,8},{5,1},{9,5},{13,9},{6,2},{10,6},{14,10},{7,3},{... | collective-permute-start | bytes 1376264 | tf_op jit(solution)/shard_map/ppermute | solution.py:16
  38.2 15.3 %copy-start.5 = (bf16[14,4,32,128]{3,2,1,0:T(8,128)(2,1)}, bf16[14,4,32,128]{3,2,1,0:T(8,128)(2,1)S(1)}, u32[]{:S(2)}) copy-start(bf16[14,4,32,128]{3,2,1,0:T(8,128)(2,1)S(1)} %collective-permute-done.4.a2) | copy-start | bytes 1376260
  42.1 0.8 copy-start.6
  42.8 6.8 %collective-permute-start.6 = (bf16[11,32,128]{2,1,0:T(8,128)(2,1)S(1)}, bf16[11,32,128]{2,1,0:T(8,128)(2,1)S(1)}, u32[]{:S(2)}, u32[]{:S(2)}) collective-permute-start(bf16[11,32,128]{2,1,0:T(8,128)(2,1)S(1)} %get-tuple-element.26), channel_id=1, source_target_pairs={{0,1},{1,2},{2,3},{4,5},{5,6},{6,7},{8,9},{9,10},{10,11},{12,13},{... | collective-permute-start | bytes 270344 | tf_op jit(solution)/shard_map/ppermute | solution.py:15
  47.7 5.8 %collective-permute-start.7 = (bf16[11,32,128]{2,1,0:T(8,128)(2,1)S(1)}, bf16[11,32,128]{2,1,0:T(8,128)(2,1)S(1)}, u32[]{:S(2)}, u32[]{:S(2)}) collective-permute-start(bf16[11,32,128]{2,1,0:T(8,128)(2,1)S(1)} %get-tuple-element.27), channel_id=1, source_target_pairs={{1,0},{2,1},{3,2},{5,4},{6,5},{7,6},{9,8},{10,9},{11,10},{13,12},{... | collective-permute-start | bytes 270344 | tf_op jit(solution)/shard_map/ppermute | solution.py:16
  49.6 3.9 %copy-start.13 = (bf16[11,32,128]{2,1,0:T(8,128)(2,1)}, bf16[11,32,128]{2,1,0:T(8,128)(2,1)S(1)}, u32[]{:S(2)}) copy-start(bf16[11,32,128]{2,1,0:T(8,128)(2,1)S(1)} %collective-permute-done.6.rl_in) | copy-start | bytes 270340
  53.5 0.6 copy-start.14
  61.1 9.8 %all-to-all-start = ((f32[16,1,128]{2,1,0:T(1,128)}), f32[16,1,128]{2,1,0:T(1,128)S(1)}, u32[]{:S(2)}, u32[]{:S(2)}) async-start(f32[16,1,128]{2,1,0:T(1,128)} %get-tuple-element.37), calls=%async_computation | async-start | bytes 16384 | tf_op jit(solution)/shard_map/all_to_all | solution.py:554
  70.9 21.0 %copy-start.12 = (f32[128]{0:T(128)}, f32[128]{0:T(128)S(1)}, u32[]{:S(2)}) copy-start(f32[128]{0:T(128)S(1)} %reduce_sum.9) | copy-start | bytes 1540
  71.6 33.8 %all-to-all-start.1 = ((f32[32,1,128]{2,1,0:T(1,128)}), f32[32,1,128]{2,1,0:T(1,128)S(1)}, u32[]{:S(2)}, u32[]{:S(2)}) async-start(f32[32,1,128]{2,1,0:T(1,128)} %broadcast_in_dim.9), calls=%async_computation.1 | async-start | bytes 32768 | tf_op jit(solution)/shard_map/all_to_all | solution.py:558
  101.5 1.0 copy-start.4
